TPU v7x, 32 devices: a whole 2x2x4 slice. The times are simulated.
32 devices in a mesh: net: 2 (over core), dp: 2 (over x), depth: 8 (over z, y).
Axes of the slice: x: 2, y: 2, z: 4, core: 2. Of those that a mesh axis runs over, the one named last changes fastest.
Arguments:
- features: bfloat16 [2, 2, 16, 64, 16, 128], P('net', 'dp', None, 'depth'), may hold values from -16 to 16
- labels: int32 [2, 64, 16, 128], P('dp', 'depth'), may hold values from 0 to 7
- masks: int32 [2, 2, 64, 16, 128], P('net', 'dp', 'depth'), may hold values 0 or 1
- conv_kernel: bfloat16 [2, 27, 16, 16], P('net'), may hold values from -0.3125 to 0.3125
- conv_bias: float32 [2, 16], P('net'), may hold values from -3 to 3
- head_weight: bfloat16 [2, 8, 16], P('net'), may hold values from -1.5 to 1.5
- head_bias: float32 [2, 8], P('net'), may hold values from -3 to 3
Outputs:
- grad_input: bfloat16 [2, 2, 16, 64, 16, 128], P('net', 'dp', None, 'depth')
- grad_kernel: float32 [2, 27, 16, 16], P('net')
- grad_bias: float32 [2, 16], P('net')
- grad_head: float32 [2, 8, 16], P('net')
- grad_head_bias: float32 [2, 8], P('net')
All inputs are finite; a program needn't handle non-finite values. No bound on the sum of `masks` on one device may be relied on, other than what follows from the above.
Results may differ from a plain program's by a relative error of at most 0.0063.
Values may be sent and summed in bfloat16 or wider, within the bound.
No kernel may reach another device: no remote copies, remote signals or barrier semaphores. Data moves between devices by JAX's collectives and lax.ppermute only.
A program may use at most 64 MiB of HBM per device.

v0:
```python
import jax
import jax.numpy as jnp
from jax import lax
from jax.sharding import PartitionSpec as P


def with_halo(x, sides, width):
    for axis, dim in sides:
        size, length = (lax.axis_size(axis), x.shape[dim])
        up = [(i, (i + 1) % size) for i in range(size - 1)]
        down = [(j, i) for i, j in up]
        last = lax.slice_in_dim(x, length - width, length, axis=dim)
        initial = lax.slice_in_dim(x, 0, width, axis=dim)
        before = lax.ppermute(last, axis, up)
        after = lax.ppermute(initial, axis, down)
        x = jnp.concatenate([before, x, after], axis=dim)
    return x


def swapped(value, axis, distance):
    mask = 2**distance
    pairs = [(source, source ^ mask) for source in range(lax.axis_size(axis))]
    return lax.ppermute(value, axis, pairs)


def pad_sides(field):
    return jnp.pad(field, ((0, 0), (0, 0), (1, 1), (1, 1)))


def correlate(padded, kernel, planes, height, breadth):
    summed = jnp.zeros((kernel.shape[1], planes, height, breadth), jnp.float32)
    for t in range(27):
        first, second, third = (t // 9, t // 3 % 3, t % 3)
        window = padded[
            :, first : first + planes, second : second + height, third : third + breadth
        ]
        summed = summed + jnp.einsum(
            "oc,cdhw->odhw", kernel[t], window, preferred_element_type=jnp.float32
        )
    return summed


def transpose_correlate(grad_padded, kernel, planes, height, breadth):
    summed = jnp.zeros((kernel.shape[2], planes, height, breadth), jnp.float32)
    for t in range(27):
        first, second, third = (2 - t // 9, 2 - t // 3 % 3, 2 - t % 3)
        window = grad_padded[
            :, first : first + planes, second : second + height, third : third + breadth
        ]
        summed = summed + jnp.einsum(
            "oc,odhw->cdhw", kernel[t], window, preferred_element_type=jnp.float32
        )
    return summed


def kernel_products(pre_half, padded, planes, height, breadth):
    pieces = []
    for t in range(27):
        first, second, third = (t // 9, t // 3 % 3, t % 3)
        window = padded[
            :, first : first + planes, second : second + height, third : third + breadth
        ]
        pieces.append(
            jnp.einsum("odhw,cdhw->oc", pre_half, window, preferred_element_type=jnp.float32)
        )
    return jnp.stack(pieces)


def forward_head(padded, kernel, bias_vec, head_mat, head_off, label_map, planes, height, breadth):
    preact = correlate(padded, kernel, planes, height, breadth) + bias_vec[:, None, None, None]
    hidden = jnp.maximum(preact, 0.0).astype(jnp.bfloat16)
    logits = (
        jnp.einsum("kc,cdhw->kdhw", head_mat, hidden, preferred_element_type=jnp.float32)
        + head_off[:, None, None, None]
    )
    log_total = jnp.log(jnp.sum(jnp.exp(logits), axis=0))
    classes = jnp.arange(logits.shape[0], dtype=jnp.int32)
    onehot = (label_map[None] == classes[:, None, None, None]).astype(jnp.float32)
    cross_ent = log_total - jnp.sum(onehot * logits, axis=0)
    soft_probs = jnp.exp(logits - log_total[None])
    return (preact, hidden, cross_ent, soft_probs, onehot)


def backward_head(peer_weight, soft_probs, onehot, preact, head_mat):
    logit_grad = peer_weight[None] * (soft_probs - onehot)
    logit_half = logit_grad.astype(jnp.bfloat16)
    hidden_grad = jnp.einsum(
        "kc,kdhw->cdhw", head_mat, logit_half, preferred_element_type=jnp.float32
    )
    pre_grad = jnp.where(preact > 0.0, hidden_grad, 0.0)
    return (logit_grad, logit_half, pre_grad)


def body(features, labels, masks, conv_kernel, conv_bias, head_weight, head_bias):
    field = features[0, 0]
    label_map = labels[0]
    selection = masks[0, 0]
    kernel = conv_kernel[0]
    bias_vec = conv_bias[0]
    head_mat = head_weight[0]
    head_off = head_bias[0]
    planes, height, breadth = (field.shape[1], field.shape[2], field.shape[3])
    padded = pad_sides(with_halo(field, (("depth", 1),), 1))
    preact, hidden, cross_ent, soft_probs, onehot = forward_head(
        padded, kernel, bias_vec, head_mat, head_off, label_map, planes, height, breadth
    )
    offered = selection.astype(jnp.float32) * jnp.exp(-cross_ent)
    peer_weight = swapped(offered, "net", 0)
    logit_grad, logit_half, pre_grad = backward_head(
        peer_weight, soft_probs, onehot, preact, head_mat
    )
    pre_half = pre_grad.astype(jnp.bfloat16)
    grad_padded = pad_sides(with_halo(pre_half, (("depth", 1),), 1))
    input_grad = transpose_correlate(grad_padded, kernel, planes, height, breadth).astype(
        jnp.bfloat16
    )
    kernel_grad = kernel_products(pre_half, padded, planes, height, breadth)
    bias_grad = jnp.sum(pre_grad, axis=(1, 2, 3))
    head_grad = jnp.einsum("kdhw,cdhw->kc", logit_half, hidden, preferred_element_type=jnp.float32)
    offset_grad = jnp.sum(logit_grad, axis=(1, 2, 3))
    kernel_grad, bias_grad, head_grad, offset_grad = lax.psum(
        (kernel_grad, bias_grad, head_grad, offset_grad), ("dp", "depth")
    )
    inverse_count = 1.0 / (lax.axis_size("dp") * lax.axis_size("depth") * planes * height * breadth)
    return (
        input_grad[None, None],
        (kernel_grad * inverse_count)[None],
        (bias_grad * inverse_count)[None],
        (head_grad * inverse_count)[None],
        (offset_grad * inverse_count)[None],
    )


def solution(mesh):
    in_specs = (
        P("net", "dp", None, "depth", None, None),
        P("dp", "depth", None, None),
        P("net", "dp", "depth", None, None),
        P("net", None, None, None),
        P("net", None),
        P("net", None, None),
        P("net", None),
    )
    out_specs = (
        P("net", "dp", None, "depth", None, None),
        P("net", None, None, None),
        P("net", None),
        P("net", None, None),
        P("net", None),
    )
    return jax.shard_map(body, mesh=mesh, in_specs=in_specs, out_specs=out_specs, check_vma=False)
```

profile of v0, /device:TPU:0, one launch (start us, length us, event | category | flops | bytes accessed | tf_op | source)
XLA Modules:
  0.0 147.9 jit_solution(3590571253808474643)
XLA Ops:
  0.7 1.4 copy.209
  2.1 0.7 fusion.270
  2.8 4.9 %collective-permute-start = (bf16[16,1,16,128]{3,0,2,1:T(8,128)(2,1)}, bf16[16,1,16,128]{3,0,2,1:T(8,128)(2,1)S(1)}, u32[]{:S(2)}, u32[]{:S(2)}) collective-permute-start(bf16[16,1,16,128]{3,0,2,1:T(8,128)(2,1)} %get-tuple-element.20), channel_id=1, source_target_pairs={{0,1},{1,2},{2,3},{3,4},{4,5},{5,6},{6,7},{8,9},{9,10},{10,11},{11... | collective-permute-start | bytes 196616 | tf_op jit(solution)/shard_map/ppermute | solution.py:14
  7.6 1.3 collective-permute-start.1
  8.9 0.4 fusion.271
  9.5 0.4 fusion.228
  9.9 0.9 fusion.272
  11.9 1.0 copy.185
  12.9 1.0 copy.184
  14.0 1.0 copy.182
  15.0 1.0 copy.181
  16.0 1.0 copy.180
  17.0 1.0 copy.183
  18.0 1.0 copy.179
  21.4 0.7 fusion.10
  22.8 0.4 fusion.169
  29.7 0.8 fusion.61
  30.8 0.4 copy-done.5
  31.2 0.8 fusion.63
  32.0 0.5 select_reduce_fusion
  33.0 1.2 collective-permute-done.2
  34.2 0.5 fusion.268
  35.0 0.5 fusion.226
  35.5 0.4 fusion.92
  35.9 0.4 fusion.91
  37.0 0.4 fusion.88
  37.8 0.4 fusion.86
  38.2 0.4 fusion.85
  39.0 0.4 fusion.83
  39.4 0.4 fusion.82
  40.1 0.4 fusion.80
  40.6 0.4 fusion.79
  41.3 0.4 fusion.77
  41.7 0.4 fusion.76
  42.5 0.4 fusion.74
  42.9 0.4 fusion.73
  44.0 0.4 fusion.70
  44.8 0.4 fusion.68
  45.2 0.4 fusion.67
  46.2 80.8 %all-reduce.2 = (f32[27,16,16]{2,1,0:T(8,128)S(1)}, f32[16]{0:T(128)S(1)}, f32[8,16]{1,0:T(8,128)S(1)}, f32[8]{0:T(128)S(1)}) all-reduce(f32[27,16,16]{2,1,0:T(8,128)S(1)} %fusion.67, f32[16]{0:T(128)S(1)} %get-tuple-element.16, f32[8,16]{1,0:T(8,128)S(1)} %convolution_bitcast_fusion.51, ...), channel_id=1, replica_groups=mesh['net'=2,'dp'=2,'depth'=8] {'dp','depth'}, use_global_device_ids=true, to_apply=%region_2.3 | all-reduce | flops 7064 | bytes 56512 | tf_op jit(solution)/shard_map/psum | solution.py:121
  127.0 0.6 multiply_bitcast_fusion.1
  127.6 0.5 multiply_bitcast_fusion.2
  128.2 1.3 collective-permute-start.4
  129.4 4.8 %collective-permute-start.3 = (bf16[16,1,16,128]{3,0,2,1:T(8,128)(2,1)S(1)}, bf16[16,1,16,128]{3,0,2,1:T(8,128)(2,1)S(1)}, u32[]{:S(2)}, u32[]{:S(2)}) collective-permute-start(bf16[16,1,16,128]{3,0,2,1:T(8,128)(2,1)S(1)} %get-tuple-element.18), channel_id=1, source_target_pairs={{0,1},{1,2},{2,3},{3,4},{4,5},{5,6},{6,7},{8,9},{9,10},{10,11},{11... | collective-permute-start | bytes 196616 | tf_op jit(solution)/shard_map/ppermute | solution.py:14
  134.2 0.5 multiply_bitcast_fusion.3
  134.7 0.8 copy.68
  135.9 0.7 select_maximum_fusion
  136.6 0.4 fusion.115
  137.3 0.4 fusion.119
  137.7 0.4 fusion.121
  138.4 0.4 fusion.125
  138.8 0.4 fusion.127
  139.5 0.4 fusion.131
  140.2 0.4 fusion.135
  140.6 0.4 convolution_bitcast_fusion.16
  141.3 0.4 convolution_bitcast_fusion.18
  142.1 0.4 convolution_bitcast_fusion.20
  142.5 0.4 convolution_bitcast_fusion.21
  143.2 0.4 fusion.110
  143.6 0.4 fusion.112
  143.9 0.4 convolution_bitcast_fusion.15
  145.0 0.8 fusion.59
  146.2 0.8 fusion.66
  147.0 0.9 copy.67
  (87 shorter events, 19.5 us)
Async XLA Ops:
  0.6 31.4 %copy-start = (bf16[1,8,16]{2,1,0:T(8,128)(2,1)S(1)}, bf16[1,8,16]{2,1,0:T(8,128)(2,1)}, u32[]{:S(2)}) copy-start(bf16[1,8,16]{2,1,0:T(8,128)(2,1)} %param.12) | copy-start | bytes 772
  0.6 8.3 %copy-start.1 = (bf16[1,27,16,16]{1,3,2,0:T(8,128)(2,1)S(1)}, bf16[1,27,16,16]{1,3,2,0:T(8,128)(2,1)}, u32[]{:S(2)}) copy-start(bf16[1,27,16,16]{1,3,2,0:T(8,128)(2,1)} %param.10) | copy-start | bytes 41476
  2.1 7.4 %copy-start.2 = (bf16[1,1,16,8,16,128]{5,4,3,2,1,0:T(8,128)(2,1)S(1)}, bf16[1,1,16,8,16,128]{5,4,3,2,1,0:T(8,128)(2,1)}, u32[]{:S(2)}) copy-start(bf16[1,1,16,8,16,128]{5,4,3,2,1,0:T(8,128)(2,1)} %param.7) | copy-start | bytes 1572868
  2.8 18.6 %collective-permute-start = (bf16[16,1,16,128]{3,0,2,1:T(8,128)(2,1)}, bf16[16,1,16,128]{3,0,2,1:T(8,128)(2,1)S(1)}, u32[]{:S(2)}, u32[]{:S(2)}) collective-permute-start(bf16[16,1,16,128]{3,0,2,1:T(8,128)(2,1)} %get-tuple-element.20), channel_id=1, source_target_pairs={{0,1},{1,2},{2,3},{3,4},{4,5},{5,6},{6,7},{8,9},{9,10},{10,11},{11... | collective-permute-start | bytes 196616 | tf_op jit(solution)/shard_map/ppermute | solution.py:14
  7.6 13.8 %collective-permute-start.1 = (bf16[16,1,16,128]{3,0,2,1:T(8,128)(2,1)}, bf16[16,1,16,128]{3,0,2,1:T(8,128)(2,1)S(1)}, u32[]{:S(2)}, u32[]{:S(2)}) collective-permute-start(bf16[16,1,16,128]{3,0,2,1:T(8,128)(2,1)} %get-tuple-element.21), channel_id=1, source_target_pairs={{1,0},{2,1},{3,2},{4,3},{5,4},{6,5},{7,6},{9,8},{10,9},{11,10},{12... | collective-permute-start | bytes 196616 | tf_op jit(solution)/shard_map/ppermute | solution.py:15
  30.5 0.7 copy-start.5
  31.2 0.9 copy-start.3
  31.2 0.9 copy-start.6
  32.0 0.8 copy-start.4
  32.9 1.3 collective-permute-start.2
  128.2 7.4 %collective-permute-start.4 = (bf16[16,1,16,128]{3,0,2,1:T(8,128)(2,1)S(1)}, bf16[16,1,16,128]{3,0,2,1:T(8,128)(2,1)S(1)}, u32[]{:S(2)}, u32[]{:S(2)}) collective-permute-start(bf16[16,1,16,128]{3,0,2,1:T(8,128)(2,1)S(1)} %get-tuple-element.19), channel_id=1, source_target_pairs={{1,0},{2,1},{3,2},{4,3},{5,4},{6,5},{7,6},{9,8},{10,9},{11,10},{12... | collective-permute-start | bytes 196616 | tf_op jit(solution)/shard_map/ppermute | solution.py:15
  129.4 6.4 %collective-permute-start.3 = (bf16[16,1,16,128]{3,0,2,1:T(8,128)(2,1)S(1)}, bf16[16,1,16,128]{3,0,2,1:T(8,128)(2,1)S(1)}, u32[]{:S(2)}, u32[]{:S(2)}) collective-permute-start(bf16[16,1,16,128]{3,0,2,1:T(8,128)(2,1)S(1)} %get-tuple-element.18), channel_id=1, source_target_pairs={{0,1},{1,2},{2,3},{3,4},{4,5},{5,6},{6,7},{8,9},{9,10},{10,11},{11... | collective-permute-start | bytes 196616 | tf_op jit(solution)/shard_map/ppermute | solution.py:14
where the time goes:
time: 149 us; the launch traced here: 148 us
  blocking collectives  80.8 us (54%)
  matrix products  32.3 us (22%)
  local copies, waits for them, and re-layouts  16.6 us (11%)
  starting transfers between devices  12.3 us (8%)
  other arithmetic  3.33 us (2%)
  waiting for transfers between devices  1.57 us (1%)
    psum x1, blocking collectives, body(): lax.psum((kernel_grad, bias_grad, head_grad, offset_grad), ('dp', 'depth'))  80.8 us
    unnamed x44, local copies, waits for them, and re-layouts  14.6 us
    dot_general x27, matrix products, transpose_correlate(): jnp.einsum('oc,odhw->cdhw', kernel[t], window, preferred_element_type=jnp...  10.8 us
    dot_general x27, matrix products, kernel_products(): jnp.einsum('odhw,cdhw->oc', pre_half, window, preferred_element_type=jnp....  10.4 us
    dot_general x27, matrix products, correlate(): jnp.einsum('oc,cdhw->odhw', kernel[t], window, preferred_element_type=jnp...  9.82 us
    ppermute x2, starting transfers between devices, with_halo(): before = lax.ppermute(last, axis, up)  9.63 us
  transfers between devices with their start and end apart: 5, of which 2 were waited for; matrix products, arithmetic and copies ran while one was open for 9% of the time, Pallas kernels for 0%

commit v1 on v0

v1 whole, which is shorter than its diff:
```python
import functools

import jax
import jax.numpy as jnp
from jax import lax
from jax.experimental import pallas as pl
from jax.experimental.pallas import tpu as pltpu
from jax.sharding import PartitionSpec as P

BF = jnp.bfloat16
F32 = jnp.float32
VM = pltpu.VMEM
SM = pltpu.SMEM


def iota(shape, dim):
    return lax.broadcasted_iota(jnp.int32, shape, dim)


def dot(a, b):
    return jnp.dot(a, b, preferred_element_type=F32)


def dot_nt(a, b):
    return lax.dot_general(a, b, (((1,), (1,)), ((), ())), preferred_element_type=F32)


def split3(x):
    high = x.astype(BF)
    rest = x - high.astype(F32)
    mid = rest.astype(BF)
    return high, mid, (rest - mid.astype(F32)).astype(BF)


def dot_exact(x, ones):
    return sum(dot(part, ones) for part in split3(x))


def moved(x):
    y = x.astype(F32)
    lane = iota(y.shape, 1)
    width = y.shape[1]
    before = jnp.where(lane == 0, 0.0, pltpu.roll(y, 1, 1))
    after = jnp.where(lane == width - 1, 0.0, pltpu.roll(y, width - 1, 1))
    return before.astype(BF), after.astype(BF)


def fill_band(kernel_ref, band_ref, ch, hh):
    rows = ch * hh
    flat = kernel_ref[...].reshape(27 * ch, ch)
    spread = (iota((ch, rows), 1) // hh == iota((ch, rows), 0)).astype(F32).astype(BF)
    wide = dot(flat, spread).astype(BF)
    masks = [(iota((ch, rows), 1) % hh == h).astype(F32).astype(BF) for h in range(hh)]
    for i in range(3):
        for k in range(3):
            taps = [wide[(9 * i + 3 * j + k) * ch : (9 * i + 3 * j + k + 1) * ch] for j in range(3)]
            col = (3 * i + k) * rows
            for h in range(hh):
                block = masks[h] * taps[1]
                if h > 0:
                    block = block + masks[h - 1] * taps[0]
                if h < hh - 1:
                    block = block + masks[h + 1] * taps[2]
                band_ref[h * ch : (h + 1) * ch, col : col + rows] = block


def head_matrix(head_ref, ch, hh, classes):
    rows = ch * hh
    spread = (iota((ch, rows), 1) % ch == iota((ch, rows), 0)).astype(F32).astype(BF)
    wide = dot(head_ref[...], spread)
    wide = jnp.broadcast_to(wide[:, None, :], (classes, hh, rows))
    keep = iota((classes, hh, rows), 2) // ch == iota((classes, hh, rows), 1)
    return jnp.where(keep, wide, 0.0).reshape(classes * hh, rows).astype(BF)


def head_matrix_t(head_ref, ch, hh, classes):
    mat = head_matrix(head_ref, ch, hh, classes)
    rows = ch * hh
    unit = (iota((rows, rows), 0) == iota((rows, rows), 1)).astype(F32).astype(BF)
    return dot_nt(unit, mat).astype(BF)


def bias_rows(bias_ref, ch, width):
    out = jnp.zeros((ch, width), F32)
    sub = iota((ch, width), 0)
    for c in range(ch):
        out = jnp.where(sub == c, bias_ref[0, c], out)
    return out


def fill_shifted(x, ref, slot, rows):
    before, after = moved(x)
    ref[slot, 0:rows] = before
    ref[slot, rows : 2 * rows] = x
    ref[slot, 2 * rows : 3 * rows] = after


def forward_pair(band, shifted_ref, slot, bias, mat, head_bias_ref, label, mask, dims):
    ch, hh, ww, classes = dims
    rows = ch * hh
    left = shifted_ref[slot : slot + 3].reshape(9 * rows, ww)
    right = shifted_ref[slot + 1 : slot + 4].reshape(9 * rows, ww)
    preact = dot(band, jnp.concatenate([left, right], axis=1))
    preact = (preact.reshape(hh, ch, 2 * ww) + bias[None]).reshape(rows, 2 * ww)
    hidden = jnp.maximum(preact, 0.0).astype(BF)
    logits = dot(mat, hidden).reshape(classes, hh, 2 * ww)
    parts = [logits[c] + head_bias_ref[0, c] for c in range(classes)]
    total = functools.reduce(jnp.add, [jnp.exp(p) for p in parts])
    log_total = jnp.log(total)
    soft = [jnp.exp(p - log_total) for p in parts]
    hot = [label == c for c in range(classes)]
    chosen = functools.reduce(jnp.add, [jnp.where(o, s, 0.0) for o, s in zip(hot, soft)])
    diffs = [s - jnp.where(o, 1.0, 0.0) for o, s in zip(hot, soft)]
    return hidden, jnp.stack(diffs).reshape(classes * hh, 2 * ww), mask * chosen


def put_pair(ref, first, second, value, ww):
    ref[first] = value[:, :ww]
    ref[second] = value[:, ww:]


def interior_kernel(
    x_ref, label_ref, mask_ref, kernel_ref, bias_ref, head_ref, head_bias_ref,
    band_ref, hidden_ref, diff_ref, offered_ref, shifted_ref,
):
    ch, planes, hh, ww = x_ref.shape
    classes = head_ref.shape[0]
    rows = ch * hh
    fill_band(kernel_ref, band_ref, ch, hh)
    mat = head_matrix(head_ref, ch, hh, classes)
    bias = bias_rows(bias_ref, ch, 2 * ww)
    for d in range(planes):
        fill_shifted(x_ref[:, d].reshape(rows, ww), shifted_ref, d, rows)
    for d in range(1, planes - 1, 2):
        label = jnp.concatenate([label_ref[d], label_ref[d + 1]], axis=1)
        mask = jnp.concatenate([mask_ref[d], mask_ref[d + 1]], axis=1).astype(F32)
        hidden, diff, offered = forward_pair(
            band_ref[...], shifted_ref, d - 1, bias, mat, head_bias_ref, label, mask,
            (ch, hh, ww, classes),
        )
        put_pair(hidden_ref, d - 1, d, hidden, ww)
        put_pair(diff_ref, d - 1, d, diff, ww)
        put_pair(offered_ref, d - 1, d, offered, ww)


def edge_kernel(
    x_ref, up_ref, down_ref, label_ref, mask_ref, bias_ref, head_ref, head_bias_ref, band_ref, inner_ref,
    hidden_ref, diff_ref, offered_ref, shifted_ref,
):
    ch, planes, hh, ww = x_ref.shape
    classes = head_ref.shape[0]
    rows = ch * hh
    mat = head_matrix(head_ref, ch, hh, classes)
    bias = bias_rows(bias_ref, ch, 2 * ww)
    offered_ref[2:planes] = inner_ref[...]
    for side in range(2):
        far_ref = (up_ref, down_ref)[side]
        far = [far_ref[p * ch : (p + 1) * ch].reshape(rows, ww) for p in range(2)]
        near = [x_ref[:, p + side * (planes - 2)].reshape(rows, ww) for p in range(2)]
        for slot, x in enumerate((near + far) if side else (far + near)):
            fill_shifted(x, shifted_ref, slot, rows)
        own = side * (planes - 1)
        far_label, far_mask = far_ref[2 * ch].astype(F32).astype(jnp.int32), far_ref[2 * ch + 1].astype(F32)
        labels = [far_label, label_ref[own]]
        masks = [far_mask, mask_ref[own].astype(F32)]
        if side:
            labels, masks = labels[::-1], masks[::-1]
        hidden, diff, offered = forward_pair(
            band_ref[...], shifted_ref, 0, bias, mat, head_bias_ref,
            jnp.concatenate(labels, axis=1), jnp.concatenate(masks, axis=1), (ch, hh, ww, classes),
        )
        put_pair(hidden_ref, 2 * side, 2 * side + 1, hidden, ww)
        put_pair(diff_ref, 2 * side, 2 * side + 1, diff, ww)
        put_pair(offered_ref, side * planes, side * planes + 1, offered, ww)


def backward_kernel(
    edge_ref, x_ref, up_ref, down_ref, weight_ref, hidden_in_ref, hidden_edge_ref, diff_in_ref, diff_edge_ref,
    head_ref, shifted_ref, packed_ref, rows_ref,
):
    ch, planes, hh, ww = x_ref.shape
    classes = head_ref.shape[0]
    rows = ch * hh
    mat_t = head_matrix_t(head_ref, ch, hh, classes)
    bias_sum = jnp.zeros((rows, ww), F32)
    offset_sum = jnp.zeros((classes * hh, ww), F32)
    hiddens, halves = [], []
    for s in range(0, planes + 2, 2):
        if s == 0 or s == planes:
            a = 0 if s == 0 else 2
            hidden = [hidden_edge_ref[a], hidden_edge_ref[a + 1]]
            diff = [diff_edge_ref[a], diff_edge_ref[a + 1]]
        else:
            hidden = [hidden_in_ref[s - 2], hidden_in_ref[s - 1]]
            diff = [diff_in_ref[s - 2], diff_in_ref[s - 1]]
        grads = []
        for p in range(2):
            g = diff[p].reshape(classes, hh, ww) * weight_ref[s + p][None]
            grads.append(g.reshape(classes * hh, ww))
        half = [g.astype(BF) for g in grads]
        pre = dot(mat_t, jnp.concatenate(half, axis=1))
        for p in range(2):
            value = jnp.where(hidden[p].astype(F32) > 0.0, pre[:, p * ww : (p + 1) * ww], 0.0)
            if 1 <= s + p <= planes:
                bias_sum = bias_sum + value
                offset_sum = offset_sum + grads[p]
                hiddens.append(hidden[p])
                halves.append(half[p])
            else:
                value = jnp.where(edge_ref[0 if s + p == 0 else 1] > 0, value, 0.0)
            value = value.astype(BF)
            before, after = moved(value)
            shifted_ref[s + p, 0:rows] = after
            shifted_ref[s + p, rows : 2 * rows] = value
            shifted_ref[s + p, 2 * rows : 3 * rows] = before
    grad_cat = jnp.concatenate([shifted_ref[s] for s in range(1, planes + 1)], axis=1)
    field = [up_ref[ch : 2 * ch]] + [x_ref[:, d] for d in range(planes)] + [down_ref[0:ch]]
    field = [f.reshape(rows, ww) for f in field]
    place = iota((ch, rows), 1) % hh
    for i in range(3):
        product = dot_nt(grad_cat, jnp.concatenate(field[i : i + planes], axis=1))
        for k in range(3):
            for j in range(3):
                total = jnp.zeros((ch, rows), F32)
                for h in range(hh):
                    if 0 <= h + j - 1 < hh:
                        r = k * rows + h * ch
                        total = jnp.where(place == h + j - 1, product[r : r + ch], total)
                t = 9 * i + 3 * j + k
                rows_ref[t * ch : (t + 1) * ch] = total
    lane16 = iota((rows, 128), 1) % 16
    by_channel = (iota((rows, 128), 0) // hh == lane16).astype(F32).astype(BF)
    sums = dot_exact(rows_ref[...], by_channel)
    blocks = [sums[t * ch : (t + 1) * ch] for t in range(27)]
    product = dot_nt(jnp.concatenate(halves, axis=1), jnp.concatenate(hiddens, axis=1))
    product = product.reshape(classes, hh, rows)
    keep = iota((classes, hh, rows), 2) // ch == iota((classes, hh, rows), 1)
    head = jnp.sum(jnp.where(keep, product, 0.0), axis=1)
    by_last = (iota((rows, 128), 0) % ch == lane16).astype(F32).astype(BF)
    head = dot_exact(head, by_last)
    blocks.append(jnp.concatenate([head, jnp.zeros((ch - classes, 128), F32)], axis=0))
    ones = jnp.ones((16, ww), F32).astype(BF)
    bias = jnp.sum(bias_sum.reshape(hh, ch, ww), axis=0)
    bias = jnp.concatenate([bias] * 8, axis=0)
    blocks.append(sum(dot_nt(ones, part) for part in split3(bias)))
    offset = sum(dot_nt(ones, part) for part in split3(offset_sum))
    by_class = (iota((classes * hh, 128), 0) // hh == iota((classes * hh, 128), 1) % 16).astype(F32).astype(BF)
    blocks.append(dot_exact(offset, by_class))
    group = iota((ch, 128), 1) // 16
    for r in range(4):
        total = jnp.zeros((ch, 128), F32)
        for g in range(8):
            if 8 * r + g < len(blocks):
                total = jnp.where(group == g, blocks[8 * r + g], total)
        packed_ref[r * ch : (r + 1) * ch] = total


def input_kernel(shifted_ref, band_ref, out_ref, turned_ref):
    ch, planes, hh, ww = out_ref.shape
    rows = ch * hh
    unit = (iota((rows, rows), 0) == iota((rows, rows), 1)).astype(F32).astype(BF)
    for i in range(3):
        for k in range(3):
            block = band_ref[:, (3 * i + k) * rows : (3 * i + k + 1) * rows]
            col = (3 * (2 - i) + k) * rows
            turned_ref[:, col : col + rows] = dot_nt(unit, block).astype(BF)
    for d in range(0, planes, 2):
        left = shifted_ref[d : d + 3].reshape(9 * rows, ww)
        right = shifted_ref[d + 1 : d + 4].reshape(9 * rows, ww)
        grad = dot(turned_ref[...], jnp.concatenate([left, right], axis=1)).astype(BF)
        out_ref[:, d] = grad[:, :ww].reshape(ch, hh, ww)
        out_ref[:, d + 1] = grad[:, ww:].reshape(ch, hh, ww)


def unpack_kernel(scale, a_ref, b_ref, kernel_ref, bias_ref, head_ref, offset_ref):
    def block(t):
        r, g = t // 8, t % 8
        value = (a_ref[r * 16 : (r + 1) * 16] + b_ref[r * 16 : (r + 1) * 16]) * scale
        return pltpu.roll(value, (128 - 16 * g) % 128, 1) if g else value

    for t in range(27):
        kernel_ref[t] = block(t)[:, 0:16]
    head_ref[...] = block(27)[0:8, 0:16]
    bias_ref[...] = block(28)[0:1, 0:16]
    offset_ref[...] = block(29)[0:1, 0:8]


def call(kernel, out_shape, in_spaces, scratch, flops, args):
    moved_bytes = sum(a.size * a.dtype.itemsize for a in args)
    return pl.pallas_call(
        kernel,
        out_shape=out_shape,
        in_specs=[pl.BlockSpec(memory_space=s) for s in in_spaces],
        out_specs=jax.tree.map(lambda _: pl.BlockSpec(memory_space=VM), out_shape),
        scratch_shapes=scratch,
        compiler_params=pltpu.CompilerParams(vmem_limit_bytes=32 << 20),
        cost_estimate=pl.CostEstimate(flops=flops, bytes_accessed=moved_bytes, transcendentals=0),
    )(*args)


def body(features, labels, masks, conv_kernel, conv_bias, head_weight, head_bias):
    x, label, mask = features[0, 0], labels[0], masks[0, 0]
    kernel, head = conv_kernel[0], head_weight[0]
    ch, planes, hh, ww = x.shape
    classes = head.shape[0]
    rows = ch * hh
    sds = jax.ShapeDtypeStruct
    size, place = lax.axis_size("depth"), lax.axis_index("depth")

    def edge(first, own):
        tail = jnp.stack([label[own], mask[own]]).astype(BF)
        return jnp.concatenate([x[:, first], x[:, first + 1], tail], axis=0)

    up = lax.ppermute(edge(planes - 2, planes - 1), "depth", [(i, i + 1) for i in range(size - 1)])
    down = lax.ppermute(edge(0, 0), "depth", [(i + 1, i) for i in range(size - 1)])

    pair_flops = 2 * rows * 9 * rows * 2 * ww
    band, hidden_in, diff_in, inner = call(
        interior_kernel,
        (
            sds((rows, 9 * rows), BF),
            sds((planes - 2, rows, ww), BF),
            sds((planes - 2, classes * hh, ww), F32),
            sds((planes - 2, hh, ww), F32),
        ),
        (VM, VM, VM, VM, SM, VM, SM),
        [VM((planes, 3 * rows, ww), BF)],
        pair_flops * (planes // 2 - 1),
        (x, label, mask, kernel, conv_bias, head, head_bias),
    )
    hidden_edge, diff_edge, offered = call(
        edge_kernel,
        (
            sds((4, rows, ww), BF),
            sds((4, classes * hh, ww), F32),
            sds((planes + 2, hh, ww), F32),
        ),
        (VM, VM, VM, VM, VM, SM, VM, SM, VM, VM),
        [VM((4, 3 * rows, ww), BF)],
        pair_flops * 2,
        (x, up, down, label, mask, conv_bias, head, head_bias, band, inner),
    )
    weight = lax.ppermute(offered, "net", [(0, 1), (1, 0)])
    edges = jnp.stack([place > 0, place < size - 1]).astype(jnp.int32)
    shifted, packed = call(
        backward_kernel,
        (sds((planes + 2, 3 * rows, ww), BF), sds((4 * ch, 128), F32)),
        (SM, VM, VM, VM, VM, VM, VM, VM, VM, VM),
        [VM((27 * ch, rows), F32)],
        2 * 9 * rows * rows * planes * ww,
        (edges, x, up, down, weight, hidden_in, hidden_edge, diff_in, diff_edge, head),
    )
    grad_input = call(
        input_kernel,
        sds((ch, planes, hh, ww), BF),
        (VM, VM),
        [VM((rows, 9 * rows), BF)],
        pair_flops * planes // 2,
        (shifted, band),
    )
    rounds = [("dp", 1 << b) for b in range((lax.axis_size("dp") - 1).bit_length())]
    rounds += [("depth", 1 << b) for b in range((size - 1).bit_length())]
    for axis, bit in rounds:
        other = lax.ppermute(packed, axis, [(i, i ^ bit) for i in range(lax.axis_size(axis))])
        if (axis, bit) != rounds[-1]:
            packed = packed + other
    scale = 1.0 / (lax.axis_size("dp") * size * planes * hh * ww)
    grad_kernel, grad_bias, grad_head, grad_offset = call(
        functools.partial(unpack_kernel, scale),
        (sds((27, ch, ch), F32), sds((1, ch), F32), sds((classes, ch), F32), sds((1, classes), F32)),
        (VM, VM),
        [],
        1000,
        (packed, other),
    )
    return grad_input[None, None], grad_kernel[None], grad_bias, grad_head[None], grad_offset


def solution(mesh):
    in_specs = (
        P("net", "dp", None, "depth", None, None),
        P("dp", "depth", None, None),
        P("net", "dp", "depth", None, None),
        P("net", None, None, None),
        P("net", None),
        P("net", None, None),
        P("net", None),
    )
    out_specs = (
        P("net", "dp", None, "depth", None, None),
        P("net", None, None, None),
        P("net", None),
        P("net", None, None),
        P("net", None),
    )
    return jax.shard_map(body, mesh=mesh, in_specs=in_specs, out_specs=out_specs, check_vma=False)
```

time: 149 us -> 42.9 us (0.29)
  blocking collectives: 80.8 us -> 0 us
  matrix products: 32.3 us -> 0 us
  local copies, waits for them, and re-layouts: 16.6 us -> 2.16 us
  Pallas kernels: 0 us -> 12.9 us
  waiting for transfers between devices: 1.57 us -> 9.96 us
  starting transfers between devices: 12.3 us -> 14.9 us
    psum x1 -> x0, blocking collectives: 80.8 us -> none  [body(): lax.psum((kernel_grad, bias_grad, head_grad, offset_grad), ('dp', 'depth'))]
    dot_general x84 -> x0, matrix products: 32.3 us -> none  [the longest x27 10.8 us: transpose_correlate(): jnp.einsum('oc,odhw->cdhw', kernel[t], window, preferred_element_type=jnp...]
    pallas_call x0 -> x5, Pallas kernels: none -> 12.9 us  [call(): pl.pallas_call(kernel, out_shape=out_shape, in_specs=[pl.BlockSpec(memory...]
    unnamed x44 -> x17, local copies, waits for them, and re-layouts: 14.6 us -> 2.14 us
    ppermute x5 -> x7, waiting for transfers between devices: 1.57 us -> 9.96 us  [the longest x4 6.37 us: body(): lax.ppermute(packed, axis, [(i, i ^ bit) for i in range(lax.axis_size(axi...]
    ppermute x5 -> x7, starting transfers between devices: 12.3 us -> 14.9 us  [the longest x4 8.67 us: body(): lax.ppermute(packed, axis, [(i, i ^ bit) for i in range(lax.axis_size(axi...]
    slice x4 -> x2, local copies, waits for them, and re-layouts: 2 us -> 0.01 us  [edge(): tail = jnp.stack([label[own], mask[own]]).astype(BF)]
    another operation x0 -> x2, other arithmetic: none -> 1.76 us
  transfers between devices with their start and end apart: 5 -> 7, of which waited for: 2 -> 5; matrix products, arithmetic and copies ran while one was open for 9% -> 1% of each run, Pallas kernels for 0% -> 13%
where the time goes in v1:
time: 42.9 us; the launch traced here: 42.7 us
  starting transfers between devices  14.9 us (35%)
  Pallas kernels  12.9 us (30%)
  waiting for transfers between devices  9.96 us (23%)
  local copies, waits for them, and re-layouts  2.16 us (5%)
  other arithmetic  1.91 us (4%)
  between operations  0.83 us (2%)
    pallas_call x5, Pallas kernels, call(): pl.pallas_call(kernel, out_shape=out_shape, in_specs=[pl.BlockSpec(memory...  12.9 us
    ppermute x4, starting transfers between devices, body(): lax.ppermute(packed, axis, [(i, i ^ bit) for i in range(lax.axis_size(axi...  8.67 us
    ppermute x4, waiting for transfers between devices, body(): lax.ppermute(packed, axis, [(i, i ^ bit) for i in range(lax.axis_size(axi...  6.37 us
    ppermute x1, starting transfers between devices, body(): lax.ppermute(edge(planes - 2, planes - 1), 'depth', [(i, i + 1) for i in...  4.88 us
    ppermute x1, waiting for transfers between devices, body(): lax.ppermute(edge(0, 0), 'depth', [(i + 1, i) for i in range(size - 1)])  2.4 us
    unnamed x17, local copies, waits for them, and re-layouts  2.14 us
    another operation x2, other arithmetic  1.76 us
    ppermute x1, starting transfers between devices, body(): lax.ppermute(edge(0, 0), 'depth', [(i + 1, i) for i in range(size - 1)])  1.29 us
  transfers between devices with their start and end apart: 7, of which 5 were waited for; matrix products, arithmetic and copies ran while one was open for 1% of the time, Pallas kernels for 13%

profile of v1, /device:TPU:0, one launch (start us, length us, event | category | flops | bytes accessed | tf_op | source)
XLA Modules:
  0.0 42.7 jit_solution(8531283264343262791)
XLA Ops:
  0.6 0.0 copy-start.2
  0.6 0.0 copy-start.1
  0.7 0.0 copy-start
  0.7 0.0 copy-start.6
  0.7 0.0 copy-start.5
  0.7 0.0 copy-start.4
  0.7 0.0 copy-start.3
  0.7 0.9 %convert.16 = bf16[1,8,16,128]{3,2,1,0:T(8,128)(2,1)S(1)} convert(s32[1,8,16,128]{3,2,1,0:T(8,128)} %param.8) | non-fusion elementwise | flops 16384 | bytes 98304 | tf_op jit(solution)/shard_map/convert.11
  1.6 0.8 %convert.17 = bf16[1,1,8,16,128]{4,3,2,1,0:T(8,128)(2,1)S(1)} convert(s32[1,1,8,16,128]{4,3,2,1,0:T(8,128)} %param.9) | non-fusion elementwise | flops 16384 | bytes 98304 | tf_op jit(solution)/shard_map/convert.9
  2.5 1.1 %copy.20 = bf16[1,1,16,8,16,128]{5,4,2,3,1,0:T(8,128)(2,1)S(1)} copy(bf16[1,1,16,8,16,128]{5,4,3,2,1,0:T(8,128)(2,1)} %param.7) | data formatting | bytes 1048576 | tf_op args[0]
  3.6 4.9 %collective-permute-start = (bf16[34,16,128]{2,1,0:T(8,128)(2,1)S(1)}, bf16[34,16,128]{2,1,0:T(8,128)(2,1)S(1)}, u32[]{:S(2)}, u32[]{:S(2)}) collective-permute-start(bf16[34,16,128]{2,1,0:T(8,128)(2,1)S(1)} %pad_maximum_fusion), channel_id=1, source_target_pairs={{0,1},{1,2},{2,3},{3,4},{4,5},{5,6},{6,7},{8,9},{9,10},{10,11},{11... | collective-permute-start | bytes 417800 | tf_op jit(solution)/shard_map/ppermute | solution.py:314
  8.5 1.3 %collective-permute-start.1 = (bf16[34,16,128]{2,1,0:T(8,128)(2,1)S(1)}, bf16[34,16,128]{2,1,0:T(8,128)(2,1)S(1)}, u32[]{:S(2)}, u32[]{:S(2)}) collective-permute-start(bf16[34,16,128]{2,1,0:T(8,128)(2,1)S(1)} %pad_maximum_fusion.1), channel_id=1, source_target_pairs={{1,0},{2,1},{3,2},{4,3},{5,4},{6,5},{7,6},{9,8},{10,9},{11,10},{12... | collective-permute-start | bytes 417800 | tf_op jit(solution)/shard_map/ppermute | solution.py:315
  9.9 0.0 copy-done.6
  9.9 0.2 copy.13
  10.1 0.0 copy-done.2
  10.1 0.0 copy-done.1
  10.1 0.0 copy-done
  10.1 0.0 copy-done.5
  10.1 0.0 copy-done.4
  10.1 0.0 copy-done.3
  10.1 3.0 %shard_map.110 = (bf16[256,2304]{1,0:T(8,128)(2,1)S(1)}, bf16[6,256,128]{2,1,0:T(8,128)(2,1)S(1)}, f32[6,128,128]{2,1,0:T(8,128)S(1)}, f32[6,16,128]{2,1,0:T(8,128)S(1)}) custom-call(bf16[16,8,16,128]{3,2,1,0:T(8,128)(2,1)S(1)} %bitcast.29, s32[8,16,128]{2,1,0:T(8,128)S(1)} %bitcast.36, s32[8,16,128]{2,1,0:T(8,128)S(1)} %bitcast.34, ...), custom_call_target="tpu_custom_call" | custom-call | flops 905969664 | bytes 669536 | tf_op jit(solution)/shard_map/pallas_call | solution.py:290
  13.2 0.0 collective-permute-done.up_ref
  13.2 2.4 %collective-permute-done.1.down_ref = bf16[34,16,128]{2,1,0:T(8,128)(2,1)S(1)} collective-permute-done((bf16[34,16,128]{2,1,0:T(8,128)(2,1)S(1)}, bf16[34,16,128]{2,1,0:T(8,128)(2,1)S(1)}, u32[]{:S(2)}, u32[]{:S(2)}) %collective-permute-start.1) | collective-permute-done | bytes 139296 | tf_op jit(solution)/shard_map/ppermute | solution.py:315
  15.6 2.4 %shard_map.111 = (bf16[4,256,128]{2,1,0:T(8,128)(2,1)S(1)}, f32[4,128,128]{2,1,0:T(8,128)S(1)}, f32[10,16,128]{2,1,0:T(8,128)S(1)}) custom-call(bf16[16,8,16,128]{3,2,1,0:T(8,128)(2,1)S(1)} %bitcast.30, bf16[34,16,128]{2,1,0:T(8,128)(2,1)S(1)} %collective-permute-done.up_ref, bf16[34,16,128]{2,1,0:T(8,128)(2,1)S(1)} %collective-permute-done.1.down_ref, ...), custom_call_target="tpu_custom_call" | custom-call | flops 603979776 | bytes 2163040 | tf_op jit(solution)/shard_map/pallas_call | solution.py:290
  18.0 0.1 collective-permute-start.2
  18.1 0.1 add_convert_fusion.edge_ref
  18.1 1.2 %collective-permute-done.2.weight_ref = f32[10,16,128]{2,1,0:T(8,128)S(1)} collective-permute-done((f32[10,16,128]{2,1,0:T(8,128)S(1)}, f32[10,16,128]{2,1,0:T(8,128)S(1)}, u32[]{:S(2)}, u32[]{:S(2)}) %collective-permute-start.2) | collective-permute-done | bytes 81952 | tf_op jit(solution)/shard_map/ppermute | solution.py:343
  19.3 4.2 %shard_map.112 = (bf16[10,768,128]{2,1,0:T(8,128)(2,1)S(1)}, f32[64,128]{1,0:T(8,128)S(1)}) custom-call(s32[2]{0:T(128)S(1)} %add_convert_fusion.edge_ref, bf16[16,8,16,128]{3,2,1,0:T(8,128)(2,1)S(1)} %bitcast.31, bf16[34,16,128]{2,1,0:T(8,128)(2,1)S(1)} %collective-permute-done.up_ref, bf16[34,16,128]{2,1,0:T(8,128)(2,1)S(1)} %collective-permute-done.1.down_ref, ...), custom_call_target="tpu_custom_call" | custom-call | flops 1207959552 | bytes 2195720 | tf_op jit(solution)/shard_map/pallas_call | solution.py:290
  23.5 1.5 %collective-permute-start.3 = (f32[64,128]{1,0:T(8,128)S(1)}, f32[64,128]{1,0:T(8,128)S(1)}, u32[]{:S(2)}, u32[]{:S(2)}) collective-permute-start(f32[64,128]{1,0:T(8,128)S(1)} %get-tuple-element.26), channel_id=1, source_target_pairs={{0,8},{8,0},{1,9},{9,1},{2,10},{10,2},{3,11},{11,3},{4,12},{12,4},... | collective-permute-start | bytes 98312 | tf_op jit(solution)/shard_map/ppermute | solution.py:364
  25.0 2.4 %collective-permute-done.3 = f32[64,128]{1,0:T(8,128)S(1)} collective-permute-done((f32[64,128]{1,0:T(8,128)S(1)}, f32[64,128]{1,0:T(8,128)S(1)}, u32[]{:S(2)}, u32[]{:S(2)}) %collective-permute-start.3) | collective-permute-done | bytes 32800 | tf_op jit(solution)/shard_map/ppermute | solution.py:364
  27.5 2.4 %collective-permute-start.4 = (f32[64,128]{1,0:T(8,128)S(1)}, f32[64,128]{1,0:T(8,128)S(1)}, u32[]{:S(2)}, u32[]{:S(2)}) collective-permute-start(f32[64,128]{1,0:T(8,128)S(1)} %add.9), channel_id=1, source_target_pairs={{0,1},{1,0},{2,3},{3,2},{4,5},{5,4},{6,7},{7,6},{8,9},{9,8},{10,11... | collective-permute-start | bytes 98312 | tf_op jit(solution)/shard_map/ppermute | solution.py:364
  29.9 1.9 %collective-permute-done.4 = f32[64,128]{1,0:T(8,128)S(1)} collective-permute-done((f32[64,128]{1,0:T(8,128)S(1)}, f32[64,128]{1,0:T(8,128)S(1)}, u32[]{:S(2)}, u32[]{:S(2)}) %collective-permute-start.4) | collective-permute-done | bytes 32800 | tf_op jit(solution)/shard_map/ppermute | solution.py:364
  31.8 1.9 %collective-permute-start.5 = (f32[64,128]{1,0:T(8,128)S(1)}, f32[64,128]{1,0:T(8,128)S(1)}, u32[]{:S(2)}, u32[]{:S(2)}) collective-permute-start(f32[64,128]{1,0:T(8,128)S(1)} %add.10), channel_id=1, source_target_pairs={{0,2},{1,3},{2,0},{3,1},{4,6},{5,7},{6,4},{7,5},{8,10},{9,11},{10,... | collective-permute-start | bytes 98312 | tf_op jit(solution)/shard_map/ppermute | solution.py:364
  33.7 2.0 %collective-permute-done.5 = f32[64,128]{1,0:T(8,128)S(1)} collective-permute-done((f32[64,128]{1,0:T(8,128)S(1)}, f32[64,128]{1,0:T(8,128)S(1)}, u32[]{:S(2)}, u32[]{:S(2)}) %collective-permute-start.5) | collective-permute-done | bytes 32800 | tf_op jit(solution)/shard_map/ppermute | solution.py:364
  35.7 2.9 %collective-permute-start.6 = (f32[64,128]{1,0:T(8,128)S(1)}, f32[64,128]{1,0:T(8,128)S(1)}, u32[]{:S(2)}, u32[]{:S(2)}) collective-permute-start(f32[64,128]{1,0:T(8,128)S(1)} %add.11.a_ref), channel_id=1, source_target_pairs={{0,4},{1,5},{2,6},{3,7},{4,0},{5,1},{6,2},{7,3},{8,12},{9,13},{10,... | collective-permute-start | bytes 98312 | tf_op jit(solution)/shard_map/ppermute | solution.py:364
  38.6 2.6 %shard_map.113 = bf16[16,8,16,128]{3,2,1,0:T(8,128)(2,1)} custom-call(bf16[10,768,128]{2,1,0:T(8,128)(2,1)S(1)} %get-tuple-element.25.shifted_ref, bf16[256,2304]{1,0:T(8,128)(2,1)S(1)} %get-tuple-element.18.band_ref), custom_call_target="tpu_custom_call" | custom-call | flops 1207959552 | bytes 3145728 | tf_op jit(solution)/shard_map/pallas_call | solution.py:290
  41.2 0.0 collective-permute-done.6.b_ref
  41.2 0.7 %shard_map.114 = (f32[27,16,16]{2,1,0:T(8,128)S(1)}, f32[1,16]{1,0:T(1,128)}, f32[8,16]{1,0:T(8,128)}, f32[1,8]{1,0:T(1,128)}) custom-call(f32[64,128]{1,0:T(8,128)S(1)} %add.11.a_ref, f32[64,128]{1,0:T(8,128)S(1)} %collective-permute-done.6.b_ref), custom_call_target="tpu_custom_call" | custom-call | flops 1000 | bytes 65536 | tf_op jit(solution)/shard_map/pallas_call | solution.py:290
  41.8 0.8 %copy.17 = f32[1,27,16,16]{1,3,2,0:T(8,128)} copy(f32[1,27,16,16]{3,2,1,0:T(8,128)S(1)} %bitcast.32) | data formatting | bytes 55296
  (8 shorter events, 0.1 us)
Async XLA Ops:
  0.6 9.4 %copy-start.2 = (s32[1,8,16,128]{3,2,1,0:T(8,128)S(1)}, s32[1,8,16,128]{3,2,1,0:T(8,128)}, u32[]{:S(2)}) copy-start(s32[1,8,16,128]{3,2,1,0:T(8,128)} %param.8) | copy-start | bytes 196612
  0.6 9.4 %copy-start.1 = (s32[1,1,8,16,128]{4,3,2,1,0:T(8,128)S(1)}, s32[1,1,8,16,128]{4,3,2,1,0:T(8,128)}, u32[]{:S(2)}) copy-start(s32[1,1,8,16,128]{4,3,2,1,0:T(8,128)} %param.9) | copy-start | bytes 196612
  0.7 9.4 %copy-start = (bf16[1,1,16,8,16,128]{5,4,3,2,1,0:T(8,128)(2,1)S(1)}, bf16[1,1,16,8,16,128]{5,4,3,2,1,0:T(8,128)(2,1)}, u32[]{:S(2)}) copy-start(bf16[1,1,16,8,16,128]{5,4,3,2,1,0:T(8,128)(2,1)} %param.7) | copy-start | bytes 1572868
  0.7 9.2 %copy-start.6 = (bf16[1,27,16,16]{1,3,2,0:T(8,128)(2,1)S(1)}, bf16[1,27,16,16]{1,3,2,0:T(8,128)(2,1)}, u32[]{:S(2)}) copy-start(bf16[1,27,16,16]{1,3,2,0:T(8,128)(2,1)} %param.10) | copy-start | bytes 41476
  0.7 9.4 %copy-start.5 = (f32[1,8]{1,0:T(1,128)S(1)}, f32[1,8]{1,0:T(1,128)}, u32[]{:S(2)}) copy-start(f32[1,8]{1,0:T(1,128)} %head_bias_ref.3) | copy-start | bytes 100
  0.7 9.4 %copy-start.4 = (f32[1,16]{1,0:T(1,128)S(1)}, f32[1,16]{1,0:T(1,128)}, u32[]{:S(2)}) copy-start(f32[1,16]{1,0:T(1,128)} %bias_ref.3) | copy-start | bytes 196
  0.7 9.4 %copy-start.3 = (bf16[1,8,16]{2,1,0:T(8,128)(2,1)S(1)}, bf16[1,8,16]{2,1,0:T(8,128)(2,1)}, u32[]{:S(2)}) copy-start(bf16[1,8,16]{2,1,0:T(8,128)(2,1)} %param.12) | copy-start | bytes 772
  3.6 9.5 %collective-permute-start = (bf16[34,16,128]{2,1,0:T(8,128)(2,1)S(1)}, bf16[34,16,128]{2,1,0:T(8,128)(2,1)S(1)}, u32[]{:S(2)}, u32[]{:S(2)}) collective-permute-start(bf16[34,16,128]{2,1,0:T(8,128)(2,1)S(1)} %pad_maximum_fusion), channel_id=1, source_target_pairs={{0,1},{1,2},{2,3},{3,4},{4,5},{5,6},{6,7},{8,9},{9,10},{10,11},{11... | collective-permute-start | bytes 417800 | tf_op jit(solution)/shard_map/ppermute | solution.py:314
  8.5 7.0 %collective-permute-start.1 = (bf16[34,16,128]{2,1,0:T(8,128)(2,1)S(1)}, bf16[34,16,128]{2,1,0:T(8,128)(2,1)S(1)}, u32[]{:S(2)}, u32[]{:S(2)}) collective-permute-start(bf16[34,16,128]{2,1,0:T(8,128)(2,1)S(1)} %pad_maximum_fusion.1), channel_id=1, source_target_pairs={{1,0},{2,1},{3,2},{4,3},{5,4},{6,5},{7,6},{9,8},{10,9},{11,10},{12... | collective-permute-start | bytes 417800 | tf_op jit(solution)/shard_map/ppermute | solution.py:315
  18.0 1.3 %collective-permute-start.2 = (f32[10,16,128]{2,1,0:T(8,128)S(1)}, f32[10,16,128]{2,1,0:T(8,128)S(1)}, u32[]{:S(2)}, u32[]{:S(2)}) collective-permute-start(f32[10,16,128]{2,1,0:T(8,128)S(1)} %get-tuple-element.20), channel_id=1, source_target_pairs={{0,16},{16,0},{1,17},{17,1},{2,18},{18,2},{3,19},{19,3},{4,20},{20... | collective-permute-start | bytes 245768 | tf_op jit(solution)/shard_map/ppermute | solution.py:343
  23.5 3.9 %collective-permute-start.3 = (f32[64,128]{1,0:T(8,128)S(1)}, f32[64,128]{1,0:T(8,128)S(1)}, u32[]{:S(2)}, u32[]{:S(2)}) collective-permute-start(f32[64,128]{1,0:T(8,128)S(1)} %get-tuple-element.26), channel_id=1, source_target_pairs={{0,8},{8,0},{1,9},{9,1},{2,10},{10,2},{3,11},{11,3},{4,12},{12,4},... | collective-permute-start | bytes 98312 | tf_op jit(solution)/shard_map/ppermute | solution.py:364
  27.5 4.3 %collective-permute-start.4 = (f32[64,128]{1,0:T(8,128)S(1)}, f32[64,128]{1,0:T(8,128)S(1)}, u32[]{:S(2)}, u32[]{:S(2)}) collective-permute-start(f32[64,128]{1,0:T(8,128)S(1)} %add.9), channel_id=1, source_target_pairs={{0,1},{1,0},{2,3},{3,2},{4,5},{5,4},{6,7},{7,6},{8,9},{9,8},{10,11... | collective-permute-start | bytes 98312 | tf_op jit(solution)/shard_map/ppermute | solution.py:364
  31.8 3.9 %collective-permute-start.5 = (f32[64,128]{1,0:T(8,128)S(1)}, f32[64,128]{1,0:T(8,128)S(1)}, u32[]{:S(2)}, u32[]{:S(2)}) collective-permute-start(f32[64,128]{1,0:T(8,128)S(1)} %add.10), channel_id=1, source_target_pairs={{0,2},{1,3},{2,0},{3,1},{4,6},{5,7},{6,4},{7,5},{8,10},{9,11},{10,... | collective-permute-start | bytes 98312 | tf_op jit(solution)/shard_map/ppermute | solution.py:364
  35.7 5.5 %collective-permute-start.6 = (f32[64,128]{1,0:T(8,128)S(1)}, f32[64,128]{1,0:T(8,128)S(1)}, u32[]{:S(2)}, u32[]{:S(2)}) collective-permute-start(f32[64,128]{1,0:T(8,128)S(1)} %add.11.a_ref), channel_id=1, source_target_pairs={{0,4},{1,5},{2,6},{3,7},{4,0},{5,1},{6,2},{7,3},{8,12},{9,13},{10,... | collective-permute-start | bytes 98312 | tf_op jit(solution)/shard_map/ppermute | solution.py:364

commit v2 on v1

v2 whole, which is shorter than its diff:
```python
import functools

import jax
import jax.numpy as jnp
from jax import lax
from jax.experimental import pallas as pl
from jax.experimental.pallas import tpu as pltpu
from jax.sharding import PartitionSpec as P

BF = jnp.bfloat16
F32 = jnp.float32
VM = pltpu.VMEM
SM = pltpu.SMEM


def iota(shape, dim):
    return lax.broadcasted_iota(jnp.int32, shape, dim)


def dot(a, b):
    return jnp.dot(a, b, preferred_element_type=F32)


def dot_nt(a, b):
    return lax.dot_general(a, b, (((1,), (1,)), ((), ())), preferred_element_type=F32)


def split3(x):
    high = x.astype(BF)
    rest = x - high.astype(F32)
    mid = rest.astype(BF)
    return high, mid, (rest - mid.astype(F32)).astype(BF)


def dot_exact(x, ones):
    return sum(dot(part, ones) for part in split3(x))


def moved(x):
    y = x.astype(F32)
    lane = iota(y.shape, 1)
    width = y.shape[1]
    before = jnp.where(lane == 0, 0.0, pltpu.roll(y, 1, 1))
    after = jnp.where(lane == width - 1, 0.0, pltpu.roll(y, width - 1, 1))
    return before.astype(BF), after.astype(BF)


def fill_band(kernel_ref, band_ref, ch, hh):
    rows = ch * hh
    flat = kernel_ref[...].reshape(27 * ch, ch)
    spread = (iota((ch, rows), 1) // hh == iota((ch, rows), 0)).astype(F32).astype(BF)
    wide = dot(flat, spread).astype(BF)
    masks = [(iota((ch, rows), 1) % hh == h).astype(F32).astype(BF) for h in range(hh)]
    for i in range(3):
        for k in range(3):
            taps = [wide[(9 * i + 3 * j + k) * ch : (9 * i + 3 * j + k + 1) * ch] for j in range(3)]
            col = (3 * i + k) * rows
            for h in range(hh):
                block = masks[h] * taps[1]
                if h > 0:
                    block = block + masks[h - 1] * taps[0]
                if h < hh - 1:
                    block = block + masks[h + 1] * taps[2]
                band_ref[h * ch : (h + 1) * ch, col : col + rows] = block


def head_matrix(head_ref, ch, hh, classes):
    rows = ch * hh
    spread = (iota((ch, rows), 1) % ch == iota((ch, rows), 0)).astype(F32).astype(BF)
    wide = dot(head_ref[...], spread)
    wide = jnp.broadcast_to(wide[:, None, :], (classes, hh, rows))
    keep = iota((classes, hh, rows), 2) // ch == iota((classes, hh, rows), 1)
    return jnp.where(keep, wide, 0.0).reshape(classes * hh, rows).astype(BF)


def head_matrix_t(head_ref, ch, hh, classes):
    mat = head_matrix(head_ref, ch, hh, classes)
    rows = ch * hh
    unit = (iota((rows, rows), 0) == iota((rows, rows), 1)).astype(F32).astype(BF)
    return dot_nt(unit, mat).astype(BF)


def bias_rows(bias_ref, ch, width):
    out = jnp.zeros((ch, width), F32)
    sub = iota((ch, width), 0)
    for c in range(ch):
        out = jnp.where(sub == c, bias_ref[0, c], out)
    return out


def shifts(x):
    before, after = moved(x)
    return jnp.concatenate([before, x, after], axis=0)


def head_pair(preact, bias, mat, head_bias_ref, label, mask, dims):
    ch, hh, ww, classes = dims
    rows = ch * hh
    preact = (preact.reshape(hh, ch, 2 * ww) + bias[None]).reshape(rows, 2 * ww)
    hidden = jnp.maximum(preact, 0.0).astype(BF)
    logits = dot(mat, hidden).reshape(classes, hh, 2 * ww)
    parts = [logits[c] + head_bias_ref[0, c] for c in range(classes)]
    total = functools.reduce(jnp.add, [jnp.exp(p) for p in parts])
    log_total = jnp.log(total)
    soft = [jnp.exp(p - log_total) for p in parts]
    hot = [label == c for c in range(classes)]
    chosen = functools.reduce(jnp.add, [jnp.where(o, s, 0.0) for o, s in zip(hot, soft)])
    diffs = [s - jnp.where(o, 1.0, 0.0) for o, s in zip(hot, soft)]
    return hidden, jnp.stack(diffs).reshape(classes * hh, 2 * ww), mask * chosen


def put_pair(ref, first, second, value, ww):
    ref[first] = value[:, :ww]
    ref[second] = value[:, ww:]


def beside(ref, first, second):
    return jnp.concatenate([ref[first], ref[second]], axis=1)


def pack_kernel(x_ref, a_ref, b_ref, sems):
    planes = x_ref.shape[1]
    odd = lax.rem(lax.axis_index("depth"), 2)
    first = pltpu.make_async_copy(x_ref.at[:, (1 - odd) * (planes - 1)], a_ref, sems.at[0])
    second = pltpu.make_async_copy(x_ref.at[:, odd * (planes - 1)], b_ref, sems.at[1])
    first.start()
    second.start()
    first.wait()
    second.wait()


def sorted_halo(a, b):
    place, size = lax.axis_index("depth"), lax.axis_size("depth")
    odd = lax.rem(place, 2) == 1
    before, after = jnp.where(odd, a, b), jnp.where(odd, b, a)
    before = jnp.where(place > 0, before, 0.0)
    after = jnp.where(place < size - 1, after, 0.0)
    return before.astype(BF), after.astype(BF)


def interior_kernel(
    x_ref, label_ref, mask_ref, kernel_ref, bias_ref, head_ref, head_bias_ref,
    band_ref, shifted_ref, hidden_ref, diff_ref, offered_ref,
):
    ch, planes, hh, ww = x_ref.shape
    classes = head_ref.shape[0]
    rows = ch * hh
    fill_band(kernel_ref, band_ref, ch, hh)
    mat = head_matrix(head_ref, ch, hh, classes)
    bias = bias_rows(bias_ref, ch, 2 * ww)
    for d in range(planes):
        shifted_ref[d] = shifts(x_ref[:, d].reshape(rows, ww))
    for d in range(1, planes - 1, 2):
        left = shifted_ref[d - 1 : d + 2].reshape(9 * rows, ww)
        right = shifted_ref[d : d + 3].reshape(9 * rows, ww)
        preact = dot(band_ref[...], jnp.concatenate([left, right], axis=1))
        hidden, diff, offered = head_pair(
            preact, bias, mat, head_bias_ref, beside(label_ref, d, d + 1),
            beside(mask_ref, d, d + 1).astype(F32), (ch, hh, ww, classes),
        )
        put_pair(hidden_ref, d - 1, d, hidden, ww)
        put_pair(diff_ref, d - 1, d, diff, ww)
        put_pair(offered_ref, d - 1, d, offered, ww)


def edge_kernel(
    a_ref, b_ref, label_ref, mask_ref, bias_ref, head_ref, head_bias_ref, band_ref, shifted_ref, inner_ref,
    halo_ref, hidden_ref, diff_ref, offered_ref,
):
    ch, hh, ww = a_ref.shape
    planes, classes = label_ref.shape[0], head_ref.shape[0]
    rows = ch * hh
    mat = head_matrix(head_ref, ch, hh, classes)
    bias = bias_rows(bias_ref, ch, 2 * ww)
    offered_ref[1 : planes - 1] = inner_ref[...]
    before, after = sorted_halo(a_ref[...].reshape(rows, ww).astype(F32), b_ref[...].reshape(rows, ww).astype(F32))
    halo_ref[0], halo_ref[1] = before, after
    left = jnp.concatenate([shifts(before), shifted_ref[0:2].reshape(6 * rows, ww)], axis=0)
    right = jnp.concatenate([shifted_ref[planes - 2 : planes].reshape(6 * rows, ww), shifts(after)], axis=0)
    preact = dot(band_ref[...], jnp.concatenate([left, right], axis=1))
    hidden, diff, offered = head_pair(
        preact, bias, mat, head_bias_ref, beside(label_ref, 0, planes - 1),
        beside(mask_ref, 0, planes - 1).astype(F32), (ch, hh, ww, classes),
    )
    put_pair(hidden_ref, 0, 1, hidden, ww)
    put_pair(diff_ref, 0, 1, diff, ww)
    put_pair(offered_ref, 0, planes - 1, offered, ww)


def backward_kernel(
    x_ref, halo_ref, weight_ref, hidden_in_ref, hidden_edge_ref, diff_in_ref, diff_edge_ref, head_ref,
    packed_ref, a_ref, b_ref, shifted_ref, rows_ref,
):
    ch, planes, hh, ww = x_ref.shape
    classes = head_ref.shape[0]
    rows = ch * hh
    mat_t = head_matrix_t(head_ref, ch, hh, classes)
    bias_sum = jnp.zeros((rows, ww), F32)
    offset_sum = jnp.zeros((classes * hh, ww), F32)
    hiddens, halves, values = [], [], []
    for d in range(planes):
        if d == 0 or d == planes - 1:
            hiddens.append(hidden_edge_ref[min(d, 1)])
            diff = diff_edge_ref[min(d, 1)]
        else:
            hiddens.append(hidden_in_ref[d - 1])
            diff = diff_in_ref[d - 1]
        grad = (diff.reshape(classes, hh, ww) * weight_ref[d][None]).reshape(classes * hh, ww)
        offset_sum = offset_sum + grad
        halves.append(grad.astype(BF))
    for d in range(0, planes, 2):
        pre = dot(mat_t, jnp.concatenate(halves[d : d + 2], axis=1))
        for p in range(2):
            value = jnp.where(hiddens[d + p].astype(F32) > 0.0, pre[:, p * ww : (p + 1) * ww], 0.0)
            bias_sum = bias_sum + value
            value = value.astype(BF)
            values.append(value)
            before, after = moved(value)
            shifted_ref[d + p] = jnp.concatenate([after, value, before], axis=0)
    odd = lax.rem(lax.axis_index("depth"), 2) == 1
    first, last = values[0].astype(F32), values[-1].astype(F32)
    a_ref[...] = jnp.where(odd, first, last).astype(BF)
    b_ref[...] = jnp.where(odd, last, first).astype(BF)
    grad_cat = jnp.concatenate([shifted_ref[d] for d in range(planes)], axis=1)
    field = [halo_ref[0]] + [x_ref[:, d].reshape(rows, ww) for d in range(planes)] + [halo_ref[1]]
    place = iota((ch, rows), 1) % hh
    for i in range(3):
        product = dot_nt(grad_cat, jnp.concatenate(field[i : i + planes], axis=1))
        for k in range(3):
            for j in range(3):
                total = jnp.zeros((ch, rows), F32)
                for h in range(hh):
                    if 0 <= h + j - 1 < hh:
                        r = k * rows + h * ch
                        total = jnp.where(place == h + j - 1, product[r : r + ch], total)
                t = 9 * i + 3 * j + k
                for half in range(rows // 128):
                    rows_ref[half, pl.ds(t, ch, stride=32)] = total[:, 128 * half : 128 * half + 128]
    for half in range(rows // 128):
        for t in range(27, 32):
            rows_ref[half, pl.ds(t, ch, stride=32)] = jnp.zeros((ch, 128), F32)
    sums = 0.0
    for half in range(rows // 128):
        pick = (iota((ch, 128), 1) + 128 * half) // hh == iota((ch, 128), 0)
        pick = pick.astype(F32).astype(BF)
        sums = sums + sum(dot_nt(pick, part) for part in split3(rows_ref[half]))
    for q in range(ch // 4):
        packed_ref[q * ch : (q + 1) * ch] = sums[:, 128 * q : 128 * q + 128]
    product = dot_nt(jnp.concatenate(halves, axis=1), jnp.concatenate(hiddens, axis=1))
    product = product.reshape(classes, hh, rows)
    keep = iota((classes, hh, rows), 2) // ch == iota((classes, hh, rows), 1)
    head = jnp.sum(jnp.where(keep, product, 0.0), axis=1)
    by_last = (iota((rows, 128), 0) % ch == iota((rows, 128), 1) % 16).astype(F32).astype(BF)
    head = dot_exact(head, by_last)
    ones = jnp.ones((16, ww), F32).astype(BF)
    bias = jnp.sum(bias_sum.reshape(hh, ch, ww), axis=0)
    bias = jnp.concatenate([bias] * 8, axis=0)
    bias = sum(dot_nt(ones, part) for part in split3(bias))[:classes]
    offset = sum(dot_nt(ones, part) for part in split3(offset_sum))
    by_class = (iota((classes * hh, 128), 0) // hh == iota((classes * hh, 128), 1) % 16).astype(F32).astype(BF)
    offset = dot_exact(offset, by_class)[:classes]
    group = iota((classes, 128), 1) // 16
    packed_ref[4 * ch : 4 * ch + classes] = jnp.where(group == 0, head, jnp.where(group == 1, bias, offset))


def inner_grad_kernel(shifted_ref, band_ref, turned_ref, out_ref):
    ch, inner, hh, ww = out_ref.shape
    rows = ch * hh
    unit = (iota((rows, rows), 0) == iota((rows, rows), 1)).astype(F32).astype(BF)
    for i in range(3):
        for k in range(3):
            block = band_ref[:, (3 * i + k) * rows : (3 * i + k + 1) * rows]
            col = (3 * (2 - i) + k) * rows
            turned_ref[:, col : col + rows] = dot_nt(unit, block).astype(BF)
    for d in range(0, inner, 2):
        left = shifted_ref[d : d + 3].reshape(9 * rows, ww)
        right = shifted_ref[d + 1 : d + 4].reshape(9 * rows, ww)
        grad = dot(turned_ref[...], jnp.concatenate([left, right], axis=1)).astype(BF)
        out_ref[:, d] = grad[:, :ww].reshape(ch, hh, ww)
        out_ref[:, d + 1] = grad[:, ww:].reshape(ch, hh, ww)


def edge_grad_kernel(a_ref, b_ref, shifted_ref, turned_ref, inner_ref, out_ref):
    ch, planes, hh, ww = out_ref.shape
    rows = ch * hh

    def turned_shifts(x):
        before, after = moved(x)
        return jnp.concatenate([after, x, before], axis=0)

    before, after = sorted_halo(a_ref[...].astype(F32), b_ref[...].astype(F32))
    left = jnp.concatenate([turned_shifts(before), shifted_ref[0:2].reshape(6 * rows, ww)], axis=0)
    right = jnp.concatenate([shifted_ref[planes - 2 : planes].reshape(6 * rows, ww), turned_shifts(after)], axis=0)
    grad = dot(turned_ref[...], jnp.concatenate([left, right], axis=1)).astype(BF)
    out_ref[:, 0] = grad[:, :ww].reshape(ch, hh, ww)
    out_ref[:, 1 : planes - 1] = inner_ref[...]
    out_ref[:, planes - 1] = grad[:, ww:].reshape(ch, hh, ww)


def unpack_kernel(scale, a_ref, b_ref, kernel_ref, bias_ref, head_ref, offset_ref):
    ch = kernel_ref.shape[0]
    for q in range(ch // 4):
        value = (a_ref[q * ch : (q + 1) * ch] + b_ref[q * ch : (q + 1) * ch]) * scale
        for r in range(4):
            turned = pltpu.roll(value, 128 - 32 * r, 1) if r else value
            kernel_ref[4 * q + r] = turned[:, 0:27]
    value = (a_ref[4 * ch :] + b_ref[4 * ch :]) * scale
    head_ref[...] = value[:, 0:16]
    bias_ref[...] = pltpu.roll(value, 112, 1)[0:1, 0:16]
    offset_ref[...] = pltpu.roll(value, 96, 1)[0:1, 0:8]


def call(kernel, out_shape, in_spaces, scratch, flops, args):
    moved_bytes = sum(a.size * a.dtype.itemsize for a in args)
    return pl.pallas_call(
        kernel,
        out_shape=out_shape,
        in_specs=[pl.BlockSpec(memory_space=s) for s in in_spaces],
        out_specs=jax.tree.map(lambda _: pl.BlockSpec(memory_space=VM), out_shape),
        scratch_shapes=scratch,
        compiler_params=pltpu.CompilerParams(vmem_limit_bytes=32 << 20),
        cost_estimate=pl.CostEstimate(flops=flops, bytes_accessed=moved_bytes, transcendentals=0),
    )(*args)


def exchange_pairs():
    crops, size = lax.axis_size("dp"), lax.axis_size("depth")
    one, two = [], []
    for c in range(crops):
        for d in range(size):
            one.append((c * size + d, c * size + (d ^ 1)))
            e = ((d + 1) ^ 1) - 1
            if 0 <= e < size:
                two.append((c * size + d, c * size + e))
            elif crops % 2 == 0:
                two.append((c * size + d, (c ^ 1) * size + d))
    return one, two


def exchanged(a, b):
    one, two = exchange_pairs()
    return lax.ppermute(a, ("dp", "depth"), one), lax.ppermute(b, ("dp", "depth"), two)


def body(features, labels, masks, conv_kernel, conv_bias, head_weight, head_bias):
    x, label, mask = features[0, 0], labels[0], masks[0, 0]
    kernel, head = conv_kernel[0], head_weight[0]
    ch, planes, hh, ww = x.shape
    classes = head.shape[0]
    rows = ch * hh
    sds = jax.ShapeDtypeStruct
    size = lax.axis_size("depth")
    pair_flops = 2 * rows * 9 * rows * 2 * ww

    plane = sds((ch, hh, ww), BF)
    ends = call(pack_kernel, (plane, plane), (pltpu.HBM,), [pltpu.SemaphoreType.DMA((2,))], 0, (x,))
    far = exchanged(*ends)
    band, shifted, hidden_in, diff_in, inner = call(
        interior_kernel,
        (
            sds((rows, 9 * rows), BF),
            sds((planes, 3 * rows, ww), BF),
            sds((planes - 2, rows, ww), BF),
            sds((planes - 2, classes * hh, ww), F32),
            sds((planes - 2, hh, ww), F32),
        ),
        (VM, VM, VM, VM, SM, VM, SM),
        [],
        pair_flops * (planes // 2 - 1),
        (x, label, mask, kernel, conv_bias, head, head_bias),
    )
    halo, hidden_edge, diff_edge, offered = call(
        edge_kernel,
        (
            sds((2, rows, ww), BF),
            sds((2, rows, ww), BF),
            sds((2, classes * hh, ww), F32),
            sds((planes, hh, ww), F32),
        ),
        (VM, VM, VM, VM, SM, VM, SM, VM, VM, VM),
        [],
        pair_flops,
        (*far, label, mask, conv_bias, head, head_bias, band, shifted, inner),
    )
    weight = lax.ppermute(offered, "net", [(0, 1), (1, 0)])
    edge = sds((rows, ww), BF)
    packed, grad_a, grad_b, grads = call(
        backward_kernel,
        (sds((4 * ch + 8, 128), F32), edge, edge, sds((planes, 3 * rows, ww), BF)),
        (VM,) * 8,
        [VM((rows // 128, 32 * ch, 128), F32)],
        2 * 9 * rows * rows * planes * ww,
        (x, halo, weight, hidden_in, hidden_edge, diff_in, diff_edge, head),
    )
    grad_far = exchanged(grad_a, grad_b)
    turned, grad_inner = call(
        inner_grad_kernel,
        (sds((rows, 9 * rows), BF), sds((ch, planes - 2, hh, ww), BF)),
        (VM, VM),
        [],
        pair_flops * (planes // 2 - 1),
        (grads, band),
    )
    grad_input = call(
        edge_grad_kernel,
        sds((ch, planes, hh, ww), BF),
        (VM,) * 5,
        [],
        pair_flops,
        (*grad_far, grads, turned, grad_inner),
    )
    rounds = [("dp", 1 << b) for b in range((lax.axis_size("dp") - 1).bit_length())]
    rounds += [("depth", 1 << b) for b in range((size - 1).bit_length())]
    for axis, bit in rounds:
        other = lax.ppermute(packed, axis, [(i, i ^ bit) for i in range(lax.axis_size(axis))])
        if (axis, bit) != rounds[-1]:
            packed = packed + other
    scale = 1.0 / (lax.axis_size("dp") * size * planes * hh * ww)
    grad_kernel, grad_bias, grad_head, grad_offset = call(
        functools.partial(unpack_kernel, scale),
        (sds((ch, ch, 27), F32), sds((1, ch), F32), sds((classes, ch), F32), sds((1, classes), F32)),
        (VM, VM),
        [],
        1000,
        (packed, other),
    )
    return (
        grad_input[None, None],
        grad_kernel.transpose(2, 0, 1)[None],
        grad_bias,
        grad_head[None],
        grad_offset,
    )


def solution(mesh):
    in_specs = (
        P("net", "dp", None, "depth", None, None),
        P("dp", "depth", None, None),
        P("net", "dp", "depth", None, None),
        P("net", None, None, None),
        P("net", None),
        P("net", None, None),
        P("net", None),
    )
    out_specs = (
        P("net", "dp", None, "depth", None, None),
        P("net", None, None, None),
        P("net", None),
        P("net", None, None),
        P("net", None),
    )
    return jax.shard_map(body, mesh=mesh, in_specs=in_specs, out_specs=out_specs, check_vma=False)
```

time: 42.9 us -> 40.2 us (0.937)
  local copies, waits for them, and re-layouts: 2.16 us -> 6.78 us
  waiting for transfers between devices: 9.96 us -> 7.2 us
  other arithmetic: 1.91 us -> 0.02 us
  starting transfers between devices: 14.9 us -> 13.1 us
  Pallas kernels: 12.9 us -> 12 us
    unnamed x17 -> x19, local copies, waits for them, and re-layouts: 2.14 us -> 6.78 us
    ppermute x4, starting transfers between devices: 8.67 us -> 4.97 us  [body(): lax.ppermute(packed, axis, [(i, i ^ bit) for i in range(lax.axis_size(axi...]
    ppermute x2 -> x4, waiting for transfers between devices: 2.4 us -> 0.01 us  [the longest x2 0.01 us: exchanged(): lax.ppermute(b, ('dp', 'depth'), two)]
    ppermute x2 -> x4, starting transfers between devices: 6.17 us -> 8.04 us  [the longest x2 5.05 us: exchanged(): lax.ppermute(a, ('dp', 'depth'), one)]
    another operation x2 -> x0, other arithmetic: 1.76 us -> none
    pallas_call x5 -> x7, Pallas kernels: 12.9 us -> 12 us  [call(): pl.pallas_call(kernel, out_shape=out_shape, in_specs=[pl.BlockSpec(memory...]
  transfers between devices with their start and end apart: 7 -> 9, of which waited for: 5 -> 4; matrix products, arithmetic and copies ran while one was open for 1% -> 3% of each run, Pallas kernels for 13% -> 16%
where the time goes in v2:
time: 40.2 us; the launch traced here: 39.8 us
  starting transfers between devices  13.1 us (33%)
  Pallas kernels  12 us (30%)
  waiting for transfers between devices  7.2 us (18%)
  local copies, waits for them, and re-layouts  6.78 us (17%)
  between operations  0.75 us (2%)
    pallas_call x7, Pallas kernels, call(): pl.pallas_call(kernel, out_shape=out_shape, in_specs=[pl.BlockSpec(memory...  12 us
    unnamed x19, local copies, waits for them, and re-layouts  6.78 us
    ppermute x4, waiting for transfers between devices, body(): lax.ppermute(packed, axis, [(i, i ^ bit) for i in range(lax.axis_size(axi...  5.95 us
    ppermute x2, starting transfers between devices, exchanged(): lax.ppermute(a, ('dp', 'depth'), one)  5.05 us
    ppermute x4, starting transfers between devices, body(): lax.ppermute(packed, axis, [(i, i ^ bit) for i in range(lax.axis_size(axi...  4.97 us
    ppermute x2, starting transfers between devices, exchanged(): lax.ppermute(b, ('dp', 'depth'), two)  2.98 us
    ppermute x1, waiting for transfers between devices, body(): weight = lax.ppermute(offered, 'net', [(0, 1), (1, 0)])  1.24 us
  transfers between devices with their start and end apart: 9, of which 4 were waited for; matrix products, arithmetic and copies ran while one was open for 3% of the time, Pallas kernels for 16%

profile of v2, /device:TPU:0, one launch (start us, length us, event | category | flops | bytes accessed | tf_op | source)
XLA Modules:
  0.0 39.8 jit_solution(16581879189136186148)
XLA Ops:
  0.6 0.0 copy-start
  0.6 1.0 %copy-done = bf16[1,1,16,8,16,128]{5,4,3,2,1,0:T(8,128)(2,1)S(1)} copy-done((bf16[1,1,16,8,16,128]{5,4,3,2,1,0:T(8,128)(2,1)S(1)}, bf16[1,1,16,8,16,128]{5,4,3,2,1,0:T(8,128)(2,1)}, u32[]{:S(2)}) %copy-start) | copy-done | bytes 524312
  1.7 3.0 %collective-permute-start = (bf16[16,16,128]{2,1,0:T(8,128)(2,1)S(1)}, bf16[16,16,128]{2,1,0:T(8,128)(2,1)S(1)}, u32[]{:S(2)}, u32[]{:S(2)}) collective-permute-start(bf16[16,16,128]{2,1,0:T(8,128)(2,1)S(1)} %get-tuple-element.26), channel_id=1, source_target_pairs={{0,1},{1,0},{2,3},{3,2},{4,5},{5,4},{6,7},{7,6},{8,9},{9,8},{10,11... | collective-permute-start | bytes 196616 | tf_op jit(solution)/shard_map/ppermute | solution.py:342
  4.8 1.5 %collective-permute-start.1 = (bf16[16,16,128]{2,1,0:T(8,128)(2,1)S(1)}, bf16[16,16,128]{2,1,0:T(8,128)(2,1)S(1)}, u32[]{:S(2)}, u32[]{:S(2)}) collective-permute-start(bf16[16,16,128]{2,1,0:T(8,128)(2,1)S(1)} %get-tuple-element.27), channel_id=1, source_target_pairs={{0,8},{1,2},{2,1},{3,4},{4,3},{5,6},{6,5},{7,15},{8,0},{9,10},{10,... | collective-permute-start | bytes 196616 | tf_op jit(solution)/shard_map/ppermute | solution.py:342
  6.2 1.0 %copy.12 = bf16[1,27,16,16]{3,2,1,0:T(8,128)(2,1)S(1)} copy(bf16[1,27,16,16]{1,3,2,0:T(8,128)(2,1)} %param.10) | data formatting | bytes 27648 | tf_op args[3]
  7.3 0.0 copy-start.1
  7.3 1.0 %copy-done.1 = bf16[1,1,16,8,16,128]{5,4,3,2,1,0:T(8,128)(2,1)S(1)} copy-done((bf16[1,1,16,8,16,128]{5,4,3,2,1,0:T(8,128)(2,1)S(1)}, bf16[1,1,16,8,16,128]{5,4,3,2,1,0:T(8,128)(2,1)}, u32[]{:S(2)}) %copy-start.1) | copy-done | bytes 524312
  8.3 0.0 copy-start.3
  8.3 0.8 %copy-done.3 = s32[1,8,16,128]{3,2,1,0:T(8,128)S(1)} copy-done((s32[1,8,16,128]{3,2,1,0:T(8,128)S(1)}, s32[1,8,16,128]{3,2,1,0:T(8,128)}, u32[]{:S(2)}) %copy-start.3) | copy-done | bytes 65560
  9.2 0.0 copy-start.4
  9.2 0.8 %copy-done.4 = s32[1,1,8,16,128]{4,3,2,1,0:T(8,128)S(1)} copy-done((s32[1,1,8,16,128]{4,3,2,1,0:T(8,128)S(1)}, s32[1,1,8,16,128]{4,3,2,1,0:T(8,128)}, u32[]{:S(2)}) %copy-start.4) | copy-done | bytes 65560
  10.0 0.0 copy-start.5
  10.0 0.7 %copy-done.5 = bf16[1,8,16]{2,1,0:T(8,128)(2,1)S(1)} copy-done((bf16[1,8,16]{2,1,0:T(8,128)(2,1)S(1)}, bf16[1,8,16]{2,1,0:T(8,128)(2,1)}, u32[]{:S(2)}) %copy-start.5) | copy-done | bytes 280
  10.7 0.0 copy-start.7
  10.7 0.7 %copy-done.7 = f32[1,16]{1,0:T(1,128)S(1)} copy-done((f32[1,16]{1,0:T(1,128)S(1)}, f32[1,16]{1,0:T(1,128)}, u32[]{:S(2)}) %copy-start.7) | copy-done | bytes 88
  11.3 0.0 copy-start.8
  11.3 0.7 %copy-done.8 = f32[1,8]{1,0:T(1,128)S(1)} copy-done((f32[1,8]{1,0:T(1,128)S(1)}, f32[1,8]{1,0:T(1,128)}, u32[]{:S(2)}) %copy-start.8) | copy-done | bytes 56
  12.0 3.0 %shard_map.111 = (bf16[256,2304]{1,0:T(8,128)(2,1)S(1)}, bf16[8,768,128]{2,1,0:T(8,128)(2,1)S(1)}, bf16[6,256,128]{2,1,0:T(8,128)(2,1)S(1)}, f32[6,128,128]{2,1,0:T(8,128)S(1)}, f32[6,16,128]{2,1,0:T(8,128)S(1)}) custom-call(bf16[16,8,16,128]{3,2,1,0:T(8,128)(2,1)S(1)} %bitcast.11, s32[8,16,128]{2,1,0:T(8,128)S(1)} %bitcast.14, s32[8,16,128]{2,1,0:T(8,128)S(1)} %bitcast.16, ...), custom_call_target="tpu_custom_call" | custom-call | flops 905969664 | bytes 669536 | tf_op jit(solution)/shard_map/pallas_call | solution.py:315
  15.0 0.0 copy-start.2
  15.0 0.0 copy-start.6
  15.0 0.0 collective-permute-done.a_ref
  15.0 0.0 collective-permute-done.1.b_ref
  15.1 1.3 %shard_map.112 = (bf16[2,256,128]{2,1,0:T(8,128)(2,1)S(1)}, bf16[2,256,128]{2,1,0:T(8,128)(2,1)S(1)}, f32[2,128,128]{2,1,0:T(8,128)S(1)}, f32[8,16,128]{2,1,0:T(8,128)S(1)}) custom-call(bf16[16,16,128]{2,1,0:T(8,128)(2,1)S(1)} %collective-permute-done.a_ref, bf16[16,16,128]{2,1,0:T(8,128)(2,1)S(1)} %collective-permute-done.1.b_ref, ...), custom_call_target="tpu_custom_call" | custom-call | flops 301989888 | bytes 3064160 | tf_op jit(solution)/shard_map/pallas_call | solution.py:315
  16.3 0.1 collective-permute-start.2
  16.4 1.2 %collective-permute-done.2.weight_ref = f32[8,16,128]{2,1,0:T(8,128)S(1)} collective-permute-done((f32[8,16,128]{2,1,0:T(8,128)S(1)}, f32[8,16,128]{2,1,0:T(8,128)S(1)}, u32[]{:S(2)}, u32[]{:S(2)}) %collective-permute-start.2) | collective-permute-done | bytes 65568 | tf_op jit(solution)/shard_map/ppermute | solution.py:385
  17.6 0.0 copy-done.2
  17.6 0.0 copy-done.6
  17.7 3.7 %shard_map.113 = (f32[72,128]{1,0:T(8,128)S(1)}, bf16[256,128]{1,0:T(8,128)(2,1)S(1)}, bf16[256,128]{1,0:T(8,128)(2,1)S(1)}, bf16[8,768,128]{2,1,0:T(8,128)(2,1)S(1)}) custom-call(bf16[16,8,16,128]{3,2,1,0:T(8,128)(2,1)S(1)} %bitcast.12, bf16[2,256,128]{2,1,0:T(8,128)(2,1)S(1)} %get-tuple-element.31.halo_ref, ...), custom_call_target="tpu_custom_call" | custom-call | flops 1207959552 | bytes 1769728 | tf_op jit(solution)/shard_map/pallas_call | solution.py:315
  21.3 0.6 %collective-permute-start.5 = (f32[72,128]{1,0:T(8,128)S(1)}, f32[72,128]{1,0:T(8,128)S(1)}, u32[]{:S(2)}, u32[]{:S(2)}) collective-permute-start(f32[72,128]{1,0:T(8,128)S(1)} %get-tuple-element.42), channel_id=1, source_target_pairs={{0,8},{8,0},{1,9},{9,1},{2,10},{10,2},{3,11},{11,3},{4,12},{12,4},... | collective-permute-start | bytes 110600 | tf_op jit(solution)/shard_map/ppermute | solution.py:415
  21.9 3.4 %collective-permute-done.5 = f32[72,128]{1,0:T(8,128)S(1)} collective-permute-done((f32[72,128]{1,0:T(8,128)S(1)}, f32[72,128]{1,0:T(8,128)S(1)}, u32[]{:S(2)}, u32[]{:S(2)}) %collective-permute-start.5) | collective-permute-done | bytes 36896 | tf_op jit(solution)/shard_map/ppermute | solution.py:415
  25.3 1.5 %collective-permute-start.6 = (f32[72,128]{1,0:T(8,128)S(1)}, f32[72,128]{1,0:T(8,128)S(1)}, u32[]{:S(2)}, u32[]{:S(2)}) collective-permute-start(f32[72,128]{1,0:T(8,128)S(1)} %add.9), channel_id=1, source_target_pairs={{0,1},{1,0},{2,3},{3,2},{4,5},{5,4},{6,7},{7,6},{8,9},{9,8},{10,11... | collective-permute-start | bytes 110600 | tf_op jit(solution)/shard_map/ppermute | solution.py:415
  26.9 2.4 %collective-permute-done.6 = f32[72,128]{1,0:T(8,128)S(1)} collective-permute-done((f32[72,128]{1,0:T(8,128)S(1)}, f32[72,128]{1,0:T(8,128)S(1)}, u32[]{:S(2)}, u32[]{:S(2)}) %collective-permute-start.6) | collective-permute-done | bytes 36896 | tf_op jit(solution)/shard_map/ppermute | solution.py:415
  29.3 1.1 %collective-permute-start.7 = (f32[72,128]{1,0:T(8,128)S(1)}, f32[72,128]{1,0:T(8,128)S(1)}, u32[]{:S(2)}, u32[]{:S(2)}) collective-permute-start(f32[72,128]{1,0:T(8,128)S(1)} %add.10), channel_id=1, source_target_pairs={{0,2},{1,3},{2,0},{3,1},{4,6},{5,7},{6,4},{7,5},{8,10},{9,11},{10,... | collective-permute-start | bytes 110600 | tf_op jit(solution)/shard_map/ppermute | solution.py:415
  30.4 2.0 %collective-permute-start.3 = (bf16[256,128]{1,0:T(8,128)(2,1)S(1)}, bf16[256,128]{1,0:T(8,128)(2,1)S(1)}, u32[]{:S(2)}, u32[]{:S(2)}) collective-permute-start(bf16[256,128]{1,0:T(8,128)(2,1)S(1)} %get-tuple-element.37), channel_id=1, source_target_pairs={{0,1},{1,0},{2,3},{3,2},{4,5},{5,4},{6,7},{7,6},{8,9},{9,8},{10,11... | collective-permute-start | bytes 196616 | tf_op jit(solution)/shard_map/ppermute | solution.py:342
  32.4 1.5 %collective-permute-start.4 = (bf16[256,128]{1,0:T(8,128)(2,1)S(1)}, bf16[256,128]{1,0:T(8,128)(2,1)S(1)}, u32[]{:S(2)}, u32[]{:S(2)}) collective-permute-start(bf16[256,128]{1,0:T(8,128)(2,1)S(1)} %get-tuple-element.38), channel_id=1, source_target_pairs={{0,8},{1,2},{2,1},{3,4},{4,3},{5,6},{6,5},{7,15},{8,0},{9,10},{10,... | collective-permute-start | bytes 196616 | tf_op jit(solution)/shard_map/ppermute | solution.py:342
  33.9 0.0 collective-permute-done.7
  33.9 1.7 %collective-permute-start.8 = (f32[72,128]{1,0:T(8,128)S(1)}, f32[72,128]{1,0:T(8,128)S(1)}, u32[]{:S(2)}, u32[]{:S(2)}) collective-permute-start(f32[72,128]{1,0:T(8,128)S(1)} %add.11.a_ref), channel_id=1, source_target_pairs={{0,4},{1,5},{2,6},{3,7},{4,0},{5,1},{6,2},{7,3},{8,12},{9,13},{10,... | collective-permute-start | bytes 110600 | tf_op jit(solution)/shard_map/ppermute | solution.py:415
  35.6 1.9 %shard_map.114 = (bf16[256,2304]{1,0:T(8,128)(2,1)S(1)}, bf16[16,6,16,128]{3,2,1,0:T(8,128)(2,1)S(1)}) custom-call(bf16[8,768,128]{2,1,0:T(8,128)(2,1)S(1)} %get-tuple-element.39.shifted_ref, bf16[256,2304]{1,0:T(8,128)(2,1)S(1)} %get-tuple-element.28.band_ref), custom_call_target="tpu_custom_call" | custom-call | flops 905969664 | bytes 2752512 | tf_op jit(solution)/shard_map/pallas_call | solution.py:315
  37.6 0.0 collective-permute-done.3.a_ref
  37.6 0.0 collective-permute-done.4.b_ref
  37.6 1.3 %shard_map.115 = bf16[16,8,16,128]{3,2,1,0:T(8,128)(2,1)} custom-call(bf16[256,128]{1,0:T(8,128)(2,1)S(1)} %collective-permute-done.3.a_ref, bf16[256,128]{1,0:T(8,128)(2,1)S(1)} %collective-permute-done.4.b_ref, bf16[8,768,128]{2,1,0:T(8,128)(2,1)S(1)} %get-tuple-element.39.shifted_ref, bf16[256,2304]{1,0:T(8,128)(2,1)S(1)} %get-tuple-element.40.turned_ref, ...), custom_call_target="tpu_custom_call" | custom-call | flops 301989888 | bytes 3276800 | tf_op jit(solution)/shard_map/pallas_call | solution.py:315
  38.9 0.1 collective-permute-done.8.b_ref
  39.1 0.8 %shard_map.116 = (f32[16,16,27]{2,1,0:T(8,128)}, f32[1,16]{1,0:T(1,128)}, f32[8,16]{1,0:T(8,128)}, f32[1,8]{1,0:T(1,128)}) custom-call(f32[72,128]{1,0:T(8,128)S(1)} %add.11.a_ref, f32[72,128]{1,0:T(8,128)S(1)} %collective-permute-done.8.b_ref), custom_call_target="tpu_custom_call" | custom-call | flops 1000 | bytes 73728 | tf_op jit(solution)/shard_map/pallas_call | solution.py:315
  (4 shorter events, 0.1 us)
Async XLA Ops:
  0.6 1.0 %copy-start = (bf16[1,1,16,8,16,128]{5,4,3,2,1,0:T(8,128)(2,1)S(1)}, bf16[1,1,16,8,16,128]{5,4,3,2,1,0:T(8,128)(2,1)}, u32[]{:S(2)}) copy-start(bf16[1,1,16,8,16,128]{5,4,3,2,1,0:T(8,128)(2,1)} %param.7) | copy-start | bytes 1572868
  1.7 13.3 %collective-permute-start = (bf16[16,16,128]{2,1,0:T(8,128)(2,1)S(1)}, bf16[16,16,128]{2,1,0:T(8,128)(2,1)S(1)}, u32[]{:S(2)}, u32[]{:S(2)}) collective-permute-start(bf16[16,16,128]{2,1,0:T(8,128)(2,1)S(1)} %get-tuple-element.26), channel_id=1, source_target_pairs={{0,1},{1,0},{2,3},{3,2},{4,5},{5,4},{6,7},{7,6},{8,9},{9,8},{10,11... | collective-permute-start | bytes 196616 | tf_op jit(solution)/shard_map/ppermute | solution.py:342
  4.8 10.3 %collective-permute-start.1 = (bf16[16,16,128]{2,1,0:T(8,128)(2,1)S(1)}, bf16[16,16,128]{2,1,0:T(8,128)(2,1)S(1)}, u32[]{:S(2)}, u32[]{:S(2)}) collective-permute-start(bf16[16,16,128]{2,1,0:T(8,128)(2,1)S(1)} %get-tuple-element.27), channel_id=1, source_target_pairs={{0,8},{1,2},{2,1},{3,4},{4,3},{5,6},{6,5},{7,15},{8,0},{9,10},{10,... | collective-permute-start | bytes 196616 | tf_op jit(solution)/shard_map/ppermute | solution.py:342
  7.3 1.0 %copy-start.1 = (bf16[1,1,16,8,16,128]{5,4,3,2,1,0:T(8,128)(2,1)S(1)}, bf16[1,1,16,8,16,128]{5,4,3,2,1,0:T(8,128)(2,1)}, u32[]{:S(2)}) copy-start(bf16[1,1,16,8,16,128]{5,4,3,2,1,0:T(8,128)(2,1)} %param.7) | copy-start | bytes 1572868
  8.3 0.8 %copy-start.3 = (s32[1,8,16,128]{3,2,1,0:T(8,128)S(1)}, s32[1,8,16,128]{3,2,1,0:T(8,128)}, u32[]{:S(2)}) copy-start(s32[1,8,16,128]{3,2,1,0:T(8,128)} %param.8) | copy-start | bytes 196612
  9.2 0.8 %copy-start.4 = (s32[1,1,8,16,128]{4,3,2,1,0:T(8,128)S(1)}, s32[1,1,8,16,128]{4,3,2,1,0:T(8,128)}, u32[]{:S(2)}) copy-start(s32[1,1,8,16,128]{4,3,2,1,0:T(8,128)} %param.9) | copy-start | bytes 196612
  10.0 0.7 %copy-start.5 = (bf16[1,8,16]{2,1,0:T(8,128)(2,1)S(1)}, bf16[1,8,16]{2,1,0:T(8,128)(2,1)}, u32[]{:S(2)}) copy-start(bf16[1,8,16]{2,1,0:T(8,128)(2,1)} %param.12) | copy-start | bytes 772
  10.7 0.7 %copy-start.7 = (f32[1,16]{1,0:T(1,128)S(1)}, f32[1,16]{1,0:T(1,128)}, u32[]{:S(2)}) copy-start(f32[1,16]{1,0:T(1,128)} %bias_ref.3) | copy-start | bytes 196
  11.3 0.7 %copy-start.8 = (f32[1,8]{1,0:T(1,128)S(1)}, f32[1,8]{1,0:T(1,128)}, u32[]{:S(2)}) copy-start(f32[1,8]{1,0:T(1,128)} %head_bias_ref.3) | copy-start | bytes 100
  15.0 2.6 %copy-start.2 = (bf16[1,1,16,8,16,128]{5,4,3,2,1,0:T(8,128)(2,1)S(1)}, bf16[1,1,16,8,16,128]{5,4,3,2,1,0:T(8,128)(2,1)}, u32[]{:S(2)}) copy-start(bf16[1,1,16,8,16,128]{5,4,3,2,1,0:T(8,128)(2,1)} %param.7) | copy-start | bytes 1572868
  15.0 2.6 %copy-start.6 = (bf16[1,8,16]{2,1,0:T(8,128)(2,1)S(1)}, bf16[1,8,16]{2,1,0:T(8,128)(2,1)}, u32[]{:S(2)}) copy-start(bf16[1,8,16]{2,1,0:T(8,128)(2,1)} %param.12) | copy-start | bytes 772
  16.3 1.3 %collective-permute-start.2 = (f32[8,16,128]{2,1,0:T(8,128)S(1)}, f32[8,16,128]{2,1,0:T(8,128)S(1)}, u32[]{:S(2)}, u32[]{:S(2)}) collective-permute-start(f32[8,16,128]{2,1,0:T(8,128)S(1)} %get-tuple-element.32), channel_id=1, source_target_pairs={{0,16},{16,0},{1,17},{17,1},{2,18},{18,2},{3,19},{19,3},{4,20},{20... | collective-permute-start | bytes 196616 | tf_op jit(solution)/shard_map/ppermute | solution.py:385
  21.3 4.0 %collective-permute-start.5 = (f32[72,128]{1,0:T(8,128)S(1)}, f32[72,128]{1,0:T(8,128)S(1)}, u32[]{:S(2)}, u32[]{:S(2)}) collective-permute-start(f32[72,128]{1,0:T(8,128)S(1)} %get-tuple-element.42), channel_id=1, source_target_pairs={{0,8},{8,0},{1,9},{9,1},{2,10},{10,2},{3,11},{11,3},{4,12},{12,4},... | collective-permute-start | bytes 110600 | tf_op jit(solution)/shard_map/ppermute | solution.py:415
  25.3 4.0 %collective-permute-start.6 = (f32[72,128]{1,0:T(8,128)S(1)}, f32[72,128]{1,0:T(8,128)S(1)}, u32[]{:S(2)}, u32[]{:S(2)}) collective-permute-start(f32[72,128]{1,0:T(8,128)S(1)} %add.9), channel_id=1, source_target_pairs={{0,1},{1,0},{2,3},{3,2},{4,5},{5,4},{6,7},{7,6},{8,9},{9,8},{10,11... | collective-permute-start | bytes 110600 | tf_op jit(solution)/shard_map/ppermute | solution.py:415
  29.3 4.6 %collective-permute-start.7 = (f32[72,128]{1,0:T(8,128)S(1)}, f32[72,128]{1,0:T(8,128)S(1)}, u32[]{:S(2)}, u32[]{:S(2)}) collective-permute-start(f32[72,128]{1,0:T(8,128)S(1)} %add.10), channel_id=1, source_target_pairs={{0,2},{1,3},{2,0},{3,1},{4,6},{5,7},{6,4},{7,5},{8,10},{9,11},{10,... | collective-permute-start | bytes 110600 | tf_op jit(solution)/shard_map/ppermute | solution.py:415
  30.4 7.2 %collective-permute-start.3 = (bf16[256,128]{1,0:T(8,128)(2,1)S(1)}, bf16[256,128]{1,0:T(8,128)(2,1)S(1)}, u32[]{:S(2)}, u32[]{:S(2)}) collective-permute-start(bf16[256,128]{1,0:T(8,128)(2,1)S(1)} %get-tuple-element.37), channel_id=1, source_target_pairs={{0,1},{1,0},{2,3},{3,2},{4,5},{5,4},{6,7},{7,6},{8,9},{9,8},{10,11... | collective-permute-start | bytes 196616 | tf_op jit(solution)/shard_map/ppermute | solution.py:342
  32.4 5.2 %collective-permute-start.4 = (bf16[256,128]{1,0:T(8,128)(2,1)S(1)}, bf16[256,128]{1,0:T(8,128)(2,1)S(1)}, u32[]{:S(2)}, u32[]{:S(2)}) collective-permute-start(bf16[256,128]{1,0:T(8,128)(2,1)S(1)} %get-tuple-element.38), channel_id=1, source_target_pairs={{0,8},{1,2},{2,1},{3,4},{4,3},{5,6},{6,5},{7,15},{8,0},{9,10},{10,... | collective-permute-start | bytes 196616 | tf_op jit(solution)/shard_map/ppermute | solution.py:342
  33.9 5.1 %collective-permute-start.8 = (f32[72,128]{1,0:T(8,128)S(1)}, f32[72,128]{1,0:T(8,128)S(1)}, u32[]{:S(2)}, u32[]{:S(2)}) collective-permute-start(f32[72,128]{1,0:T(8,128)S(1)} %add.11.a_ref), channel_id=1, source_target_pairs={{0,4},{1,5},{2,6},{3,7},{4,0},{5,1},{6,2},{7,3},{8,12},{9,13},{10,... | collective-permute-start | bytes 110600 | tf_op jit(solution)/shard_map/ppermute | solution.py:415

commit v3 on v2

--- a/solution.py
+++ b/solution.py
@@ -47,9 +47,12 @@
 
 def fill_band(kernel_ref, band_ref, ch, hh):
     rows = ch * hh
-    flat = kernel_ref[...].reshape(27 * ch, ch)
-    spread = (iota((ch, rows), 1) // hh == iota((ch, rows), 0)).astype(F32).astype(BF)
-    wide = dot(flat, spread).astype(BF)
+    unit = (iota((32, 27), 0) == iota((32, 27), 1)).astype(F32).astype(BF)
+    by_tap = dot_nt(unit, kernel_ref[...].reshape(ch * ch, 27))
+    wide = jnp.broadcast_to(by_tap[:27, None, :], (27, ch, ch * ch))
+    wide = jnp.where(iota((27, ch, ch * ch), 2) // ch == iota((27, ch, ch * ch), 1), wide, 0.0)
+    spread = (iota((ch * ch, rows), 1) // hh == iota((ch * ch, rows), 0) % ch).astype(F32).astype(BF)
+    wide = dot(wide.reshape(27 * ch, ch * ch).astype(BF), spread).astype(BF)
     masks = [(iota((ch, rows), 1) % hh == h).astype(F32).astype(BF) for h in range(hh)]
     for i in range(3):
         for k in range(3):
@@ -81,11 +84,9 @@
 
 
 def bias_rows(bias_ref, ch, width):
-    out = jnp.zeros((ch, width), F32)
-    sub = iota((ch, width), 0)
-    for c in range(ch):
-        out = jnp.where(sub == c, bias_ref[0, c], out)
-    return out
+    square = jnp.broadcast_to(bias_ref[...], (ch, ch))
+    column = jnp.sum(jnp.where(iota((ch, ch), 0) == iota((ch, ch), 1), square, 0.0), axis=1, keepdims=True)
+    return jnp.broadcast_to(column, (ch, width))
 
 
 def shifts(x):
@@ -99,7 +100,7 @@
     preact = (preact.reshape(hh, ch, 2 * ww) + bias[None]).reshape(rows, 2 * ww)
     hidden = jnp.maximum(preact, 0.0).astype(BF)
     logits = dot(mat, hidden).reshape(classes, hh, 2 * ww)
-    parts = [logits[c] + head_bias_ref[0, c] for c in range(classes)]
+    parts = [logits[c] + head_bias_ref[0:1, c : c + 1] for c in range(classes)]
     total = functools.reduce(jnp.add, [jnp.exp(p) for p in parts])
     log_total = jnp.log(total)
     soft = [jnp.exp(p - log_total) for p in parts]
@@ -118,15 +119,19 @@
     return jnp.concatenate([ref[first], ref[second]], axis=1)
 
 
-def pack_kernel(x_ref, a_ref, b_ref, sems):
-    planes = x_ref.shape[1]
+def load_kernel(*refs):
+    count = (len(refs) - 3) // 2
+    sources, targets, (a_ref, b_ref, sems) = refs[:count], refs[count : 2 * count], refs[2 * count :]
+    planes = sources[0].shape[1]
+    copies = [pltpu.make_async_copy(s, t, sems.at[n]) for n, (s, t) in enumerate(zip(sources, targets))]
+    for copy in copies:
+        copy.start()
+    copies[0].wait()
     odd = lax.rem(lax.axis_index("depth"), 2)
-    first = pltpu.make_async_copy(x_ref.at[:, (1 - odd) * (planes - 1)], a_ref, sems.at[0])
-    second = pltpu.make_async_copy(x_ref.at[:, odd * (planes - 1)], b_ref, sems.at[1])
-    first.start()
-    second.start()
-    first.wait()
-    second.wait()
+    a_ref[...] = targets[0][:, (1 - odd) * (planes - 1)]
+    b_ref[...] = targets[0][:, odd * (planes - 1)]
+    for copy in copies[1:]:
+        copy.wait()
 
 
 def sorted_halo(a, b):
@@ -353,8 +358,19 @@
     pair_flops = 2 * rows * 9 * rows * 2 * ww
 
     plane = sds((ch, hh, ww), BF)
-    ends = call(pack_kernel, (plane, plane), (pltpu.HBM,), [pltpu.SemaphoreType.DMA((2,))], 0, (x,))
-    far = exchanged(*ends)
+    inputs = (x, label, mask, kernel.transpose(1, 2, 0), conv_bias, head, head_bias)
+    inputs = tuple(pltpu.with_memory_space_constraint(v, pltpu.HBM) for v in inputs)
+    shapes = tuple(sds(v.shape, v.dtype) for v in inputs)
+    *inputs, end_a, end_b = call(
+        load_kernel,
+        (*shapes, plane, plane),
+        (pltpu.HBM,) * len(inputs),
+        [pltpu.SemaphoreType.DMA((len(inputs),))],
+        0,
+        inputs,
+    )
+    x, label, mask, kernel, conv_bias, head, head_bias = inputs
+    far = exchanged(end_a, end_b)
     band, shifted, hidden_in, diff_in, inner = call(
         interior_kernel,
         (
@@ -364,7 +380,7 @@
             sds((planes - 2, classes * hh, ww), F32),
             sds((planes - 2, hh, ww), F32),
         ),
-        (VM, VM, VM, VM, SM, VM, SM),
+        (VM,) * 7,
         [],
         pair_flops * (planes // 2 - 1),
         (x, label, mask, kernel, conv_bias, head, head_bias),
@@ -377,7 +393,7 @@
             sds((2, classes * hh, ww), F32),
             sds((planes, hh, ww), F32),
         ),
-        (VM, VM, VM, VM, SM, VM, SM, VM, VM, VM),
+        (VM,) * 10,
         [],
         pair_flops,
         (*far, label, mask, conv_bias, head, head_bias, band, shifted, inner),
@@ -392,7 +408,6 @@
         2 * 9 * rows * rows * planes * ww,
         (x, halo, weight, hidden_in, hidden_edge, diff_in, diff_edge, head),
     )
-    grad_far = exchanged(grad_a, grad_b)
     turned, grad_inner = call(
         inner_grad_kernel,
         (sds((rows, 9 * rows), BF), sds((ch, planes - 2, hh, ww), BF)),
@@ -401,6 +416,19 @@
         pair_flops * (planes // 2 - 1),
         (grads, band),
     )
+    rounds = [("dp", 1 << b) for b in range((lax.axis_size("dp") - 1).bit_length())]
+    rounds += [("depth", 1 << b) for b in range((size - 1).bit_length())]
+    ends, pairs, grad_far = [grad_a, grad_b], exchange_pairs(), []
+    for n, (axis, bit) in enumerate(rounds):
+        other = lax.ppermute(packed, axis, [(i, i ^ bit) for i in range(lax.axis_size(axis))])
+        if 1 <= n <= 2:
+            grad_far.append(lax.ppermute(ends[n - 1], ("dp", "depth"), pairs[n - 1]))
+        if n < len(rounds) - 1:
+            packed = packed + other
+        if n == 0:
+            packed, grad_inner, ends[0] = lax.optimization_barrier((packed, grad_inner, ends[0]))
+        if n == 1:
+            packed, ends[1] = lax.optimization_barrier((packed, ends[1]))
     grad_input = call(
         edge_grad_kernel,
         sds((ch, planes, hh, ww), BF),
@@ -409,12 +437,6 @@
         pair_flops,
         (*grad_far, grads, turned, grad_inner),
     )
-    rounds = [("dp", 1 << b) for b in range((lax.axis_size("dp") - 1).bit_length())]
-    rounds += [("depth", 1 << b) for b in range((size - 1).bit_length())]
-    for axis, bit in rounds:
-        other = lax.ppermute(packed, axis, [(i, i ^ bit) for i in range(lax.axis_size(axis))])
-        if (axis, bit) != rounds[-1]:
-            packed = packed + other
     scale = 1.0 / (lax.axis_size("dp") * size * planes * hh * ww)
     grad_kernel, grad_bias, grad_head, grad_offset = call(
         functools.partial(unpack_kernel, scale),

time: 40.2 us -> 34.3 us (0.85)
  local copies, waits for them, and re-layouts: 6.78 us -> 0 us
  starting transfers between devices: 13.1 us -> 13.9 us
    unnamed x19 -> x0, local copies, waits for them, and re-layouts: 6.78 us -> none
    ppermute x4, starting transfers between devices: 4.97 us -> 7.57 us  [body(): lax.ppermute(packed, axis, [(i, i ^ bit) for i in range(lax.axis_size(axi...]
    ppermute x2 -> x1, starting transfers between devices: 5.05 us -> 3.03 us  [exchanged(): lax.ppermute(a, ('dp', 'depth'), one)]
    ppermute x0 -> x2, starting transfers between devices: none -> 1.77 us  [body(): grad_far.append(lax.ppermute(ends[n - 1], ('dp', 'depth'), pairs[n - 1]))]
    ppermute x2 -> x1, starting transfers between devices: 2.98 us -> 1.49 us  [exchanged(): lax.ppermute(b, ('dp', 'depth'), two)]
  transfers between devices with their start and end apart: 9 -> 9, of which waited for: 4 -> 6; matrix products, arithmetic and copies ran while one was open for 3% -> 0% of each run, Pallas kernels for 16% -> 17%
where the time goes in v3:
time: 34.3 us; the launch traced here: 34.2 us
  starting transfers between devices  13.9 us (41%)
  Pallas kernels  12.2 us (36%)
  waiting for transfers between devices  7.36 us (21%)
  between operations  0.69 us (2%)
    pallas_call x7, Pallas kernels, call(): pl.pallas_call(kernel, out_shape=out_shape, in_specs=[pl.BlockSpec(memory...  12.2 us
    ppermute x4, starting transfers between devices, body(): lax.ppermute(packed, axis, [(i, i ^ bit) for i in range(lax.axis_size(axi...  7.57 us
    ppermute x4, waiting for transfers between devices, body(): lax.ppermute(packed, axis, [(i, i ^ bit) for i in range(lax.axis_size(axi...  5.99 us
    ppermute x1, starting transfers between devices, exchanged(): lax.ppermute(a, ('dp', 'depth'), one)  3.03 us
    ppermute x2, starting transfers between devices, body(): grad_far.append(lax.ppermute(ends[n - 1], ('dp', 'depth'), pairs[n - 1]))  1.77 us
    ppermute x1, starting transfers between devices, exchanged(): lax.ppermute(b, ('dp', 'depth'), two)  1.49 us
    ppermute x1, waiting for transfers between devices, body(): weight = lax.ppermute(offered, 'net', [(0, 1), (1, 0)])  1.24 us
  transfers between devices with their start and end apart: 9, of which 6 were waited for; matrix products, arithmetic and copies ran while one was open for 0% of the time, Pallas kernels for 17%

profile of v3, /device:TPU:0, one launch (start us, length us, event | category | flops | bytes accessed | tf_op | source)
XLA Modules:
  0.0 34.2 jit_solution(16971562604624890047)
XLA Ops:
  0.6 1.1 %shard_map.110 = (bf16[16,8,16,128]{3,2,1,0:T(8,128)(2,1)S(1)}, s32[8,16,128]{2,1,0:T(8,128)S(1)}, s32[8,16,128]{2,1,0:T(8,128)S(1)}, bf16[16,16,27]{2,1,0:T(8,1...) custom-call(bf16[16,8,16,128]{3,2,1,0:T(8,128)(2,1)} %bitcast.12, ...), custom_call_target="tpu_custom_call" | custom-call | bytes 669536 | tf_op jit(solution)/shard_map/pallas_call | solution.py:320
  1.8 3.0 %collective-permute-start = (bf16[16,16,128]{2,1,0:T(8,128)(2,1)S(1)}, bf16[16,16,128]{2,1,0:T(8,128)(2,1)S(1)}, u32[]{:S(2)}, u32[]{:S(2)}) collective-permute-start(bf16[16,16,128]{2,1,0:T(8,128)(2,1)S(1)} %get-tuple-element.39), channel_id=1, source_target_pairs={{0,1},{1,0},{2,3},{3,2},{4,5},{5,4},{6,7},{7,6},{8,9},{9,8},{10,11... | collective-permute-start | bytes 196616 | tf_op jit(solution)/shard_map/ppermute | solution.py:347
  4.8 1.5 %collective-permute-start.1 = (bf16[16,16,128]{2,1,0:T(8,128)(2,1)S(1)}, bf16[16,16,128]{2,1,0:T(8,128)(2,1)S(1)}, u32[]{:S(2)}, u32[]{:S(2)}) collective-permute-start(bf16[16,16,128]{2,1,0:T(8,128)(2,1)S(1)} %get-tuple-element.40), channel_id=1, source_target_pairs={{0,8},{1,2},{2,1},{3,4},{4,3},{5,6},{6,5},{7,15},{8,0},{9,10},{10,... | collective-permute-start | bytes 196616 | tf_op jit(solution)/shard_map/ppermute | solution.py:347
  6.3 2.6 %shard_map.111 = (bf16[256,2304]{1,0:T(8,128)(2,1)S(1)}, bf16[8,768,128]{2,1,0:T(8,128)(2,1)S(1)}, bf16[6,256,128]{2,1,0:T(8,128)(2,1)S(1)}, f32[6,128,128]{2,1,0:T(8,128)S(1)}, f32[6,16,128]{2,1,0:T(8,128)S(1)}) custom-call(bf16[16,8,16,128]{3,2,1,0:T(8,128)(2,1)S(1)} %get-tuple-element.38.x_ref, s32[8,16,128]{2,1,0:T(8,128)S(1)} %get-tuple-element.41.label_ref, ...), custom_call_target="tpu_custom_call" | custom-call | flops 905969664 | bytes 669536 | tf_op jit(solution)/shard_map/pallas_call | solution.py:320
  8.9 0.0 collective-permute-done.a_ref
  9.0 0.1 collective-permute-done.1.b_ref
  9.1 0.7 %shard_map.112 = (bf16[2,256,128]{2,1,0:T(8,128)(2,1)S(1)}, bf16[2,256,128]{2,1,0:T(8,128)(2,1)S(1)}, f32[2,128,128]{2,1,0:T(8,128)S(1)}, f32[8,16,128]{2,1,0:T(8,128)S(1)}) custom-call(bf16[16,16,128]{2,1,0:T(8,128)(2,1)S(1)} %collective-permute-done.a_ref, bf16[16,16,128]{2,1,0:T(8,128)(2,1)S(1)} %collective-permute-done.1.b_ref, ...), custom_call_target="tpu_custom_call" | custom-call | flops 301989888 | bytes 3064160 | tf_op jit(solution)/shard_map/pallas_call | solution.py:320
  9.8 0.1 collective-permute-start.2
  9.9 1.2 %collective-permute-done.2.weight_ref = f32[8,16,128]{2,1,0:T(8,128)S(1)} collective-permute-done((f32[8,16,128]{2,1,0:T(8,128)S(1)}, f32[8,16,128]{2,1,0:T(8,128)S(1)}, u32[]{:S(2)}, u32[]{:S(2)}) %collective-permute-start.2) | collective-permute-done | bytes 65568 | tf_op jit(solution)/shard_map/ppermute | solution.py:401
  11.1 3.7 %shard_map.113 = (f32[72,128]{1,0:T(8,128)S(1)}, bf16[256,128]{1,0:T(8,128)(2,1)S(1)}, bf16[256,128]{1,0:T(8,128)(2,1)S(1)}, bf16[8,768,128]{2,1,0:T(8,128)(2,1)S(1)}) custom-call(bf16[16,8,16,128]{3,2,1,0:T(8,128)(2,1)S(1)} %get-tuple-element.38.x_ref, bf16[2,256,128]{2,1,0:T(8,128)(2,1)S(1)} %get-tuple-element.50.halo_ref, ...), custom_call_target="tpu_custom_call" | custom-call | flops 1207959552 | bytes 1769728 | tf_op jit(solution)/shard_map/pallas_call | solution.py:320
  14.8 1.6 %collective-permute-start.3 = (f32[72,128]{1,0:T(8,128)S(1)}, f32[72,128]{1,0:T(8,128)S(1)}, u32[]{:S(2)}, u32[]{:S(2)}) collective-permute-start(f32[72,128]{1,0:T(8,128)S(1)} %get-tuple-element.56), channel_id=1, source_target_pairs={{0,8},{8,0},{1,9},{9,1},{2,10},{10,2},{3,11},{11,3},{4,12},{12,4},... | collective-permute-start | bytes 110600 | tf_op jit(solution)/shard_map/ppermute | solution.py:423
  16.3 1.9 %shard_map.114 = (bf16[256,2304]{1,0:T(8,128)(2,1)S(1)}, bf16[16,6,16,128]{3,2,1,0:T(8,128)(2,1)S(1)}) custom-call(bf16[8,768,128]{2,1,0:T(8,128)(2,1)S(1)} %get-tuple-element.57.shifted_ref, bf16[256,2304]{1,0:T(8,128)(2,1)S(1)} %get-tuple-element.47.band_ref), custom_call_target="tpu_custom_call" | custom-call | flops 905969664 | bytes 2752512 | tf_op jit(solution)/shard_map/pallas_call | solution.py:320
  18.3 0.5 %collective-permute-done.3 = f32[72,128]{1,0:T(8,128)S(1)} collective-permute-done((f32[72,128]{1,0:T(8,128)S(1)}, f32[72,128]{1,0:T(8,128)S(1)}, u32[]{:S(2)}, u32[]{:S(2)}) %collective-permute-start.3) | collective-permute-done | bytes 36896 | tf_op jit(solution)/shard_map/ppermute | solution.py:423
  18.8 1.4 %collective-permute-start.5 = (f32[72,128]{1,0:T(8,128)S(1)}, f32[72,128]{1,0:T(8,128)S(1)}, u32[]{:S(2)}, u32[]{:S(2)}) collective-permute-start(f32[72,128]{1,0:T(8,128)S(1)} %add.9), channel_id=1, source_target_pairs={{0,1},{1,0},{2,3},{3,2},{4,5},{5,4},{6,7},{7,6},{8,9},{9,8},{10,11... | collective-permute-start | bytes 110600 | tf_op jit(solution)/shard_map/ppermute | solution.py:423
  20.2 0.6 %collective-permute-start.4 = (bf16[256,128]{1,0:T(8,128)(2,1)S(1)}, bf16[256,128]{1,0:T(8,128)(2,1)S(1)}, u32[]{:S(2)}, u32[]{:S(2)}) collective-permute-start(bf16[256,128]{1,0:T(8,128)(2,1)S(1)} %get-tuple-element.60), channel_id=1, source_target_pairs={{0,1},{1,0},{2,3},{3,2},{4,5},{5,4},{6,7},{7,6},{8,9},{9,8},{10,11... | collective-permute-start | bytes 196616 | tf_op jit(solution)/shard_map/ppermute | solution.py:425
  20.8 2.2 %collective-permute-done.5 = f32[72,128]{1,0:T(8,128)S(1)} collective-permute-done((f32[72,128]{1,0:T(8,128)S(1)}, f32[72,128]{1,0:T(8,128)S(1)}, u32[]{:S(2)}, u32[]{:S(2)}) %collective-permute-start.5) | collective-permute-done | bytes 36896 | tf_op jit(solution)/shard_map/ppermute | solution.py:423
  23.1 1.2 %collective-permute-start.6 = (bf16[256,128]{1,0:T(8,128)(2,1)S(1)}, bf16[256,128]{1,0:T(8,128)(2,1)S(1)}, u32[]{:S(2)}, u32[]{:S(2)}) collective-permute-start(bf16[256,128]{1,0:T(8,128)(2,1)S(1)} %get-tuple-element.63), channel_id=1, source_target_pairs={{0,8},{1,2},{2,1},{3,4},{4,3},{5,6},{6,5},{7,15},{8,0},{9,10},{10,... | collective-permute-start | bytes 196616 | tf_op jit(solution)/shard_map/ppermute | solution.py:425
  24.3 1.4 %collective-permute-start.7 = (f32[72,128]{1,0:T(8,128)S(1)}, f32[72,128]{1,0:T(8,128)S(1)}, u32[]{:S(2)}, u32[]{:S(2)}) collective-permute-start(f32[72,128]{1,0:T(8,128)S(1)} %add.10), channel_id=1, source_target_pairs={{0,2},{1,3},{2,0},{3,1},{4,6},{5,7},{6,4},{7,5},{8,10},{9,11},{10,... | collective-permute-start | bytes 110600 | tf_op jit(solution)/shard_map/ppermute | solution.py:423
  25.7 2.6 %collective-permute-done.7 = f32[72,128]{1,0:T(8,128)S(1)} collective-permute-done((f32[72,128]{1,0:T(8,128)S(1)}, f32[72,128]{1,0:T(8,128)S(1)}, u32[]{:S(2)}, u32[]{:S(2)}) %collective-permute-start.7) | collective-permute-done | bytes 36896 | tf_op jit(solution)/shard_map/ppermute | solution.py:423
  28.3 3.2 %collective-permute-start.8 = (f32[72,128]{1,0:T(8,128)S(1)}, f32[72,128]{1,0:T(8,128)S(1)}, u32[]{:S(2)}, u32[]{:S(2)}) collective-permute-start(f32[72,128]{1,0:T(8,128)S(1)} %add.11.a_ref), channel_id=1, source_target_pairs={{0,4},{1,5},{2,6},{3,7},{4,0},{5,1},{6,2},{7,3},{8,12},{9,13},{10,... | collective-permute-start | bytes 110600 | tf_op jit(solution)/shard_map/ppermute | solution.py:423
  31.5 0.0 collective-permute-done.4.a_ref
  31.5 0.0 collective-permute-done.6.b_ref
  31.5 1.3 %shard_map.115 = bf16[16,8,16,128]{3,2,1,0:T(8,128)(2,1)} custom-call(bf16[256,128]{1,0:T(8,128)(2,1)S(1)} %collective-permute-done.4.a_ref, bf16[256,128]{1,0:T(8,128)(2,1)S(1)} %collective-permute-done.6.b_ref, bf16[8,768,128]{2,1,0:T(8,128)(2,1)S(1)} %get-tuple-element.57.shifted_ref, bf16[256,2304]{1,0:T(8,128)(2,1)S(1)} %get-tuple-element.64.turned_ref, ...), custom_call_target="tpu_custom_call" | custom-call | flops 301989888 | bytes 3276800 | tf_op jit(solution)/shard_map/pallas_call | solution.py:320
  32.8 0.6 %collective-permute-done.8.b_ref = f32[72,128]{1,0:T(8,128)S(1)} collective-permute-done((f32[72,128]{1,0:T(8,128)S(1)}, f32[72,128]{1,0:T(8,128)S(1)}, u32[]{:S(2)}, u32[]{:S(2)}) %collective-permute-start.8) | collective-permute-done | bytes 36896 | tf_op jit(solution)/shard_map/ppermute | solution.py:423
  33.4 0.8 %shard_map.116 = (f32[16,16,27]{2,1,0:T(8,128)}, f32[1,16]{1,0:T(1,128)}, f32[8,16]{1,0:T(8,128)}, f32[1,8]{1,0:T(1,128)}) custom-call(f32[72,128]{1,0:T(8,128)S(1)} %add.11.a_ref, f32[72,128]{1,0:T(8,128)S(1)} %collective-permute-done.8.b_ref), custom_call_target="tpu_custom_call" | custom-call | flops 1000 | bytes 73728 | tf_op jit(solution)/shard_map/pallas_call | solution.py:320
  (3 shorter events, 0.0 us)
Async XLA Ops:
  1.8 7.2 %collective-permute-start = (bf16[16,16,128]{2,1,0:T(8,128)(2,1)S(1)}, bf16[16,16,128]{2,1,0:T(8,128)(2,1)S(1)}, u32[]{:S(2)}, u32[]{:S(2)}) collective-permute-start(bf16[16,16,128]{2,1,0:T(8,128)(2,1)S(1)} %get-tuple-element.39), channel_id=1, source_target_pairs={{0,1},{1,0},{2,3},{3,2},{4,5},{5,4},{6,7},{7,6},{8,9},{9,8},{10,11... | collective-permute-start | bytes 196616 | tf_op jit(solution)/shard_map/ppermute | solution.py:347
  4.8 4.3 %collective-permute-start.1 = (bf16[16,16,128]{2,1,0:T(8,128)(2,1)S(1)}, bf16[16,16,128]{2,1,0:T(8,128)(2,1)S(1)}, u32[]{:S(2)}, u32[]{:S(2)}) collective-permute-start(bf16[16,16,128]{2,1,0:T(8,128)(2,1)S(1)} %get-tuple-element.40), channel_id=1, source_target_pairs={{0,8},{1,2},{2,1},{3,4},{4,3},{5,6},{6,5},{7,15},{8,0},{9,10},{10,... | collective-permute-start | bytes 196616 | tf_op jit(solution)/shard_map/ppermute | solution.py:347
  9.8 1.3 %collective-permute-start.2 = (f32[8,16,128]{2,1,0:T(8,128)S(1)}, f32[8,16,128]{2,1,0:T(8,128)S(1)}, u32[]{:S(2)}, u32[]{:S(2)}) collective-permute-start(f32[8,16,128]{2,1,0:T(8,128)S(1)} %get-tuple-element.51), channel_id=1, source_target_pairs={{0,16},{16,0},{1,17},{17,1},{2,18},{18,2},{3,19},{19,3},{4,20},{20... | collective-permute-start | bytes 196616 | tf_op jit(solution)/shard_map/ppermute | solution.py:401
  14.8 4.0 %collective-permute-start.3 = (f32[72,128]{1,0:T(8,128)S(1)}, f32[72,128]{1,0:T(8,128)S(1)}, u32[]{:S(2)}, u32[]{:S(2)}) collective-permute-start(f32[72,128]{1,0:T(8,128)S(1)} %get-tuple-element.56), channel_id=1, source_target_pairs={{0,8},{8,0},{1,9},{9,1},{2,10},{10,2},{3,11},{11,3},{4,12},{12,4},... | collective-permute-start | bytes 110600 | tf_op jit(solution)/shard_map/ppermute | solution.py:423
  18.8 4.3 %collective-permute-start.5 = (f32[72,128]{1,0:T(8,128)S(1)}, f32[72,128]{1,0:T(8,128)S(1)}, u32[]{:S(2)}, u32[]{:S(2)}) collective-permute-start(f32[72,128]{1,0:T(8,128)S(1)} %add.9), channel_id=1, source_target_pairs={{0,1},{1,0},{2,3},{3,2},{4,5},{5,4},{6,7},{7,6},{8,9},{9,8},{10,11... | collective-permute-start | bytes 110600 | tf_op jit(solution)/shard_map/ppermute | solution.py:423
  20.2 11.2 %collective-permute-start.4 = (bf16[256,128]{1,0:T(8,128)(2,1)S(1)}, bf16[256,128]{1,0:T(8,128)(2,1)S(1)}, u32[]{:S(2)}, u32[]{:S(2)}) collective-permute-start(bf16[256,128]{1,0:T(8,128)(2,1)S(1)} %get-tuple-element.60), channel_id=1, source_target_pairs={{0,1},{1,0},{2,3},{3,2},{4,5},{5,4},{6,7},{7,6},{8,9},{9,8},{10,11... | collective-permute-start | bytes 196616 | tf_op jit(solution)/shard_map/ppermute | solution.py:425
  23.1 8.4 %collective-permute-start.6 = (bf16[256,128]{1,0:T(8,128)(2,1)S(1)}, bf16[256,128]{1,0:T(8,128)(2,1)S(1)}, u32[]{:S(2)}, u32[]{:S(2)}) collective-permute-start(bf16[256,128]{1,0:T(8,128)(2,1)S(1)} %get-tuple-element.63), channel_id=1, source_target_pairs={{0,8},{1,2},{2,1},{3,4},{4,3},{5,6},{6,5},{7,15},{8,0},{9,10},{10,... | collective-permute-start | bytes 196616 | tf_op jit(solution)/shard_map/ppermute | solution.py:425
  24.3 4.0 %collective-permute-start.7 = (f32[72,128]{1,0:T(8,128)S(1)}, f32[72,128]{1,0:T(8,128)S(1)}, u32[]{:S(2)}, u32[]{:S(2)}) collective-permute-start(f32[72,128]{1,0:T(8,128)S(1)} %add.10), channel_id=1, source_target_pairs={{0,2},{1,3},{2,0},{3,1},{4,6},{5,7},{6,4},{7,5},{8,10},{9,11},{10,... | collective-permute-start | bytes 110600 | tf_op jit(solution)/shard_map/ppermute | solution.py:423
  28.3 5.1 %collective-permute-start.8 = (f32[72,128]{1,0:T(8,128)S(1)}, f32[72,128]{1,0:T(8,128)S(1)}, u32[]{:S(2)}, u32[]{:S(2)}) collective-permute-start(f32[72,128]{1,0:T(8,128)S(1)} %add.11.a_ref), channel_id=1, source_target_pairs={{0,4},{1,5},{2,6},{3,7},{4,0},{5,1},{6,2},{7,3},{8,12},{9,13},{10,... | collective-permute-start | bytes 110600 | tf_op jit(solution)/shard_map/ppermute | solution.py:423

commit v4 on v3

--- a/solution.py
+++ b/solution.py
@@ -268,7 +268,8 @@
     packed_ref[4 * ch : 4 * ch + classes] = jnp.where(group == 0, head, jnp.where(group == 1, bias, offset))
 
 
-def inner_grad_kernel(shifted_ref, band_ref, turned_ref, out_ref):
+def inner_grad_kernel(shifted_ref, band_ref, end_ref, turned_ref, out_ref, end_out_ref):
+    end_out_ref[...] = end_ref[...]
     ch, inner, hh, ww = out_ref.shape
     rows = ch * hh
     unit = (iota((rows, rows), 0) == iota((rows, rows), 1)).astype(F32).astype(BF)
@@ -408,27 +409,25 @@
         2 * 9 * rows * rows * planes * ww,
         (x, halo, weight, hidden_in, hidden_edge, diff_in, diff_edge, head),
     )
-    turned, grad_inner = call(
+    turned, grad_inner, grad_a = call(
         inner_grad_kernel,
-        (sds((rows, 9 * rows), BF), sds((ch, planes - 2, hh, ww), BF)),
-        (VM, VM),
+        (sds((rows, 9 * rows), BF), sds((ch, planes - 2, hh, ww), BF), edge),
+        (VM, VM, VM),
         [],
         pair_flops * (planes // 2 - 1),
-        (grads, band),
+        (grads, band, grad_a),
     )
     rounds = [("dp", 1 << b) for b in range((lax.axis_size("dp") - 1).bit_length())]
     rounds += [("depth", 1 << b) for b in range((size - 1).bit_length())]
     ends, pairs, grad_far = [grad_a, grad_b], exchange_pairs(), []
     for n, (axis, bit) in enumerate(rounds):
         other = lax.ppermute(packed, axis, [(i, i ^ bit) for i in range(lax.axis_size(axis))])
-        if 1 <= n <= 2:
-            grad_far.append(lax.ppermute(ends[n - 1], ("dp", "depth"), pairs[n - 1]))
+        if n <= 1:
+            grad_far.append(lax.ppermute(ends[n], ("dp", "depth"), pairs[n]))
         if n < len(rounds) - 1:
             packed = packed + other
         if n == 0:
-            packed, grad_inner, ends[0] = lax.optimization_barrier((packed, grad_inner, ends[0]))
-        if n == 1:
-            packed, ends[1] = lax.optimization_barrier((packed, ends[1]))
+            packed, grad_inner, ends[1] = lax.optimization_barrier((packed, grad_inner, ends[1]))
     grad_input = call(
         edge_grad_kernel,
         sds((ch, planes, hh, ww), BF),

time: 34.3 us -> 33.2 us (0.968)
  waiting for transfers between devices: 7.36 us -> 5.17 us
  starting transfers between devices: 13.9 us -> 15 us
    ppermute x4, waiting for transfers between devices: 5.99 us -> 3.8 us  [body(): lax.ppermute(packed, axis, [(i, i ^ bit) for i in range(lax.axis_size(axi...]
    ppermute x4, starting transfers between devices: 7.57 us -> 8.29 us  [body(): lax.ppermute(packed, axis, [(i, i ^ bit) for i in range(lax.axis_size(axi...]
  transfers between devices with their start and end apart: 9 -> 9, of which waited for: 6 -> 6; matrix products, arithmetic and copies ran while one was open for 0% -> 0% of each run, Pallas kernels for 17% -> 18%
where the time goes in v4:
time: 33.2 us; the launch traced here: 33 us
  starting transfers between devices  15 us (45%)
  Pallas kernels  12.2 us (37%)
  waiting for transfers between devices  5.17 us (16%)
  between operations  0.69 us (2%)
    pallas_call x7, Pallas kernels, call(): pl.pallas_call(kernel, out_shape=out_shape, in_specs=[pl.BlockSpec(memory...  12.2 us
    ppermute x4, starting transfers between devices, body(): lax.ppermute(packed, axis, [(i, i ^ bit) for i in range(lax.axis_size(axi...  8.29 us
    ppermute x4, waiting for transfers between devices, body(): lax.ppermute(packed, axis, [(i, i ^ bit) for i in range(lax.axis_size(axi...  3.8 us
    ppermute x1, starting transfers between devices, exchanged(): lax.ppermute(a, ('dp', 'depth'), one)  3.03 us
    ppermute x2, starting transfers between devices, body(): grad_far.append(lax.ppermute(ends[n], ('dp', 'depth'), pairs[n]))  2.08 us
    ppermute x1, starting transfers between devices, exchanged(): lax.ppermute(b, ('dp', 'depth'), two)  1.49 us
    ppermute x1, waiting for transfers between devices, body(): weight = lax.ppermute(offered, 'net', [(0, 1), (1, 0)])  1.24 us
  transfers between devices with their start and end apart: 9, of which 6 were waited for; matrix products, arithmetic and copies ran while one was open for 0% of the time, Pallas kernels for 18%

profile of v4, /device:TPU:0, one launch (start us, length us, event | category | flops | bytes accessed | tf_op | source)
XLA Modules:
  0.0 33.0 jit_solution(9513847170226249334)
XLA Ops:
  0.6 1.1 %shard_map.110 = (bf16[16,8,16,128]{3,2,1,0:T(8,128)(2,1)S(1)}, s32[8,16,128]{2,1,0:T(8,128)S(1)}, s32[8,16,128]{2,1,0:T(8,128)S(1)}, bf16[16,16,27]{2,1,0:T(8,1...) custom-call(bf16[16,8,16,128]{3,2,1,0:T(8,128)(2,1)} %bitcast.12, ...), custom_call_target="tpu_custom_call" | custom-call | bytes 669536 | tf_op jit(solution)/shard_map/pallas_call | solution.py:321
  1.8 3.0 %collective-permute-start = (bf16[16,16,128]{2,1,0:T(8,128)(2,1)S(1)}, bf16[16,16,128]{2,1,0:T(8,128)(2,1)S(1)}, u32[]{:S(2)}, u32[]{:S(2)}) collective-permute-start(bf16[16,16,128]{2,1,0:T(8,128)(2,1)S(1)} %get-tuple-element.38), channel_id=1, source_target_pairs={{0,1},{1,0},{2,3},{3,2},{4,5},{5,4},{6,7},{7,6},{8,9},{9,8},{10,11... | collective-permute-start | bytes 196616 | tf_op jit(solution)/shard_map/ppermute | solution.py:348
  4.8 1.5 %collective-permute-start.1 = (bf16[16,16,128]{2,1,0:T(8,128)(2,1)S(1)}, bf16[16,16,128]{2,1,0:T(8,128)(2,1)S(1)}, u32[]{:S(2)}, u32[]{:S(2)}) collective-permute-start(bf16[16,16,128]{2,1,0:T(8,128)(2,1)S(1)} %get-tuple-element.39), channel_id=1, source_target_pairs={{0,8},{1,2},{2,1},{3,4},{4,3},{5,6},{6,5},{7,15},{8,0},{9,10},{10,... | collective-permute-start | bytes 196616 | tf_op jit(solution)/shard_map/ppermute | solution.py:348
  6.3 2.6 %shard_map.111 = (bf16[256,2304]{1,0:T(8,128)(2,1)S(1)}, bf16[8,768,128]{2,1,0:T(8,128)(2,1)S(1)}, bf16[6,256,128]{2,1,0:T(8,128)(2,1)S(1)}, f32[6,128,128]{2,1,0:T(8,128)S(1)}, f32[6,16,128]{2,1,0:T(8,128)S(1)}) custom-call(bf16[16,8,16,128]{3,2,1,0:T(8,128)(2,1)S(1)} %get-tuple-element.37.x_ref, s32[8,16,128]{2,1,0:T(8,128)S(1)} %get-tuple-element.40.label_ref, ...), custom_call_target="tpu_custom_call" | custom-call | flops 905969664 | bytes 669536 | tf_op jit(solution)/shard_map/pallas_call | solution.py:321
  8.9 0.0 collective-permute-done.a_ref
  9.0 0.1 collective-permute-done.1.b_ref
  9.1 0.7 %shard_map.112 = (bf16[2,256,128]{2,1,0:T(8,128)(2,1)S(1)}, bf16[2,256,128]{2,1,0:T(8,128)(2,1)S(1)}, f32[2,128,128]{2,1,0:T(8,128)S(1)}, f32[8,16,128]{2,1,0:T(8,128)S(1)}) custom-call(bf16[16,16,128]{2,1,0:T(8,128)(2,1)S(1)} %collective-permute-done.a_ref, bf16[16,16,128]{2,1,0:T(8,128)(2,1)S(1)} %collective-permute-done.1.b_ref, ...), custom_call_target="tpu_custom_call" | custom-call | flops 301989888 | bytes 3064160 | tf_op jit(solution)/shard_map/pallas_call | solution.py:321
  9.8 0.1 collective-permute-start.2
  9.9 1.2 %collective-permute-done.2.weight_ref = f32[8,16,128]{2,1,0:T(8,128)S(1)} collective-permute-done((f32[8,16,128]{2,1,0:T(8,128)S(1)}, f32[8,16,128]{2,1,0:T(8,128)S(1)}, u32[]{:S(2)}, u32[]{:S(2)}) %collective-permute-start.2) | collective-permute-done | bytes 65568 | tf_op jit(solution)/shard_map/ppermute | solution.py:402
  11.1 3.7 %shard_map.113 = (f32[72,128]{1,0:T(8,128)S(1)}, bf16[256,128]{1,0:T(8,128)(2,1)S(1)}, bf16[256,128]{1,0:T(8,128)(2,1)S(1)}, bf16[8,768,128]{2,1,0:T(8,128)(2,1)S(1)}) custom-call(bf16[16,8,16,128]{3,2,1,0:T(8,128)(2,1)S(1)} %get-tuple-element.37.x_ref, bf16[2,256,128]{2,1,0:T(8,128)(2,1)S(1)} %get-tuple-element.49.halo_ref, ...), custom_call_target="tpu_custom_call" | custom-call | flops 1207959552 | bytes 1769728 | tf_op jit(solution)/shard_map/pallas_call | solution.py:321
  14.8 1.6 %collective-permute-start.4 = (f32[72,128]{1,0:T(8,128)S(1)}, f32[72,128]{1,0:T(8,128)S(1)}, u32[]{:S(2)}, u32[]{:S(2)}) collective-permute-start(f32[72,128]{1,0:T(8,128)S(1)} %get-tuple-element.58), channel_id=1, source_target_pairs={{0,8},{8,0},{1,9},{9,1},{2,10},{10,2},{3,11},{11,3},{4,12},{12,4},... | collective-permute-start | bytes 110600 | tf_op jit(solution)/shard_map/ppermute | solution.py:424
  16.3 1.9 %shard_map.114 = (bf16[256,2304]{1,0:T(8,128)(2,1)S(1)}, bf16[16,6,16,128]{3,2,1,0:T(8,128)(2,1)S(1)}, bf16[256,128]{1,0:T(8,128)(2,1)S(1)}) custom-call(bf16[8,768,128]{2,1,0:T(8,128)(2,1)S(1)} %get-tuple-element.55.shifted_ref, bf16[256,2304]{1,0:T(8,128)(2,1)S(1)} %get-tuple-element.46.band_ref, bf16[256,128]{1,0:T(8,128)(2,1)S(1)} %get-tuple-element.56.end_ref), custom_call_target="tpu_custom_call" | custom-call | flops 905969664 | bytes 2818048 | tf_op jit(solution)/shard_map/pallas_call | solution.py:321
  18.3 0.5 %collective-permute-done.4 = f32[72,128]{1,0:T(8,128)S(1)} collective-permute-done((f32[72,128]{1,0:T(8,128)S(1)}, f32[72,128]{1,0:T(8,128)S(1)}, u32[]{:S(2)}, u32[]{:S(2)}) %collective-permute-start.4) | collective-permute-done | bytes 36896 | tf_op jit(solution)/shard_map/ppermute | solution.py:424
  18.8 1.4 %collective-permute-start.6 = (f32[72,128]{1,0:T(8,128)S(1)}, f32[72,128]{1,0:T(8,128)S(1)}, u32[]{:S(2)}, u32[]{:S(2)}) collective-permute-start(f32[72,128]{1,0:T(8,128)S(1)} %add.9), channel_id=1, source_target_pairs={{0,1},{1,0},{2,3},{3,2},{4,5},{5,4},{6,7},{7,6},{8,9},{9,8},{10,11... | collective-permute-start | bytes 110600 | tf_op jit(solution)/shard_map/ppermute | solution.py:424
  20.2 0.6 %collective-permute-start.3 = (bf16[256,128]{1,0:T(8,128)(2,1)S(1)}, bf16[256,128]{1,0:T(8,128)(2,1)S(1)}, u32[]{:S(2)}, u32[]{:S(2)}) collective-permute-start(bf16[256,128]{1,0:T(8,128)(2,1)S(1)} %get-tuple-element.57), channel_id=1, source_target_pairs={{0,1},{1,0},{2,3},{3,2},{4,5},{5,4},{6,7},{7,6},{8,9},{9,8},{10,11... | collective-permute-start | bytes 196616 | tf_op jit(solution)/shard_map/ppermute | solution.py:426
  20.8 1.5 %collective-permute-start.5 = (bf16[256,128]{1,0:T(8,128)(2,1)S(1)}, bf16[256,128]{1,0:T(8,128)(2,1)S(1)}, u32[]{:S(2)}, u32[]{:S(2)}) collective-permute-start(bf16[256,128]{1,0:T(8,128)(2,1)S(1)} %get-tuple-element.61), channel_id=1, source_target_pairs={{0,8},{1,2},{2,1},{3,4},{4,3},{5,6},{6,5},{7,15},{8,0},{9,10},{10,... | collective-permute-start | bytes 196616 | tf_op jit(solution)/shard_map/ppermute | solution.py:426
  22.3 0.7 %collective-permute-done.6 = f32[72,128]{1,0:T(8,128)S(1)} collective-permute-done((f32[72,128]{1,0:T(8,128)S(1)}, f32[72,128]{1,0:T(8,128)S(1)}, u32[]{:S(2)}, u32[]{:S(2)}) %collective-permute-start.6) | collective-permute-done | bytes 36896 | tf_op jit(solution)/shard_map/ppermute | solution.py:424
  23.1 2.2 %collective-permute-start.7 = (f32[72,128]{1,0:T(8,128)S(1)}, f32[72,128]{1,0:T(8,128)S(1)}, u32[]{:S(2)}, u32[]{:S(2)}) collective-permute-start(f32[72,128]{1,0:T(8,128)S(1)} %add.10), channel_id=1, source_target_pairs={{0,2},{1,3},{2,0},{3,1},{4,6},{5,7},{6,4},{7,5},{8,10},{9,11},{10,... | collective-permute-start | bytes 110600 | tf_op jit(solution)/shard_map/ppermute | solution.py:424
  25.2 1.9 %collective-permute-done.7 = f32[72,128]{1,0:T(8,128)S(1)} collective-permute-done((f32[72,128]{1,0:T(8,128)S(1)}, f32[72,128]{1,0:T(8,128)S(1)}, u32[]{:S(2)}, u32[]{:S(2)}) %collective-permute-start.7) | collective-permute-done | bytes 36896 | tf_op jit(solution)/shard_map/ppermute | solution.py:424
  27.2 3.1 %collective-permute-start.8 = (f32[72,128]{1,0:T(8,128)S(1)}, f32[72,128]{1,0:T(8,128)S(1)}, u32[]{:S(2)}, u32[]{:S(2)}) collective-permute-start(f32[72,128]{1,0:T(8,128)S(1)} %add.11.a_ref), channel_id=1, source_target_pairs={{0,4},{1,5},{2,6},{3,7},{4,0},{5,1},{6,2},{7,3},{8,12},{9,13},{10,... | collective-permute-start | bytes 110600 | tf_op jit(solution)/shard_map/ppermute | solution.py:424
  30.3 0.0 collective-permute-done.3.a_ref
  30.3 0.0 collective-permute-done.5.b_ref
  30.3 1.3 %shard_map.115 = bf16[16,8,16,128]{3,2,1,0:T(8,128)(2,1)} custom-call(bf16[256,128]{1,0:T(8,128)(2,1)S(1)} %collective-permute-done.3.a_ref, bf16[256,128]{1,0:T(8,128)(2,1)S(1)} %collective-permute-done.5.b_ref, bf16[8,768,128]{2,1,0:T(8,128)(2,1)S(1)} %get-tuple-element.55.shifted_ref, bf16[256,2304]{1,0:T(8,128)(2,1)S(1)} %get-tuple-element.62.turned_ref, ...), custom_call_target="tpu_custom_call" | custom-call | flops 301989888 | bytes 3276800 | tf_op jit(solution)/shard_map/pallas_call | solution.py:321
  31.7 0.6 %collective-permute-done.8.b_ref = f32[72,128]{1,0:T(8,128)S(1)} collective-permute-done((f32[72,128]{1,0:T(8,128)S(1)}, f32[72,128]{1,0:T(8,128)S(1)}, u32[]{:S(2)}, u32[]{:S(2)}) %collective-permute-start.8) | collective-permute-done | bytes 36896 | tf_op jit(solution)/shard_map/ppermute | solution.py:424
  32.2 0.8 %shard_map.116 = (f32[16,16,27]{2,1,0:T(8,128)}, f32[1,16]{1,0:T(1,128)}, f32[8,16]{1,0:T(8,128)}, f32[1,8]{1,0:T(1,128)}) custom-call(f32[72,128]{1,0:T(8,128)S(1)} %add.11.a_ref, f32[72,128]{1,0:T(8,128)S(1)} %collective-permute-done.8.b_ref), custom_call_target="tpu_custom_call" | custom-call | flops 1000 | bytes 73728 | tf_op jit(solution)/shard_map/pallas_call | solution.py:321
  (3 shorter events, 0.0 us)
Async XLA Ops:
  1.8 7.2 %collective-permute-start = (bf16[16,16,128]{2,1,0:T(8,128)(2,1)S(1)}, bf16[16,16,128]{2,1,0:T(8,128)(2,1)S(1)}, u32[]{:S(2)}, u32[]{:S(2)}) collective-permute-start(bf16[16,16,128]{2,1,0:T(8,128)(2,1)S(1)} %get-tuple-element.38), channel_id=1, source_target_pairs={{0,1},{1,0},{2,3},{3,2},{4,5},{5,4},{6,7},{7,6},{8,9},{9,8},{10,11... | collective-permute-start | bytes 196616 | tf_op jit(solution)/shard_map/ppermute | solution.py:348
  4.8 4.3 %collective-permute-start.1 = (bf16[16,16,128]{2,1,0:T(8,128)(2,1)S(1)}, bf16[16,16,128]{2,1,0:T(8,128)(2,1)S(1)}, u32[]{:S(2)}, u32[]{:S(2)}) collective-permute-start(bf16[16,16,128]{2,1,0:T(8,128)(2,1)S(1)} %get-tuple-element.39), channel_id=1, source_target_pairs={{0,8},{1,2},{2,1},{3,4},{4,3},{5,6},{6,5},{7,15},{8,0},{9,10},{10,... | collective-permute-start | bytes 196616 | tf_op jit(solution)/shard_map/ppermute | solution.py:348
  9.8 1.3 %collective-permute-start.2 = (f32[8,16,128]{2,1,0:T(8,128)S(1)}, f32[8,16,128]{2,1,0:T(8,128)S(1)}, u32[]{:S(2)}, u32[]{:S(2)}) collective-permute-start(f32[8,16,128]{2,1,0:T(8,128)S(1)} %get-tuple-element.50), channel_id=1, source_target_pairs={{0,16},{16,0},{1,17},{17,1},{2,18},{18,2},{3,19},{19,3},{4,20},{20... | collective-permute-start | bytes 196616 | tf_op jit(solution)/shard_map/ppermute | solution.py:402
  14.8 4.0 %collective-permute-start.4 = (f32[72,128]{1,0:T(8,128)S(1)}, f32[72,128]{1,0:T(8,128)S(1)}, u32[]{:S(2)}, u32[]{:S(2)}) collective-permute-start(f32[72,128]{1,0:T(8,128)S(1)} %get-tuple-element.58), channel_id=1, source_target_pairs={{0,8},{8,0},{1,9},{9,1},{2,10},{10,2},{3,11},{11,3},{4,12},{12,4},... | collective-permute-start | bytes 110600 | tf_op jit(solution)/shard_map/ppermute | solution.py:424
  18.8 4.3 %collective-permute-start.6 = (f32[72,128]{1,0:T(8,128)S(1)}, f32[72,128]{1,0:T(8,128)S(1)}, u32[]{:S(2)}, u32[]{:S(2)}) collective-permute-start(f32[72,128]{1,0:T(8,128)S(1)} %add.9), channel_id=1, source_target_pairs={{0,1},{1,0},{2,3},{3,2},{4,5},{5,4},{6,7},{7,6},{8,9},{9,8},{10,11... | collective-permute-start | bytes 110600 | tf_op jit(solution)/shard_map/ppermute | solution.py:424
  20.2 10.1 %collective-permute-start.3 = (bf16[256,128]{1,0:T(8,128)(2,1)S(1)}, bf16[256,128]{1,0:T(8,128)(2,1)S(1)}, u32[]{:S(2)}, u32[]{:S(2)}) collective-permute-start(bf16[256,128]{1,0:T(8,128)(2,1)S(1)} %get-tuple-element.57), channel_id=1, source_target_pairs={{0,1},{1,0},{2,3},{3,2},{4,5},{5,4},{6,7},{7,6},{8,9},{9,8},{10,11... | collective-permute-start | bytes 196616 | tf_op jit(solution)/shard_map/ppermute | solution.py:426
  20.8 9.5 %collective-permute-start.5 = (bf16[256,128]{1,0:T(8,128)(2,1)S(1)}, bf16[256,128]{1,0:T(8,128)(2,1)S(1)}, u32[]{:S(2)}, u32[]{:S(2)}) collective-permute-start(bf16[256,128]{1,0:T(8,128)(2,1)S(1)} %get-tuple-element.61), channel_id=1, source_target_pairs={{0,8},{1,2},{2,1},{3,4},{4,3},{5,6},{6,5},{7,15},{8,0},{9,10},{10,... | collective-permute-start | bytes 196616 | tf_op jit(solution)/shard_map/ppermute | solution.py:426
  23.1 4.1 %collective-permute-start.7 = (f32[72,128]{1,0:T(8,128)S(1)}, f32[72,128]{1,0:T(8,128)S(1)}, u32[]{:S(2)}, u32[]{:S(2)}) collective-permute-start(f32[72,128]{1,0:T(8,128)S(1)} %add.10), channel_id=1, source_target_pairs={{0,2},{1,3},{2,0},{3,1},{4,6},{5,7},{6,4},{7,5},{8,10},{9,11},{10,... | collective-permute-start | bytes 110600 | tf_op jit(solution)/shard_map/ppermute | solution.py:424
  27.2 5.1 %collective-permute-start.8 = (f32[72,128]{1,0:T(8,128)S(1)}, f32[72,128]{1,0:T(8,128)S(1)}, u32[]{:S(2)}, u32[]{:S(2)}) collective-permute-start(f32[72,128]{1,0:T(8,128)S(1)} %add.11.a_ref), channel_id=1, source_target_pairs={{0,4},{1,5},{2,6},{3,7},{4,0},{5,1},{6,2},{7,3},{8,12},{9,13},{10,... | collective-permute-start | bytes 110600 | tf_op jit(solution)/shard_map/ppermute | solution.py:424

commit v5 on v4

--- a/solution.py
+++ b/solution.py
@@ -143,33 +143,43 @@
     return before.astype(BF), after.astype(BF)
 
 
+def turner(ch, hh):
+    rows = ch * hh
+    row, col = iota((rows, rows), 0), iota((rows, rows), 1)
+    return ((row // ch == col % hh) & (row % ch == col // hh)).astype(F32).astype(BF)
+
+
 def interior_kernel(
     x_ref, label_ref, mask_ref, kernel_ref, bias_ref, head_ref, head_bias_ref,
-    band_ref, shifted_ref, hidden_ref, diff_ref, offered_ref,
+    band_ref, shifted_ref, turned_ref, hidden_ref, diff_ref, offered_ref,
 ):
     ch, planes, hh, ww = x_ref.shape
     classes = head_ref.shape[0]
     rows = ch * hh
+    inner = planes - 2
     fill_band(kernel_ref, band_ref, ch, hh)
     mat = head_matrix(head_ref, ch, hh, classes)
     bias = bias_rows(bias_ref, ch, 2 * ww)
+    field = [x_ref[:, d].reshape(rows, ww) for d in range(planes)]
     for d in range(planes):
-        shifted_ref[d] = shifts(x_ref[:, d].reshape(rows, ww))
-    for d in range(1, planes - 1, 2):
-        left = shifted_ref[d - 1 : d + 2].reshape(9 * rows, ww)
-        right = shifted_ref[d : d + 3].reshape(9 * rows, ww)
-        preact = dot(band_ref[...], jnp.concatenate([left, right], axis=1))
+        shifted_ref[d] = shifts(field[d])
+    wide = [shifted_ref[d : d + 3].reshape(9 * rows, ww) for d in range(inner)]
+    preact = dot(band_ref[...], jnp.concatenate(wide, axis=1))
+    for d in range(0, inner, 2):
         hidden, diff, offered = head_pair(
-            preact, bias, mat, head_bias_ref, beside(label_ref, d, d + 1),
-            beside(mask_ref, d, d + 1).astype(F32), (ch, hh, ww, classes),
+            preact[:, d * ww : (d + 2) * ww], bias, mat, head_bias_ref, beside(label_ref, d + 1, d + 2),
+            beside(mask_ref, d + 1, d + 2).astype(F32), (ch, hh, ww, classes),
         )
-        put_pair(hidden_ref, d - 1, d, hidden, ww)
-        put_pair(diff_ref, d - 1, d, diff, ww)
-        put_pair(offered_ref, d - 1, d, offered, ww)
+        put_pair(hidden_ref, d, d + 1, hidden, ww)
+        put_pair(diff_ref, d, d + 1, diff, ww)
+        put_pair(offered_ref, d, d + 1, offered, ww)
+    turned = dot(turner(ch, hh), jnp.concatenate(field, axis=1)).astype(BF)
+    for d in range(planes):
+        turned_ref[d] = turned[:, d * ww : (d + 1) * ww]
 
 
 def edge_kernel(
-    a_ref, b_ref, label_ref, mask_ref, bias_ref, head_ref, head_bias_ref, band_ref, shifted_ref, inner_ref,
+    a_ref, b_ref, label_ref, mask_ref, bias_ref, head_ref, head_bias_ref, band_ref, shifted_ref,
     halo_ref, hidden_ref, diff_ref, offered_ref,
 ):
     ch, hh, ww = a_ref.shape
@@ -177,9 +187,7 @@
     rows = ch * hh
     mat = head_matrix(head_ref, ch, hh, classes)
     bias = bias_rows(bias_ref, ch, 2 * ww)
-    offered_ref[1 : planes - 1] = inner_ref[...]
     before, after = sorted_halo(a_ref[...].reshape(rows, ww).astype(F32), b_ref[...].reshape(rows, ww).astype(F32))
-    halo_ref[0], halo_ref[1] = before, after
     left = jnp.concatenate([shifts(before), shifted_ref[0:2].reshape(6 * rows, ww)], axis=0)
     right = jnp.concatenate([shifted_ref[planes - 2 : planes].reshape(6 * rows, ww), shifts(after)], axis=0)
     preact = dot(band_ref[...], jnp.concatenate([left, right], axis=1))
@@ -189,69 +197,111 @@
     )
     put_pair(hidden_ref, 0, 1, hidden, ww)
     put_pair(diff_ref, 0, 1, diff, ww)
-    put_pair(offered_ref, 0, planes - 1, offered, ww)
-
-
-def backward_kernel(
-    x_ref, halo_ref, weight_ref, hidden_in_ref, hidden_edge_ref, diff_in_ref, diff_edge_ref, head_ref,
+    put_pair(offered_ref, 0, 1, offered, ww)
+    turned = dot(turner(ch, hh), jnp.concatenate([before, after], axis=1)).astype(BF)
+    put_pair(halo_ref, 0, 1, turned, ww)
+
+
+def backward_planes(diff_ref, weight_ref, hidden_ref, head_ref, shifted_ref):
+    count, rows, ww = hidden_ref.shape
+    classes, ch = head_ref.shape
+    hh = rows // ch
+    mat_t = head_matrix_t(head_ref, ch, hh, classes)
+    offset_sum, halves = 0.0, []
+    for d in range(count):
+        grad = (diff_ref[d].reshape(classes, hh, ww) * weight_ref[d][None]).reshape(classes * hh, ww)
+        offset_sum = offset_sum + grad
+        halves.append(grad.astype(BF))
+    halves = jnp.concatenate(halves, axis=1)
+    hiddens = jnp.concatenate([hidden_ref[d] for d in range(count)], axis=1)
+    pre = jnp.where(hiddens.astype(F32) > 0.0, dot(mat_t, halves), 0.0)
+    bias_sum = sum(pre[:, d * ww : (d + 1) * ww] for d in range(count))
+    values = [pre[:, d * ww : (d + 1) * ww].astype(BF) for d in range(count)]
+    for d in range(count):
+        before, after = moved(values[d])
+        shifted_ref[d] = jnp.concatenate([after, values[d], before], axis=0)
+    return values, bias_sum, offset_sum, dot_nt(halves, hiddens)
+
+
+STEP = 3
+
+
+def weight_products(shifted_ref, fields, ch, hh, totals):
+    count, rows3, ww = shifted_ref.shape
+    rows = rows3 // 3
+    span = STEP + 2
+    spot = iota((ch, 256), 1) // ch % span
+    grads = [shifted_ref[d] for d in range(count)]
+    for h0 in range(0, hh, STEP):
+        step = min(STEP, hh - h0)
+        left = [g[k * rows + h0 * ch : k * rows + (h0 + step) * ch] for k in range(3) for g in grads]
+        left = [jnp.concatenate(left[k * count : (k + 1) * count], axis=1) for k in range(3)]
+        low, high = max(h0 - 1, 0), min(h0 + span - 1, hh)
+        right = []
+        for i in range(3):
+            if h0 == 0:
+                right.append(jnp.zeros((ch, count * ww), BF))
+            right.append(jnp.concatenate([f[low * ch : high * ch] for f in fields[i]], axis=1))
+            if h0 + span - 1 > hh:
+                right.append(jnp.zeros(((h0 + span - 1 - hh) * ch, count * ww), BF))
+        right.append(jnp.zeros((256 - 3 * span * ch, count * ww), BF))
+        product = dot_nt(jnp.concatenate(left, axis=0), jnp.concatenate(right, axis=0))
+        for k in range(3):
+            for j in range(3):
+                total = jnp.zeros((ch, 256), F32)
+                for h in range(step):
+                    r = (k * step + h) * ch
+                    total = jnp.where(spot == h + j, product[r : r + ch], total)
+                totals[3 * k + j] = totals[3 * k + j] + total
+    return totals
+
+
+def inner_backward_kernel(
+    turned_ref, weight_ref, hidden_ref, diff_ref, head_ref, after_ref,
+    shifted_ref, total_ref, bias_ref, offset_ref, product_ref,
+):
+    del after_ref
+    classes, ch = head_ref.shape
+    inner, rows, ww = hidden_ref.shape
+    _, bias_ref[...], offset_ref[...], product_ref[...] = backward_planes(
+        diff_ref, weight_ref, hidden_ref, head_ref, shifted_ref
+    )
+    fields = [[turned_ref[d + i] for d in range(inner)] for i in range(3)]
+    totals = weight_products(shifted_ref, fields, ch, rows // ch, [0.0] * 9)
+    for n in range(9):
+        total_ref[n] = totals[n]
+
+
+def edge_backward_kernel(
+    turned_ref, halo_ref, weight_ref, hidden_ref, diff_ref, head_ref, total_ref, bias_in_ref, offset_in_ref, product_in_ref,
     packed_ref, a_ref, b_ref, shifted_ref, rows_ref,
 ):
-    ch, planes, hh, ww = x_ref.shape
-    classes = head_ref.shape[0]
-    rows = ch * hh
-    mat_t = head_matrix_t(head_ref, ch, hh, classes)
-    bias_sum = jnp.zeros((rows, ww), F32)
-    offset_sum = jnp.zeros((classes * hh, ww), F32)
-    hiddens, halves, values = [], [], []
-    for d in range(planes):
-        if d == 0 or d == planes - 1:
-            hiddens.append(hidden_edge_ref[min(d, 1)])
-            diff = diff_edge_ref[min(d, 1)]
-        else:
-            hiddens.append(hidden_in_ref[d - 1])
-            diff = diff_in_ref[d - 1]
-        grad = (diff.reshape(classes, hh, ww) * weight_ref[d][None]).reshape(classes * hh, ww)
-        offset_sum = offset_sum + grad
-        halves.append(grad.astype(BF))
-    for d in range(0, planes, 2):
-        pre = dot(mat_t, jnp.concatenate(halves[d : d + 2], axis=1))
-        for p in range(2):
-            value = jnp.where(hiddens[d + p].astype(F32) > 0.0, pre[:, p * ww : (p + 1) * ww], 0.0)
-            bias_sum = bias_sum + value
-            value = value.astype(BF)
-            values.append(value)
-            before, after = moved(value)
-            shifted_ref[d + p] = jnp.concatenate([after, value, before], axis=0)
+    classes, ch = head_ref.shape
+    planes, rows, ww = turned_ref.shape
+    hh = rows // ch
+    values, bias_sum, offset_sum, product = backward_planes(diff_ref, weight_ref, hidden_ref, head_ref, shifted_ref)
+    bias_sum, offset_sum = bias_sum + bias_in_ref[...], offset_sum + offset_in_ref[...]
+    product = product + product_in_ref[...]
     odd = lax.rem(lax.axis_index("depth"), 2) == 1
-    first, last = values[0].astype(F32), values[-1].astype(F32)
+    first, last = values[0].astype(F32), values[1].astype(F32)
     a_ref[...] = jnp.where(odd, first, last).astype(BF)
     b_ref[...] = jnp.where(odd, last, first).astype(BF)
-    grad_cat = jnp.concatenate([shifted_ref[d] for d in range(planes)], axis=1)
-    field = [halo_ref[0]] + [x_ref[:, d].reshape(rows, ww) for d in range(planes)] + [halo_ref[1]]
-    place = iota((ch, rows), 1) % hh
-    for i in range(3):
-        product = dot_nt(grad_cat, jnp.concatenate(field[i : i + planes], axis=1))
-        for k in range(3):
-            for j in range(3):
-                total = jnp.zeros((ch, rows), F32)
-                for h in range(hh):
-                    if 0 <= h + j - 1 < hh:
-                        r = k * rows + h * ch
-                        total = jnp.where(place == h + j - 1, product[r : r + ch], total)
-                t = 9 * i + 3 * j + k
-                for half in range(rows // 128):
-                    rows_ref[half, pl.ds(t, ch, stride=32)] = total[:, 128 * half : 128 * half + 128]
-    for half in range(rows // 128):
-        for t in range(27, 32):
-            rows_ref[half, pl.ds(t, ch, stride=32)] = jnp.zeros((ch, 128), F32)
-    sums = 0.0
-    for half in range(rows // 128):
-        pick = (iota((ch, 128), 1) + 128 * half) // hh == iota((ch, 128), 0)
-        pick = pick.astype(F32).astype(BF)
-        sums = sums + sum(dot_nt(pick, part) for part in split3(rows_ref[half]))
+    fields = [
+        [halo_ref[0], turned_ref[planes - 2]],
+        [turned_ref[0], turned_ref[planes - 1]],
+        [turned_ref[1], halo_ref[1]],
+    ]
+    totals = weight_products(shifted_ref, fields, ch, hh, [total_ref[n] for n in range(9)])
+    part = iota((ch, 256), 1) // (ch * (STEP + 2))
+    for half in range(2):
+        for t in range(32):
+            i, j, k = t // 9, t // 3 % 3, t % 3
+            value = jnp.where(part == i, totals[3 * k + j], 0.0) if t < 27 else jnp.zeros((ch, 256), F32)
+            rows_ref[half, pl.ds(t, ch, stride=32)] = value[:, 128 * half : 128 * half + 128]
+    pick = (iota((ch, 128), 1) % ch == iota((ch, 128), 0)).astype(F32).astype(BF)
+    sums = sum(dot_nt(pick, part) for half in range(2) for part in split3(rows_ref[half]))
     for q in range(ch // 4):
         packed_ref[q * ch : (q + 1) * ch] = sums[:, 128 * q : 128 * q + 128]
-    product = dot_nt(jnp.concatenate(halves, axis=1), jnp.concatenate(hiddens, axis=1))
     product = product.reshape(classes, hh, rows)
     keep = iota((classes, hh, rows), 2) // ch == iota((classes, hh, rows), 1)
     head = jnp.sum(jnp.where(keep, product, 0.0), axis=1)
@@ -268,7 +318,7 @@
     packed_ref[4 * ch : 4 * ch + classes] = jnp.where(group == 0, head, jnp.where(group == 1, bias, offset))
 
 
-def inner_grad_kernel(shifted_ref, band_ref, end_ref, turned_ref, out_ref, end_out_ref):
+def inner_grad_kernel(shifted_ref, edge_ref, band_ref, end_ref, turned_ref, out_ref, end_out_ref):
     end_out_ref[...] = end_ref[...]
     ch, inner, hh, ww = out_ref.shape
     rows = ch * hh
@@ -278,15 +328,14 @@
             block = band_ref[:, (3 * i + k) * rows : (3 * i + k + 1) * rows]
             col = (3 * (2 - i) + k) * rows
             turned_ref[:, col : col + rows] = dot_nt(unit, block).astype(BF)
-    for d in range(0, inner, 2):
-        left = shifted_ref[d : d + 3].reshape(9 * rows, ww)
-        right = shifted_ref[d + 1 : d + 4].reshape(9 * rows, ww)
-        grad = dot(turned_ref[...], jnp.concatenate([left, right], axis=1)).astype(BF)
-        out_ref[:, d] = grad[:, :ww].reshape(ch, hh, ww)
-        out_ref[:, d + 1] = grad[:, ww:].reshape(ch, hh, ww)
-
-
-def edge_grad_kernel(a_ref, b_ref, shifted_ref, turned_ref, inner_ref, out_ref):
+    planes = [edge_ref[0]] + [shifted_ref[d] for d in range(inner)] + [edge_ref[1]]
+    wide = [jnp.concatenate(planes[d : d + 3], axis=0) for d in range(inner)]
+    grad = dot(turned_ref[...], jnp.concatenate(wide, axis=1)).astype(BF)
+    for d in range(inner):
+        out_ref[:, d] = grad[:, d * ww : (d + 1) * ww].reshape(ch, hh, ww)
+
+
+def edge_grad_kernel(a_ref, b_ref, shifted_ref, edge_ref, turned_ref, inner_ref, out_ref):
     ch, planes, hh, ww = out_ref.shape
     rows = ch * hh
 
@@ -295,8 +344,8 @@
         return jnp.concatenate([after, x, before], axis=0)
 
     before, after = sorted_halo(a_ref[...].astype(F32), b_ref[...].astype(F32))
-    left = jnp.concatenate([turned_shifts(before), shifted_ref[0:2].reshape(6 * rows, ww)], axis=0)
-    right = jnp.concatenate([shifted_ref[planes - 2 : planes].reshape(6 * rows, ww), turned_shifts(after)], axis=0)
+    left = jnp.concatenate([turned_shifts(before), edge_ref[0], shifted_ref[0]], axis=0)
+    right = jnp.concatenate([shifted_ref[planes - 3], edge_ref[1], turned_shifts(after)], axis=0)
     grad = dot(turned_ref[...], jnp.concatenate([left, right], axis=1)).astype(BF)
     out_ref[:, 0] = grad[:, :ww].reshape(ch, hh, ww)
     out_ref[:, 1 : planes - 1] = inner_ref[...]
@@ -372,50 +421,68 @@
     )
     x, label, mask, kernel, conv_bias, head, head_bias = inputs
     far = exchanged(end_a, end_b)
-    band, shifted, hidden_in, diff_in, inner = call(
+    inner = planes - 2
+    band, shifted, turned_x, hidden_in, diff_in, offered_in = call(
         interior_kernel,
         (
             sds((rows, 9 * rows), BF),
             sds((planes, 3 * rows, ww), BF),
-            sds((planes - 2, rows, ww), BF),
-            sds((planes - 2, classes * hh, ww), F32),
-            sds((planes - 2, hh, ww), F32),
+            sds((planes, rows, ww), BF),
+            sds((inner, rows, ww), BF),
+            sds((inner, classes * hh, ww), F32),
+            sds((inner, hh, ww), F32),
         ),
         (VM,) * 7,
         [],
-        pair_flops * (planes // 2 - 1),
+        pair_flops * inner // 2,
         (x, label, mask, kernel, conv_bias, head, head_bias),
     )
-    halo, hidden_edge, diff_edge, offered = call(
+    peers = [(0, 1), (1, 0)]
+    weight_in = lax.ppermute(offered_in, "net", peers)
+    halo, hidden_edge, diff_edge, offered_edge = call(
         edge_kernel,
         (
             sds((2, rows, ww), BF),
             sds((2, rows, ww), BF),
             sds((2, classes * hh, ww), F32),
-            sds((planes, hh, ww), F32),
+            sds((2, hh, ww), F32),
         ),
-        (VM,) * 10,
+        (VM,) * 9,
         [],
         pair_flops,
-        (*far, label, mask, conv_bias, head, head_bias, band, shifted, inner),
-    )
-    weight = lax.ppermute(offered, "net", [(0, 1), (1, 0)])
+        (*far, label, mask, conv_bias, head, head_bias, band, shifted),
+    )
+    weight_edge = lax.ppermute(offered_edge, "net", peers)
+    sums = (
+        sds((9, ch, 256), F32),
+        sds((rows, ww), F32),
+        sds((classes * hh, ww), F32),
+        sds((classes * hh, rows), F32),
+    )
+    grads, *sums = call(
+        inner_backward_kernel,
+        (sds((inner, 3 * rows, ww), BF), *sums),
+        (VM,) * 6,
+        [],
+        pair_flops * inner // 2,
+        (turned_x, weight_in, hidden_in, diff_in, head, halo),
+    )
     edge = sds((rows, ww), BF)
-    packed, grad_a, grad_b, grads = call(
-        backward_kernel,
-        (sds((4 * ch + 8, 128), F32), edge, edge, sds((planes, 3 * rows, ww), BF)),
-        (VM,) * 8,
-        [VM((rows // 128, 32 * ch, 128), F32)],
-        2 * 9 * rows * rows * planes * ww,
-        (x, halo, weight, hidden_in, hidden_edge, diff_in, diff_edge, head),
+    packed, grad_a, grad_b, grad_edge = call(
+        edge_backward_kernel,
+        (sds((4 * ch + 8, 128), F32), edge, edge, sds((2, 3 * rows, ww), BF)),
+        (VM,) * 10,
+        [VM((2, 32 * ch, 128), F32)],
+        pair_flops,
+        (turned_x, halo, weight_edge, hidden_edge, diff_edge, head, *sums),
     )
     turned, grad_inner, grad_a = call(
         inner_grad_kernel,
-        (sds((rows, 9 * rows), BF), sds((ch, planes - 2, hh, ww), BF), edge),
-        (VM, VM, VM),
+        (sds((rows, 9 * rows), BF), sds((ch, inner, hh, ww), BF), edge),
+        (VM,) * 4,
         [],
-        pair_flops * (planes // 2 - 1),
-        (grads, band, grad_a),
+        pair_flops * inner // 2,
+        (grads, grad_edge, band, grad_a),
     )
     rounds = [("dp", 1 << b) for b in range((lax.axis_size("dp") - 1).bit_length())]
     rounds += [("depth", 1 << b) for b in range((size - 1).bit_length())]
@@ -431,10 +498,10 @@
     grad_input = call(
         edge_grad_kernel,
         sds((ch, planes, hh, ww), BF),
-        (VM,) * 5,
+        (VM,) * 6,
         [],
         pair_flops,
-        (*grad_far, grads, turned, grad_inner),
+        (*grad_far, grads, grad_edge, turned, grad_inner),
     )
     scale = 1.0 / (lax.axis_size("dp") * size * planes * hh * ww)
     grad_kernel, grad_bias, grad_head, grad_offset = call(

time: 33.2 us -> 31.2 us (0.940)
  Pallas kernels: 12.2 us -> 11 us
  waiting for transfers between devices: 5.17 us -> 4.46 us
    ppermute x1 -> x2, waiting for transfers between devices: 1.24 us -> 0.01 us  [the longest x1 0.01 us: body(): weight_in = lax.ppermute(offered_in, 'net', peers)]
    pallas_call x7 -> x8, Pallas kernels: 12.2 us -> 11 us  [call(): pl.pallas_call(kernel, out_shape=out_shape, in_specs=[pl.BlockSpec(memory...]
    ppermute x1, waiting for transfers between devices: 0.12 us -> 0.57 us  [exchanged(): lax.ppermute(b, ('dp', 'depth'), two)]
  transfers between devices with their start and end apart: 9 -> 10, of which waited for: 6 -> 5; matrix products, arithmetic and copies ran while one was open for 0% -> 0% of each run, Pallas kernels for 18% -> 24%
where the time goes in v5:
time: 31.2 us; the launch traced here: 31 us
  starting transfers between devices  14.9 us (48%)
  Pallas kernels  11 us (35%)
  waiting for transfers between devices  4.46 us (14%)
  between operations  0.72 us (2%)
    pallas_call x8, Pallas kernels, call(): pl.pallas_call(kernel, out_shape=out_shape, in_specs=[pl.BlockSpec(memory...  11 us
    ppermute x4, starting transfers between devices, body(): lax.ppermute(packed, axis, [(i, i ^ bit) for i in range(lax.axis_size(axi...  8.14 us
    ppermute x4, waiting for transfers between devices, body(): lax.ppermute(packed, axis, [(i, i ^ bit) for i in range(lax.axis_size(axi...  3.88 us
    ppermute x1, starting transfers between devices, exchanged(): lax.ppermute(a, ('dp', 'depth'), one)  3.03 us
    ppermute x2, starting transfers between devices, body(): grad_far.append(lax.ppermute(ends[n], ('dp', 'depth'), pairs[n]))  2.06 us
    ppermute x1, starting transfers between devices, exchanged(): lax.ppermute(b, ('dp', 'depth'), two)  1.49 us
  transfers between devices with their start and end apart: 10, of which 5 were waited for; matrix products, arithmetic and copies ran while one was open for 0% of the time, Pallas kernels for 24%

profile of v5, /device:TPU:0, one launch (start us, length us, event | category | flops | bytes accessed | tf_op | source)
XLA Modules:
  0.0 31.0 jit_solution(18141632344291174044)
XLA Ops:
  0.6 1.1 %shard_map.110 = (bf16[16,8,16,128]{3,2,1,0:T(8,128)(2,1)S(1)}, s32[8,16,128]{2,1,0:T(8,128)S(1)}, s32[8,16,128]{2,1,0:T(8,128)S(1)}, bf16[16,16,27]{2,1,0:T(8,1...) custom-call(bf16[16,8,16,128]{3,2,1,0:T(8,128)(2,1)} %bitcast.12, ...), custom_call_target="tpu_custom_call" | custom-call | bytes 669536 | tf_op jit(solution)/shard_map/pallas_call | solution.py:370
  1.8 3.0 %collective-permute-start.1 = (bf16[16,16,128]{2,1,0:T(8,128)(2,1)S(1)}, bf16[16,16,128]{2,1,0:T(8,128)(2,1)S(1)}, u32[]{:S(2)}, u32[]{:S(2)}) collective-permute-start(bf16[16,16,128]{2,1,0:T(8,128)(2,1)S(1)} %get-tuple-element.54), channel_id=1, source_target_pairs={{0,1},{1,0},{2,3},{3,2},{4,5},{5,4},{6,7},{7,6},{8,9},{9,8},{10,11... | collective-permute-start | bytes 196616 | tf_op jit(solution)/shard_map/ppermute | solution.py:397
  4.8 1.5 %collective-permute-start.2 = (bf16[16,16,128]{2,1,0:T(8,128)(2,1)S(1)}, bf16[16,16,128]{2,1,0:T(8,128)(2,1)S(1)}, u32[]{:S(2)}, u32[]{:S(2)}) collective-permute-start(bf16[16,16,128]{2,1,0:T(8,128)(2,1)S(1)} %get-tuple-element.55), channel_id=1, source_target_pairs={{0,8},{1,2},{2,1},{3,4},{4,3},{5,6},{6,5},{7,15},{8,0},{9,10},{10,... | collective-permute-start | bytes 196616 | tf_op jit(solution)/shard_map/ppermute | solution.py:397
  6.3 2.1 %shard_map.111 = (bf16[256,2304]{1,0:T(8,128)(2,1)S(1)}, bf16[8,768,128]{2,1,0:T(8,128)(2,1)S(1)}, bf16[8,256,128]{2,1,0:T(8,128)(2,1)S(1)}, bf16[6,256,128]{2,1...) custom-call(bf16[16,8,16,128]{3,2,1,0:T(8,128)(2,1)S(1)} %get-tuple-element.43.x_ref, ...), custom_call_target="tpu_custom_call" | custom-call | flops 905969664 | bytes 669536 | tf_op jit(solution)/shard_map/pallas_call | solution.py:370
  8.4 0.1 collective-permute-start
  8.5 0.0 collective-permute-done.1.a_ref
  8.5 0.6 %collective-permute-done.2.b_ref = bf16[16,16,128]{2,1,0:T(8,128)(2,1)S(1)} collective-permute-done((bf16[16,16,128]{2,1,0:T(8,128)(2,1)S(1)}, bf16[16,16,128]{2,1,0:T(8,128)(2,1)S(1)}, u32[]{:S(2)}, u32[]{:S(2)}) %collective-permute-start.2) | collective-permute-done | bytes 65568 | tf_op jit(solution)/shard_map/ppermute | solution.py:397
  9.1 0.7 %shard_map.112 = (bf16[2,256,128]{2,1,0:T(8,128)(2,1)S(1)}, bf16[2,256,128]{2,1,0:T(8,128)(2,1)S(1)}, f32[2,128,128]{2,1,0:T(8,128)S(1)}, f32[2,16,128]{2,1,0:T(8,128)S(1)}) custom-call(bf16[16,16,128]{2,1,0:T(8,128)(2,1)S(1)} %collective-permute-done.1.a_ref, bf16[16,16,128]{2,1,0:T(8,128)(2,1)S(1)} %collective-permute-done.2.b_ref, ...), custom_call_target="tpu_custom_call" | custom-call | flops 301989888 | bytes 3015008 | tf_op jit(solution)/shard_map/pallas_call | solution.py:370
  9.8 0.1 collective-permute-start.3
  9.9 0.0 collective-permute-done.weight_ref
  9.9 1.3 %shard_map.113 = (bf16[6,768,128]{2,1,0:T(8,128)(2,1)S(1)}, f32[9,16,256]{2,1,0:T(8,128)S(1)}, f32[256,128]{1,0:T(8,128)S(1)}, f32[128,128]{1,0:T(8,128)S(1)}, f32[128,256]{1,0:T(8,128)S(1)}) custom-call(bf16[8,256,128]{2,1,0:T(8,128)(2,1)S(1)} %get-tuple-element.50.turned_ref, f32[6,16,128]{2,1,0:T(8,128)S(1)} %collective-permute-done.weight_ref, ...), custom_call_target="tpu_custom_call" | custom-call | flops 905969664 | bytes 1491200 | tf_op jit(solution)/shard_map/pallas_call | solution.py:370
  11.2 0.0 collective-permute-done.3.weight_ref
  11.2 1.6 %shard_map.114 = (f32[72,128]{1,0:T(8,128)S(1)}, bf16[256,128]{1,0:T(8,128)(2,1)S(1)}, bf16[256,128]{1,0:T(8,128)(2,1)S(1)}, bf16[2,768,128]{2,1,0:T(8,128)(2,1)S(1)}) custom-call(bf16[8,256,128]{2,1,0:T(8,128)(2,1)S(1)} %get-tuple-element.50.turned_ref, bf16[2,256,128]{2,1,0:T(8,128)(2,1)S(1)} %get-tuple-element.58.after_ref.halo_ref, ...), custom_call_target="tpu_custom_call" | custom-call | flops 301989888 | bytes 1409280 | tf_op jit(solution)/shard_map/pallas_call | solution.py:370
  12.9 1.5 %collective-permute-start.5 = (f32[72,128]{1,0:T(8,128)S(1)}, f32[72,128]{1,0:T(8,128)S(1)}, u32[]{:S(2)}, u32[]{:S(2)}) collective-permute-start(f32[72,128]{1,0:T(8,128)S(1)} %get-tuple-element.70), channel_id=1, source_target_pairs={{0,8},{8,0},{1,9},{9,1},{2,10},{10,2},{3,11},{11,3},{4,12},{12,4},... | collective-permute-start | bytes 110600 | tf_op jit(solution)/shard_map/ppermute | solution.py:491
  14.4 1.9 %shard_map.115 = (bf16[256,2304]{1,0:T(8,128)(2,1)S(1)}, bf16[16,6,16,128]{3,2,1,0:T(8,128)(2,1)S(1)}, bf16[256,128]{1,0:T(8,128)(2,1)S(1)}) custom-call(bf16[6,768,128]{2,1,0:T(8,128)(2,1)S(1)} %get-tuple-element.59.shifted_ref, bf16[2,768,128]{2,1,0:T(8,128)(2,1)S(1)} %get-tuple-element.67.edge_ref, bf16[256,2304]{1,0:T(8,128)(2,1)S(1)} %get-tuple-element.56.band_ref, ...), custom_call_target="tpu_custom_call" | custom-call | flops 905969664 | bytes 2818048 | tf_op jit(solution)/shard_map/pallas_call | solution.py:370
  16.3 0.5 %collective-permute-done.5 = f32[72,128]{1,0:T(8,128)S(1)} collective-permute-done((f32[72,128]{1,0:T(8,128)S(1)}, f32[72,128]{1,0:T(8,128)S(1)}, u32[]{:S(2)}, u32[]{:S(2)}) %collective-permute-start.5) | collective-permute-done | bytes 36896 | tf_op jit(solution)/shard_map/ppermute | solution.py:491
  16.8 1.4 %collective-permute-start.7 = (f32[72,128]{1,0:T(8,128)S(1)}, f32[72,128]{1,0:T(8,128)S(1)}, u32[]{:S(2)}, u32[]{:S(2)}) collective-permute-start(f32[72,128]{1,0:T(8,128)S(1)} %add.9), channel_id=1, source_target_pairs={{0,1},{1,0},{2,3},{3,2},{4,5},{5,4},{6,7},{7,6},{8,9},{9,8},{10,11... | collective-permute-start | bytes 110600 | tf_op jit(solution)/shard_map/ppermute | solution.py:491
  18.3 0.6 %collective-permute-start.4 = (bf16[256,128]{1,0:T(8,128)(2,1)S(1)}, bf16[256,128]{1,0:T(8,128)(2,1)S(1)}, u32[]{:S(2)}, u32[]{:S(2)}) collective-permute-start(bf16[256,128]{1,0:T(8,128)(2,1)S(1)} %get-tuple-element.69), channel_id=1, source_target_pairs={{0,1},{1,0},{2,3},{3,2},{4,5},{5,4},{6,7},{7,6},{8,9},{9,8},{10,11... | collective-permute-start | bytes 196616 | tf_op jit(solution)/shard_map/ppermute | solution.py:493
  18.9 1.5 %collective-permute-start.6 = (bf16[256,128]{1,0:T(8,128)(2,1)S(1)}, bf16[256,128]{1,0:T(8,128)(2,1)S(1)}, u32[]{:S(2)}, u32[]{:S(2)}) collective-permute-start(bf16[256,128]{1,0:T(8,128)(2,1)S(1)} %get-tuple-element.73), channel_id=1, source_target_pairs={{0,8},{1,2},{2,1},{3,4},{4,3},{5,6},{6,5},{7,15},{8,0},{9,10},{10,... | collective-permute-start | bytes 196616 | tf_op jit(solution)/shard_map/ppermute | solution.py:493
  20.4 0.8 %collective-permute-done.7 = f32[72,128]{1,0:T(8,128)S(1)} collective-permute-done((f32[72,128]{1,0:T(8,128)S(1)}, f32[72,128]{1,0:T(8,128)S(1)}, u32[]{:S(2)}, u32[]{:S(2)}) %collective-permute-start.7) | collective-permute-done | bytes 36896 | tf_op jit(solution)/shard_map/ppermute | solution.py:491
  21.2 2.1 %collective-permute-start.8 = (f32[72,128]{1,0:T(8,128)S(1)}, f32[72,128]{1,0:T(8,128)S(1)}, u32[]{:S(2)}, u32[]{:S(2)}) collective-permute-start(f32[72,128]{1,0:T(8,128)S(1)} %add.10), channel_id=1, source_target_pairs={{0,2},{1,3},{2,0},{3,1},{4,6},{5,7},{6,4},{7,5},{8,10},{9,11},{10,... | collective-permute-start | bytes 110600 | tf_op jit(solution)/shard_map/ppermute | solution.py:491
  23.3 1.9 %collective-permute-done.8 = f32[72,128]{1,0:T(8,128)S(1)} collective-permute-done((f32[72,128]{1,0:T(8,128)S(1)}, f32[72,128]{1,0:T(8,128)S(1)}, u32[]{:S(2)}, u32[]{:S(2)}) %collective-permute-start.8) | collective-permute-done | bytes 36896 | tf_op jit(solution)/shard_map/ppermute | solution.py:491
  25.2 3.1 %collective-permute-start.9 = (f32[72,128]{1,0:T(8,128)S(1)}, f32[72,128]{1,0:T(8,128)S(1)}, u32[]{:S(2)}, u32[]{:S(2)}) collective-permute-start(f32[72,128]{1,0:T(8,128)S(1)} %add.11.a_ref), channel_id=1, source_target_pairs={{0,4},{1,5},{2,6},{3,7},{4,0},{5,1},{6,2},{7,3},{8,12},{9,13},{10,... | collective-permute-start | bytes 110600 | tf_op jit(solution)/shard_map/ppermute | solution.py:491
  28.3 0.0 collective-permute-done.4.a_ref
  28.3 0.0 collective-permute-done.6.b_ref
  28.3 1.4 %shard_map.116 = bf16[16,8,16,128]{3,2,1,0:T(8,128)(2,1)} custom-call(bf16[256,128]{1,0:T(8,128)(2,1)S(1)} %collective-permute-done.4.a_ref, bf16[256,128]{1,0:T(8,128)(2,1)S(1)} %collective-permute-done.6.b_ref, bf16[6,768,128]{2,1,0:T(8,128)(2,1)S(1)} %get-tuple-element.59.shifted_ref, bf16[2,768,128]{2,1,0:T(8,128)(2,1)S(1)} %get-tuple-element.67.edge_ref, ...), custom_call_target="tpu_custom_call" | custom-call | flops 301989888 | bytes 3276800 | tf_op jit(solution)/shard_map/pallas_call | solution.py:370
  29.7 0.6 %collective-permute-done.9.b_ref = f32[72,128]{1,0:T(8,128)S(1)} collective-permute-done((f32[72,128]{1,0:T(8,128)S(1)}, f32[72,128]{1,0:T(8,128)S(1)}, u32[]{:S(2)}, u32[]{:S(2)}) %collective-permute-start.9) | collective-permute-done | bytes 36896 | tf_op jit(solution)/shard_map/ppermute | solution.py:491
  30.3 0.8 %shard_map.117 = (f32[16,16,27]{2,1,0:T(8,128)}, f32[1,16]{1,0:T(1,128)}, f32[8,16]{1,0:T(8,128)}, f32[1,8]{1,0:T(1,128)}) custom-call(f32[72,128]{1,0:T(8,128)S(1)} %add.11.a_ref, f32[72,128]{1,0:T(8,128)S(1)} %collective-permute-done.9.b_ref), custom_call_target="tpu_custom_call" | custom-call | flops 1000 | bytes 73728 | tf_op jit(solution)/shard_map/pallas_call | solution.py:370
  (3 shorter events, 0.0 us)
Async XLA Ops:
  1.8 6.7 %collective-permute-start.1 = (bf16[16,16,128]{2,1,0:T(8,128)(2,1)S(1)}, bf16[16,16,128]{2,1,0:T(8,128)(2,1)S(1)}, u32[]{:S(2)}, u32[]{:S(2)}) collective-permute-start(bf16[16,16,128]{2,1,0:T(8,128)(2,1)S(1)} %get-tuple-element.54), channel_id=1, source_target_pairs={{0,1},{1,0},{2,3},{3,2},{4,5},{5,4},{6,7},{7,6},{8,9},{9,8},{10,11... | collective-permute-start | bytes 196616 | tf_op jit(solution)/shard_map/ppermute | solution.py:397
  4.8 4.3 %collective-permute-start.2 = (bf16[16,16,128]{2,1,0:T(8,128)(2,1)S(1)}, bf16[16,16,128]{2,1,0:T(8,128)(2,1)S(1)}, u32[]{:S(2)}, u32[]{:S(2)}) collective-permute-start(bf16[16,16,128]{2,1,0:T(8,128)(2,1)S(1)} %get-tuple-element.55), channel_id=1, source_target_pairs={{0,8},{1,2},{2,1},{3,4},{4,3},{5,6},{6,5},{7,15},{8,0},{9,10},{10,... | collective-permute-start | bytes 196616 | tf_op jit(solution)/shard_map/ppermute | solution.py:397
  8.4 1.5 %collective-permute-start = (f32[6,16,128]{2,1,0:T(8,128)S(1)}, f32[6,16,128]{2,1,0:T(8,128)S(1)}, u32[]{:S(2)}, u32[]{:S(2)}) collective-permute-start(f32[6,16,128]{2,1,0:T(8,128)S(1)} %get-tuple-element.51), channel_id=1, source_target_pairs={{0,16},{16,0},{1,17},{17,1},{2,18},{18,2},{3,19},{19,3},{4,20},{20... | collective-permute-start | bytes 147464 | tf_op jit(solution)/shard_map/ppermute | solution.py:441
  9.8 1.4 %collective-permute-start.3 = (f32[2,16,128]{2,1,0:T(8,128)S(1)}, f32[2,16,128]{2,1,0:T(8,128)S(1)}, u32[]{:S(2)}, u32[]{:S(2)}) collective-permute-start(f32[2,16,128]{2,1,0:T(8,128)S(1)} %get-tuple-element.60), channel_id=1, source_target_pairs={{0,16},{16,0},{1,17},{17,1},{2,18},{18,2},{3,19},{19,3},{4,20},{20... | collective-permute-start | bytes 49160 | tf_op jit(solution)/shard_map/ppermute | solution.py:455
  12.9 4.0 %collective-permute-start.5 = (f32[72,128]{1,0:T(8,128)S(1)}, f32[72,128]{1,0:T(8,128)S(1)}, u32[]{:S(2)}, u32[]{:S(2)}) collective-permute-start(f32[72,128]{1,0:T(8,128)S(1)} %get-tuple-element.70), channel_id=1, source_target_pairs={{0,8},{8,0},{1,9},{9,1},{2,10},{10,2},{3,11},{11,3},{4,12},{12,4},... | collective-permute-start | bytes 110600 | tf_op jit(solution)/shard_map/ppermute | solution.py:491
  16.8 4.3 %collective-permute-start.7 = (f32[72,128]{1,0:T(8,128)S(1)}, f32[72,128]{1,0:T(8,128)S(1)}, u32[]{:S(2)}, u32[]{:S(2)}) collective-permute-start(f32[72,128]{1,0:T(8,128)S(1)} %add.9), channel_id=1, source_target_pairs={{0,1},{1,0},{2,3},{3,2},{4,5},{5,4},{6,7},{7,6},{8,9},{9,8},{10,11... | collective-permute-start | bytes 110600 | tf_op jit(solution)/shard_map/ppermute | solution.py:491
  18.3 10.0 %collective-permute-start.4 = (bf16[256,128]{1,0:T(8,128)(2,1)S(1)}, bf16[256,128]{1,0:T(8,128)(2,1)S(1)}, u32[]{:S(2)}, u32[]{:S(2)}) collective-permute-start(bf16[256,128]{1,0:T(8,128)(2,1)S(1)} %get-tuple-element.69), channel_id=1, source_target_pairs={{0,1},{1,0},{2,3},{3,2},{4,5},{5,4},{6,7},{7,6},{8,9},{9,8},{10,11... | collective-permute-start | bytes 196616 | tf_op jit(solution)/shard_map/ppermute | solution.py:493
  18.9 9.5 %collective-permute-start.6 = (bf16[256,128]{1,0:T(8,128)(2,1)S(1)}, bf16[256,128]{1,0:T(8,128)(2,1)S(1)}, u32[]{:S(2)}, u32[]{:S(2)}) collective-permute-start(bf16[256,128]{1,0:T(8,128)(2,1)S(1)} %get-tuple-element.73), channel_id=1, source_target_pairs={{0,8},{1,2},{2,1},{3,4},{4,3},{5,6},{6,5},{7,15},{8,0},{9,10},{10,... | collective-permute-start | bytes 196616 | tf_op jit(solution)/shard_map/ppermute | solution.py:493
  21.2 4.0 %collective-permute-start.8 = (f32[72,128]{1,0:T(8,128)S(1)}, f32[72,128]{1,0:T(8,128)S(1)}, u32[]{:S(2)}, u32[]{:S(2)}) collective-permute-start(f32[72,128]{1,0:T(8,128)S(1)} %add.10), channel_id=1, source_target_pairs={{0,2},{1,3},{2,0},{3,1},{4,6},{5,7},{6,4},{7,5},{8,10},{9,11},{10,... | collective-permute-start | bytes 110600 | tf_op jit(solution)/shard_map/ppermute | solution.py:491
  25.2 5.0 %collective-permute-start.9 = (f32[72,128]{1,0:T(8,128)S(1)}, f32[72,128]{1,0:T(8,128)S(1)}, u32[]{:S(2)}, u32[]{:S(2)}) collective-permute-start(f32[72,128]{1,0:T(8,128)S(1)} %add.11.a_ref), channel_id=1, source_target_pairs={{0,4},{1,5},{2,6},{3,7},{4,0},{5,1},{6,2},{7,3},{8,12},{9,13},{10,... | collective-permute-start | bytes 110600 | tf_op jit(solution)/shard_map/ppermute | solution.py:491

commit v6 on v5

--- a/solution.py
+++ b/solution.py
@@ -15,6 +15,14 @@
 
 def iota(shape, dim):
     return lax.broadcasted_iota(jnp.int32, shape, dim)
+
+
+def over(x, n):
+    return lax.shift_right_logical(x, n.bit_length() - 1) if n & (n - 1) == 0 else x // n
+
+
+def rest(x, n):
+    return lax.bitwise_and(x, n - 1) if n & (n - 1) == 0 else lax.rem(x, n)
 
 
 def dot(a, b):
@@ -50,10 +58,10 @@
     unit = (iota((32, 27), 0) == iota((32, 27), 1)).astype(F32).astype(BF)
     by_tap = dot_nt(unit, kernel_ref[...].reshape(ch * ch, 27))
     wide = jnp.broadcast_to(by_tap[:27, None, :], (27, ch, ch * ch))
-    wide = jnp.where(iota((27, ch, ch * ch), 2) // ch == iota((27, ch, ch * ch), 1), wide, 0.0)
-    spread = (iota((ch * ch, rows), 1) // hh == iota((ch * ch, rows), 0) % ch).astype(F32).astype(BF)
+    wide = jnp.where(over(iota((27, ch, ch * ch), 2), ch) == iota((27, ch, ch * ch), 1), wide, 0.0)
+    spread = (over(iota((ch * ch, rows), 1), hh) == rest(iota((ch * ch, rows), 0), ch)).astype(F32).astype(BF)
     wide = dot(wide.reshape(27 * ch, ch * ch).astype(BF), spread).astype(BF)
-    masks = [(iota((ch, rows), 1) % hh == h).astype(F32).astype(BF) for h in range(hh)]
+    masks = [(rest(iota((ch, rows), 1), hh) == h).astype(F32).astype(BF) for h in range(hh)]
     for i in range(3):
         for k in range(3):
             taps = [wide[(9 * i + 3 * j + k) * ch : (9 * i + 3 * j + k + 1) * ch] for j in range(3)]
@@ -69,18 +77,11 @@
 
 def head_matrix(head_ref, ch, hh, classes):
     rows = ch * hh
-    spread = (iota((ch, rows), 1) % ch == iota((ch, rows), 0)).astype(F32).astype(BF)
+    spread = (rest(iota((ch, rows), 1), ch) == iota((ch, rows), 0)).astype(F32).astype(BF)
     wide = dot(head_ref[...], spread)
     wide = jnp.broadcast_to(wide[:, None, :], (classes, hh, rows))
-    keep = iota((classes, hh, rows), 2) // ch == iota((classes, hh, rows), 1)
+    keep = over(iota((classes, hh, rows), 2), ch) == iota((classes, hh, rows), 1)
     return jnp.where(keep, wide, 0.0).reshape(classes * hh, rows).astype(BF)
-
-
-def head_matrix_t(head_ref, ch, hh, classes):
-    mat = head_matrix(head_ref, ch, hh, classes)
-    rows = ch * hh
-    unit = (iota((rows, rows), 0) == iota((rows, rows), 1)).astype(F32).astype(BF)
-    return dot_nt(unit, mat).astype(BF)
 
 
 def bias_rows(bias_ref, ch, width):
@@ -146,12 +147,13 @@
 def turner(ch, hh):
     rows = ch * hh
     row, col = iota((rows, rows), 0), iota((rows, rows), 1)
-    return ((row // ch == col % hh) & (row % ch == col // hh)).astype(F32).astype(BF)
+    return ((over(row, ch) == rest(col, hh)) & (rest(row, ch) == over(col, hh))).astype(F32).astype(BF)
 
 
 def interior_kernel(
     x_ref, label_ref, mask_ref, kernel_ref, bias_ref, head_ref, head_bias_ref,
-    band_ref, shifted_ref, turned_ref, hidden_ref, diff_ref, offered_ref,
+    band_ref, mat_ref, mat_t_ref, turner_ref, bias_out_ref,
+    shifted_ref, turned_ref, hidden_ref, diff_ref, offered_ref,
 ):
     ch, planes, hh, ww = x_ref.shape
     classes = head_ref.shape[0]
@@ -173,40 +175,40 @@
         put_pair(hidden_ref, d, d + 1, hidden, ww)
         put_pair(diff_ref, d, d + 1, diff, ww)
         put_pair(offered_ref, d, d + 1, offered, ww)
-    turned = dot(turner(ch, hh), jnp.concatenate(field, axis=1)).astype(BF)
+    turn = turner(ch, hh)
+    turned = dot(turn, jnp.concatenate(field, axis=1)).astype(BF)
     for d in range(planes):
         turned_ref[d] = turned[:, d * ww : (d + 1) * ww]
+    unit = (iota((rows, rows), 0) == iota((rows, rows), 1)).astype(F32).astype(BF)
+    mat_ref[...], mat_t_ref[...], turner_ref[...], bias_out_ref[...] = mat, dot_nt(unit, mat).astype(BF), turn, bias
 
 
 def edge_kernel(
-    a_ref, b_ref, label_ref, mask_ref, bias_ref, head_ref, head_bias_ref, band_ref, shifted_ref,
+    a_ref, b_ref, label_ref, mask_ref, head_bias_ref, band_ref, mat_ref, turner_ref, bias_ref, shifted_ref,
     halo_ref, hidden_ref, diff_ref, offered_ref,
 ):
     ch, hh, ww = a_ref.shape
-    planes, classes = label_ref.shape[0], head_ref.shape[0]
-    rows = ch * hh
-    mat = head_matrix(head_ref, ch, hh, classes)
-    bias = bias_rows(bias_ref, ch, 2 * ww)
+    planes, classes = label_ref.shape[0], mat_ref.shape[0] // hh
+    rows = ch * hh
     before, after = sorted_halo(a_ref[...].reshape(rows, ww).astype(F32), b_ref[...].reshape(rows, ww).astype(F32))
     left = jnp.concatenate([shifts(before), shifted_ref[0:2].reshape(6 * rows, ww)], axis=0)
     right = jnp.concatenate([shifted_ref[planes - 2 : planes].reshape(6 * rows, ww), shifts(after)], axis=0)
     preact = dot(band_ref[...], jnp.concatenate([left, right], axis=1))
     hidden, diff, offered = head_pair(
-        preact, bias, mat, head_bias_ref, beside(label_ref, 0, planes - 1),
+        preact, bias_ref[...], mat_ref[...], head_bias_ref, beside(label_ref, 0, planes - 1),
         beside(mask_ref, 0, planes - 1).astype(F32), (ch, hh, ww, classes),
     )
     put_pair(hidden_ref, 0, 1, hidden, ww)
     put_pair(diff_ref, 0, 1, diff, ww)
     put_pair(offered_ref, 0, 1, offered, ww)
-    turned = dot(turner(ch, hh), jnp.concatenate([before, after], axis=1)).astype(BF)
+    turned = dot(turner_ref[...], jnp.concatenate([before, after], axis=1)).astype(BF)
     put_pair(halo_ref, 0, 1, turned, ww)
 
 
-def backward_planes(diff_ref, weight_ref, hidden_ref, head_ref, shifted_ref):
+def backward_planes(diff_ref, weight_ref, hidden_ref, mat_t_ref, shifted_ref):
     count, rows, ww = hidden_ref.shape
-    classes, ch = head_ref.shape
-    hh = rows // ch
-    mat_t = head_matrix_t(head_ref, ch, hh, classes)
+    hh = weight_ref.shape[1]
+    classes = diff_ref.shape[1] // hh
     offset_sum, halves = 0.0, []
     for d in range(count):
         grad = (diff_ref[d].reshape(classes, hh, ww) * weight_ref[d][None]).reshape(classes * hh, ww)
@@ -214,7 +216,7 @@
         halves.append(grad.astype(BF))
     halves = jnp.concatenate(halves, axis=1)
     hiddens = jnp.concatenate([hidden_ref[d] for d in range(count)], axis=1)
-    pre = jnp.where(hiddens.astype(F32) > 0.0, dot(mat_t, halves), 0.0)
+    pre = jnp.where(hiddens.astype(F32) > 0.0, dot(mat_t_ref[...], halves), 0.0)
     bias_sum = sum(pre[:, d * ww : (d + 1) * ww] for d in range(count))
     values = [pre[:, d * ww : (d + 1) * ww].astype(BF) for d in range(count)]
     for d in range(count):
@@ -230,7 +232,7 @@
     count, rows3, ww = shifted_ref.shape
     rows = rows3 // 3
     span = STEP + 2
-    spot = iota((ch, 256), 1) // ch % span
+    spot = rest(over(iota((ch, 256), 1), ch), span)
     grads = [shifted_ref[d] for d in range(count)]
     for h0 in range(0, hh, STEP):
         step = min(STEP, hh - h0)
@@ -257,29 +259,29 @@
 
 
 def inner_backward_kernel(
-    turned_ref, weight_ref, hidden_ref, diff_ref, head_ref, after_ref,
+    turned_ref, weight_ref, hidden_ref, diff_ref, mat_t_ref, after_ref,
     shifted_ref, total_ref, bias_ref, offset_ref, product_ref,
 ):
     del after_ref
-    classes, ch = head_ref.shape
     inner, rows, ww = hidden_ref.shape
+    hh = weight_ref.shape[1]
     _, bias_ref[...], offset_ref[...], product_ref[...] = backward_planes(
-        diff_ref, weight_ref, hidden_ref, head_ref, shifted_ref
+        diff_ref, weight_ref, hidden_ref, mat_t_ref, shifted_ref
     )
     fields = [[turned_ref[d + i] for d in range(inner)] for i in range(3)]
-    totals = weight_products(shifted_ref, fields, ch, rows // ch, [0.0] * 9)
+    totals = weight_products(shifted_ref, fields, rows // hh, hh, [0.0] * 9)
     for n in range(9):
         total_ref[n] = totals[n]
 
 
 def edge_backward_kernel(
-    turned_ref, halo_ref, weight_ref, hidden_ref, diff_ref, head_ref, total_ref, bias_in_ref, offset_in_ref, product_in_ref,
+    turned_ref, halo_ref, weight_ref, hidden_ref, diff_ref, mat_t_ref, total_ref, bias_in_ref, offset_in_ref, product_in_ref,
     packed_ref, a_ref, b_ref, shifted_ref, rows_ref,
 ):
-    classes, ch = head_ref.shape
     planes, rows, ww = turned_ref.shape
-    hh = rows // ch
-    values, bias_sum, offset_sum, product = backward_planes(diff_ref, weight_ref, hidden_ref, head_ref, shifted_ref)
+    hh = weight_ref.shape[1]
+    ch, classes = rows // hh, diff_ref.shape[1] // hh
+    values, bias_sum, offset_sum, product = backward_planes(diff_ref, weight_ref, hidden_ref, mat_t_ref, shifted_ref)
     bias_sum, offset_sum = bias_sum + bias_in_ref[...], offset_sum + offset_in_ref[...]
     product = product + product_in_ref[...]
     odd = lax.rem(lax.axis_index("depth"), 2) == 1
@@ -292,34 +294,33 @@
         [turned_ref[1], halo_ref[1]],
     ]
     totals = weight_products(shifted_ref, fields, ch, hh, [total_ref[n] for n in range(9)])
-    part = iota((ch, 256), 1) // (ch * (STEP + 2))
+    part = over(iota((ch, 256), 1), ch * (STEP + 2))
     for half in range(2):
         for t in range(32):
             i, j, k = t // 9, t // 3 % 3, t % 3
             value = jnp.where(part == i, totals[3 * k + j], 0.0) if t < 27 else jnp.zeros((ch, 256), F32)
             rows_ref[half, pl.ds(t, ch, stride=32)] = value[:, 128 * half : 128 * half + 128]
-    pick = (iota((ch, 128), 1) % ch == iota((ch, 128), 0)).astype(F32).astype(BF)
+    pick = (rest(iota((ch, 128), 1), ch) == iota((ch, 128), 0)).astype(F32).astype(BF)
     sums = sum(dot_nt(pick, part) for half in range(2) for part in split3(rows_ref[half]))
     for q in range(ch // 4):
         packed_ref[q * ch : (q + 1) * ch] = sums[:, 128 * q : 128 * q + 128]
     product = product.reshape(classes, hh, rows)
-    keep = iota((classes, hh, rows), 2) // ch == iota((classes, hh, rows), 1)
+    keep = over(iota((classes, hh, rows), 2), ch) == iota((classes, hh, rows), 1)
     head = jnp.sum(jnp.where(keep, product, 0.0), axis=1)
-    by_last = (iota((rows, 128), 0) % ch == iota((rows, 128), 1) % 16).astype(F32).astype(BF)
+    by_last = (rest(iota((rows, 128), 0), ch) == rest(iota((rows, 128), 1), 16)).astype(F32).astype(BF)
     head = dot_exact(head, by_last)
     ones = jnp.ones((16, ww), F32).astype(BF)
     bias = jnp.sum(bias_sum.reshape(hh, ch, ww), axis=0)
     bias = jnp.concatenate([bias] * 8, axis=0)
     bias = sum(dot_nt(ones, part) for part in split3(bias))[:classes]
     offset = sum(dot_nt(ones, part) for part in split3(offset_sum))
-    by_class = (iota((classes * hh, 128), 0) // hh == iota((classes * hh, 128), 1) % 16).astype(F32).astype(BF)
+    by_class = (over(iota((classes * hh, 128), 0), hh) == rest(iota((classes * hh, 128), 1), 16)).astype(F32).astype(BF)
     offset = dot_exact(offset, by_class)[:classes]
-    group = iota((classes, 128), 1) // 16
+    group = over(iota((classes, 128), 1), 16)
     packed_ref[4 * ch : 4 * ch + classes] = jnp.where(group == 0, head, jnp.where(group == 1, bias, offset))
 
 
-def inner_grad_kernel(shifted_ref, edge_ref, band_ref, end_ref, turned_ref, out_ref, end_out_ref):
-    end_out_ref[...] = end_ref[...]
+def inner_grad_kernel(shifted_ref, edge_ref, band_ref, turned_ref, out_ref):
     ch, inner, hh, ww = out_ref.shape
     rows = ch * hh
     unit = (iota((rows, rows), 0) == iota((rows, rows), 1)).astype(F32).astype(BF)
@@ -352,14 +353,16 @@
     out_ref[:, planes - 1] = grad[:, ww:].reshape(ch, hh, ww)
 
 
-def unpack_kernel(scale, a_ref, b_ref, kernel_ref, bias_ref, head_ref, offset_ref):
+def unpack_kernel(scale, own_ref, *refs):
+    others, (kernel_ref, bias_ref, head_ref, offset_ref) = refs[:-4], refs[-4:]
     ch = kernel_ref.shape[0]
+    total = functools.reduce(jnp.add, [r[...] for r in others], own_ref[...]) * scale
     for q in range(ch // 4):
-        value = (a_ref[q * ch : (q + 1) * ch] + b_ref[q * ch : (q + 1) * ch]) * scale
+        value = total[q * ch : (q + 1) * ch]
         for r in range(4):
             turned = pltpu.roll(value, 128 - 32 * r, 1) if r else value
             kernel_ref[4 * q + r] = turned[:, 0:27]
-    value = (a_ref[4 * ch :] + b_ref[4 * ch :]) * scale
+    value = total[4 * ch :]
     head_ref[...] = value[:, 0:16]
     bias_ref[...] = pltpu.roll(value, 112, 1)[0:1, 0:16]
     offset_ref[...] = pltpu.roll(value, 96, 1)[0:1, 0:8]
@@ -397,6 +400,18 @@
     return lax.ppermute(a, ("dp", "depth"), one), lax.ppermute(b, ("dp", "depth"), two)
 
 
+def reduction_rounds():
+    count = lax.axis_size("dp") * lax.axis_size("depth")
+    bits = [1 << b for b in range((count - 1).bit_length())]
+    bits = bits[-1:] + bits[1:2] + bits[:1] + bits[2:-1] if len(bits) >= 4 else bits
+    rounds = []
+    for n in range(0, len(bits), 2):
+        masks = bits[n : n + 2]
+        masks = masks + [sum(masks)] if len(masks) == 2 else masks
+        rounds.append([[(i, i ^ m) for i in range(count)] for m in masks])
+    return rounds
+
+
 def body(features, labels, masks, conv_kernel, conv_bias, head_weight, head_bias):
     x, label, mask = features[0, 0], labels[0], masks[0, 0]
     kernel, head = conv_kernel[0], head_weight[0]
@@ -422,10 +437,14 @@
     x, label, mask, kernel, conv_bias, head, head_bias = inputs
     far = exchanged(end_a, end_b)
     inner = planes - 2
-    band, shifted, turned_x, hidden_in, diff_in, offered_in = call(
+    band, mat, mat_t, turn, bias, shifted, turned_x, hidden_in, diff_in, offered_in = call(
         interior_kernel,
         (
             sds((rows, 9 * rows), BF),
+            sds((classes * hh, rows), BF),
+            sds((rows, classes * hh), BF),
+            sds((rows, rows), BF),
+            sds((ch, 2 * ww), F32),
             sds((planes, 3 * rows, ww), BF),
             sds((planes, rows, ww), BF),
             sds((inner, rows, ww), BF),
@@ -447,10 +466,10 @@
             sds((2, classes * hh, ww), F32),
             sds((2, hh, ww), F32),
         ),
-        (VM,) * 9,
+        (VM,) * 10,
         [],
         pair_flops,
-        (*far, label, mask, conv_bias, head, head_bias, band, shifted),
+        (*far, label, mask, head_bias, band, mat, turn, bias, shifted),
     )
     weight_edge = lax.ppermute(offered_edge, "net", peers)
     sums = (
@@ -465,7 +484,7 @@
         (VM,) * 6,
         [],
         pair_flops * inner // 2,
-        (turned_x, weight_in, hidden_in, diff_in, head, halo),
+        (turned_x, weight_in, hidden_in, diff_in, mat_t, halo),
     )
     edge = sds((rows, ww), BF)
     packed, grad_a, grad_b, grad_edge = call(
@@ -474,27 +493,25 @@
         (VM,) * 10,
         [VM((2, 32 * ch, 128), F32)],
         pair_flops,
-        (turned_x, halo, weight_edge, hidden_edge, diff_edge, head, *sums),
-    )
-    turned, grad_inner, grad_a = call(
+        (turned_x, halo, weight_edge, hidden_edge, diff_edge, mat_t, *sums),
+    )
+    rounds, pairs = reduction_rounds(), exchange_pairs()
+    for n, masks in enumerate(rounds):
+        others = [lax.ppermute(packed, ("dp", "depth"), p) for p in masks]
+        if n == 0:
+            grad_far = [lax.ppermute(e, ("dp", "depth"), p) for e, p in zip((grad_a, grad_b), pairs)]
+        if n < len(rounds) - 1:
+            packed = functools.reduce(jnp.add, others, packed)
+        if n == len(rounds) - 2:
+            packed, band = lax.optimization_barrier((packed, band))
+    turned, grad_inner = call(
         inner_grad_kernel,
-        (sds((rows, 9 * rows), BF), sds((ch, inner, hh, ww), BF), edge),
-        (VM,) * 4,
+        (sds((rows, 9 * rows), BF), sds((ch, inner, hh, ww), BF)),
+        (VM,) * 3,
         [],
         pair_flops * inner // 2,
-        (grads, grad_edge, band, grad_a),
-    )
-    rounds = [("dp", 1 << b) for b in range((lax.axis_size("dp") - 1).bit_length())]
-    rounds += [("depth", 1 << b) for b in range((size - 1).bit_length())]
-    ends, pairs, grad_far = [grad_a, grad_b], exchange_pairs(), []
-    for n, (axis, bit) in enumerate(rounds):
-        other = lax.ppermute(packed, axis, [(i, i ^ bit) for i in range(lax.axis_size(axis))])
-        if n <= 1:
-            grad_far.append(lax.ppermute(ends[n], ("dp", "depth"), pairs[n]))
-        if n < len(rounds) - 1:
-            packed = packed + other
-        if n == 0:
-            packed, grad_inner, ends[1] = lax.optimization_barrier((packed, grad_inner, ends[1]))
+        (grads, grad_edge, band),
+    )
     grad_input = call(
         edge_grad_kernel,
         sds((ch, planes, hh, ww), BF),
@@ -507,10 +524,10 @@
     grad_kernel, grad_bias, grad_head, grad_offset = call(
         functools.partial(unpack_kernel, scale),
         (sds((ch, ch, 27), F32), sds((1, ch), F32), sds((classes, ch), F32), sds((1, classes), F32)),
-        (VM, VM),
+        (VM,) * (1 + len(others)),
         [],
         1000,
-        (packed, other),
+        (packed, *others),
     )
     return (
         grad_input[None, None],

time: 31.2 us -> 28.9 us (0.926)
  waiting for transfers between devices: 4.46 us -> 1.86 us
  starting transfers between devices: 14.9 us -> 15.6 us
  Pallas kernels: 11 us -> 10.6 us
    ppermute x6 -> x8, waiting for transfers between devices: 3.88 us -> 1.27 us  [the longest x6 1.27 us: body(): others = [lax.ppermute(packed, ('dp', 'depth'), p) for p in masks]]
    ppermute x6 -> x8, starting transfers between devices: 10.2 us -> 10.9 us  [the longest x6 8.49 us: body(): others = [lax.ppermute(packed, ('dp', 'depth'), p) for p in masks]]
    pallas_call x8, Pallas kernels: 11 us -> 10.6 us  [call(): pl.pallas_call(kernel, out_shape=out_shape, in_specs=[pl.BlockSpec(memory...]
  transfers between devices with their start and end apart: 10 -> 12, of which waited for: 5 -> 4; matrix products, arithmetic and copies ran while one was open for 0% -> 0% of each run, Pallas kernels for 24% -> 25%
where the time goes in v6:
time: 28.9 us; the launch traced here: 28.7 us
  starting transfers between devices  15.6 us (54%)
  Pallas kernels  10.6 us (37%)
  waiting for transfers between devices  1.86 us (6%)
  between operations  0.71 us (2%)
    pallas_call x8, Pallas kernels, call(): pl.pallas_call(kernel, out_shape=out_shape, in_specs=[pl.BlockSpec(memory...  10.6 us
    ppermute x6, starting transfers between devices, body(): others = [lax.ppermute(packed, ('dp', 'depth'), p) for p in masks]  8.49 us
    ppermute x1, starting transfers between devices, exchanged(): lax.ppermute(a, ('dp', 'depth'), one)  3.03 us
    ppermute x2, starting transfers between devices, body(): lax.ppermute(e, ('dp', 'depth'), p)  2.41 us
    ppermute x1, starting transfers between devices, exchanged(): lax.ppermute(b, ('dp', 'depth'), two)  1.49 us
    ppermute x6, waiting for transfers between devices, body(): others = [lax.ppermute(packed, ('dp', 'depth'), p) for p in masks]  1.27 us
  transfers between devices with their start and end apart: 12, of which 4 were waited for; matrix products, arithmetic and copies ran while one was open for 0% of the time, Pallas kernels for 25%

profile of v6, /device:TPU:0, one launch (start us, length us, event | category | flops | bytes accessed | tf_op | source)
XLA Modules:
  0.0 28.7 jit_solution(10072967857007484345)
XLA Ops:
  0.6 1.1 %shard_map.110 = (bf16[16,8,16,128]{3,2,1,0:T(8,128)(2,1)S(1)}, s32[8,16,128]{2,1,0:T(8,128)S(1)}, s32[8,16,128]{2,1,0:T(8,128)S(1)}, bf16[16,16,27]{2,1,0:T(8,1...) custom-call(bf16[16,8,16,128]{3,2,1,0:T(8,128)(2,1)} %bitcast.12, ...), custom_call_target="tpu_custom_call" | custom-call | bytes 669536 | tf_op jit(solution)/shard_map/pallas_call | solution.py:373
  1.8 3.0 %collective-permute-start = (bf16[16,16,128]{2,1,0:T(8,128)(2,1)S(1)}, bf16[16,16,128]{2,1,0:T(8,128)(2,1)S(1)}, u32[]{:S(2)}, u32[]{:S(2)}) collective-permute-start(bf16[16,16,128]{2,1,0:T(8,128)(2,1)S(1)} %get-tuple-element.53), channel_id=1, source_target_pairs={{0,1},{1,0},{2,3},{3,2},{4,5},{5,4},{6,7},{7,6},{8,9},{9,8},{10,11... | collective-permute-start | bytes 196616 | tf_op jit(solution)/shard_map/ppermute | solution.py:400
  4.8 1.5 %collective-permute-start.1 = (bf16[16,16,128]{2,1,0:T(8,128)(2,1)S(1)}, bf16[16,16,128]{2,1,0:T(8,128)(2,1)S(1)}, u32[]{:S(2)}, u32[]{:S(2)}) collective-permute-start(bf16[16,16,128]{2,1,0:T(8,128)(2,1)S(1)} %get-tuple-element.54), channel_id=1, source_target_pairs={{0,8},{1,2},{2,1},{3,4},{4,3},{5,6},{6,5},{7,15},{8,0},{9,10},{10,... | collective-permute-start | bytes 196616 | tf_op jit(solution)/shard_map/ppermute | solution.py:400
  6.3 2.2 %shard_map.111 = (bf16[256,2304]{1,0:T(8,128)(2,1)S(1)}, bf16[128,256]{1,0:T(8,128)(2,1)S(1)}, bf16[256,128]{1,0:T(8,128)(2,1)S(1)}, bf16[256,256]{1,0:T(8,128)(...) custom-call(bf16[16,8,16,128]{3,2,1,0:T(8,128)(2,1)S(1)} %get-tuple-, ...), custom_call_target="tpu_custom_call" | custom-call | flops 905969664 | bytes 669536 | tf_op jit(solution)/shard_map/pallas_call | solution.py:373
  8.5 0.1 collective-permute-start.3
  8.6 0.0 collective-permute-done.a_ref
  8.6 0.5 %collective-permute-done.1.b_ref = bf16[16,16,128]{2,1,0:T(8,128)(2,1)S(1)} collective-permute-done((bf16[16,16,128]{2,1,0:T(8,128)(2,1)S(1)}, bf16[16,16,128]{2,1,0:T(8,128)(2,1)S(1)}, u32[]{:S(2)}, u32[]{:S(2)}) %collective-permute-start.1) | collective-permute-done | bytes 65568 | tf_op jit(solution)/shard_map/ppermute | solution.py:400
  9.1 0.8 %shard_map.112 = (bf16[2,256,128]{2,1,0:T(8,128)(2,1)S(1)}, bf16[2,256,128]{2,1,0:T(8,128)(2,1)S(1)}, f32[2,128,128]{2,1,0:T(8,128)S(1)}, f32[2,16,128]{2,1,0:T(8,128)S(1)}) custom-call(bf16[16,16,128]{2,1,0:T(8,128)(2,1)S(1)} %collective-permute-done.a_ref, bf16[16,16,128]{2,1,0:T(8,128)(2,1)S(1)} %collective-permute-done.1.b_ref, ...), custom_call_target="tpu_custom_call" | custom-call | flops 301989888 | bytes 3227680 | tf_op jit(solution)/shard_map/pallas_call | solution.py:373
  9.8 0.1 collective-permute-start.2
  9.9 0.0 collective-permute-done.3.weight_ref
  9.9 1.0 %shard_map.113 = (bf16[6,768,128]{2,1,0:T(8,128)(2,1)S(1)}, f32[9,16,256]{2,1,0:T(8,128)S(1)}, f32[256,128]{1,0:T(8,128)S(1)}, f32[128,128]{1,0:T(8,128)S(1)}, f32[128,256]{1,0:T(8,128)S(1)}) custom-call(bf16[8,256,128]{2,1,0:T(8,128)(2,1)S(1)} %get-tuple-element.52.turned_ref, f32[6,16,128]{2,1,0:T(8,128)S(1)} %collective-permute-done.3.weight_ref, ...), custom_call_target="tpu_custom_call" | custom-call | flops 905969664 | bytes 1556480 | tf_op jit(solution)/shard_map/pallas_call | solution.py:373
  11.0 0.1 collective-permute-done.2.weight_ref
  11.1 1.4 %shard_map.114 = (f32[72,128]{1,0:T(8,128)S(1)}, bf16[256,128]{1,0:T(8,128)(2,1)S(1)}, bf16[256,128]{1,0:T(8,128)(2,1)S(1)}, bf16[2,768,128]{2,1,0:T(8,128)(2,1)S(1)}) custom-call(bf16[8,256,128]{2,1,0:T(8,128)(2,1)S(1)} %get-tuple-element.52.turned_ref, bf16[2,256,128]{2,1,0:T(8,128)(2,1)S(1)} %get-tuple-element.60.after_ref.halo_ref, ...), custom_call_target="tpu_custom_call" | custom-call | flops 301989888 | bytes 1474560 | tf_op jit(solution)/shard_map/pallas_call | solution.py:373
  12.5 3.4 %collective-permute-start.8 = (f32[72,128]{1,0:T(8,128)S(1)}, f32[72,128]{1,0:T(8,128)S(1)}, u32[]{:S(2)}, u32[]{:S(2)}) collective-permute-start(f32[72,128]{1,0:T(8,128)S(1)} %get-tuple-element.76), channel_id=1, source_target_pairs={{0,10},{1,11},{2,8},{3,9},{4,14},{5,15},{6,12},{7,13},{8,2},{9,3},... | collective-permute-start | bytes 110600 | tf_op jit(solution)/shard_map/ppermute | solution.py:500
  15.9 0.0 collective-permute-start.7
  15.9 0.6 %collective-permute-start.6 = (f32[72,128]{1,0:T(8,128)S(1)}, f32[72,128]{1,0:T(8,128)S(1)}, u32[]{:S(2)}, u32[]{:S(2)}) collective-permute-start(f32[72,128]{1,0:T(8,128)S(1)} %get-tuple-element.76), channel_id=1, source_target_pairs={{0,8},{1,9},{2,10},{3,11},{4,12},{5,13},{6,14},{7,15},{8,0},{9,1},... | collective-permute-start | bytes 110600 | tf_op jit(solution)/shard_map/ppermute | solution.py:500
  16.5 0.9 %collective-permute-start.4 = (bf16[256,128]{1,0:T(8,128)(2,1)S(1)}, bf16[256,128]{1,0:T(8,128)(2,1)S(1)}, u32[]{:S(2)}, u32[]{:S(2)}) collective-permute-start(bf16[256,128]{1,0:T(8,128)(2,1)S(1)} %get-tuple-element.72), channel_id=1, source_target_pairs={{0,1},{1,0},{2,3},{3,2},{4,5},{5,4},{6,7},{7,6},{8,9},{9,8},{10,11... | collective-permute-start | bytes 196616 | tf_op jit(solution)/shard_map/ppermute | solution.py:502
  17.5 1.5 %collective-permute-start.5 = (bf16[256,128]{1,0:T(8,128)(2,1)S(1)}, bf16[256,128]{1,0:T(8,128)(2,1)S(1)}, u32[]{:S(2)}, u32[]{:S(2)}) collective-permute-start(bf16[256,128]{1,0:T(8,128)(2,1)S(1)} %get-tuple-element.73), channel_id=1, source_target_pairs={{0,8},{1,2},{2,1},{3,4},{4,3},{5,6},{6,5},{7,15},{8,0},{9,10},{10,... | collective-permute-start | bytes 196616 | tf_op jit(solution)/shard_map/ppermute | solution.py:502
  18.9 0.0 collective-permute-done.8
  18.9 1.0 %collective-permute-done.7 = f32[72,128]{1,0:T(8,128)S(1)} collective-permute-done((f32[72,128]{1,0:T(8,128)S(1)}, f32[72,128]{1,0:T(8,128)S(1)}, u32[]{:S(2)}, u32[]{:S(2)}) %collective-permute-start.7) | collective-permute-done | bytes 36896 | tf_op jit(solution)/shard_map/ppermute | solution.py:500
  19.9 0.3 %collective-permute-done.6 = f32[72,128]{1,0:T(8,128)S(1)} collective-permute-done((f32[72,128]{1,0:T(8,128)S(1)}, f32[72,128]{1,0:T(8,128)S(1)}, u32[]{:S(2)}, u32[]{:S(2)}) %collective-permute-start.6) | collective-permute-done | bytes 36896 | tf_op jit(solution)/shard_map/ppermute | solution.py:500
  20.2 2.8 %collective-permute-start.11 = (f32[72,128]{1,0:T(8,128)S(1)}, f32[72,128]{1,0:T(8,128)S(1)}, u32[]{:S(2)}, u32[]{:S(2)}) collective-permute-start(f32[72,128]{1,0:T(8,128)S(1)} %add_add_fusion.own_ref), channel_id=1, source_target_pairs={{0,5},{1,4},{2,7},{3,6},{4,1},{5,0},{6,3},{7,2},{8,13},{9,12},{10,... | collective-permute-start | bytes 110600 | tf_op jit(solution)/shard_map/ppermute | solution.py:500
  23.0 0.3 %collective-permute-start.10 = (f32[72,128]{1,0:T(8,128)S(1)}, f32[72,128]{1,0:T(8,128)S(1)}, u32[]{:S(2)}, u32[]{:S(2)}) collective-permute-start(f32[72,128]{1,0:T(8,128)S(1)} %add_add_fusion.own_ref), channel_id=1, source_target_pairs={{0,4},{1,5},{2,6},{3,7},{4,0},{5,1},{6,2},{7,3},{8,12},{9,13},{10,... | collective-permute-start | bytes 110600 | tf_op jit(solution)/shard_map/ppermute | solution.py:500
  23.3 1.4 %collective-permute-start.9 = (f32[72,128]{1,0:T(8,128)S(1)}, f32[72,128]{1,0:T(8,128)S(1)}, u32[]{:S(2)}, u32[]{:S(2)}) collective-permute-start(f32[72,128]{1,0:T(8,128)S(1)} %add_add_fusion.own_ref), channel_id=1, source_target_pairs={{0,1},{1,0},{2,3},{3,2},{4,5},{5,4},{6,7},{7,6},{8,9},{9,8},{10,11... | collective-permute-start | bytes 110600 | tf_op jit(solution)/shard_map/ppermute | solution.py:500
  24.7 1.9 %shard_map.115 = (bf16[256,2304]{1,0:T(8,128)(2,1)S(1)}, bf16[16,6,16,128]{3,2,1,0:T(8,128)(2,1)S(1)}) custom-call(bf16[6,768,128]{2,1,0:T(8,128)(2,1)S(1)} %get-tuple-element.74.shifted_ref, bf16[2,768,128]{2,1,0:T(8,128)(2,1)S(1)} %get-tuple-element.75.edge_ref, bf16[256,2304]{1,0:T(8,128)(2,1)S(1)} %get-tuple-element.77.band_ref), custom_call_target="tpu_custom_call" | custom-call | flops 905969664 | bytes 2752512 | tf_op jit(solution)/shard_map/pallas_call | solution.py:373
  26.6 0.0 collective-permute-done.4.a_ref
  26.6 0.0 collective-permute-done.5.b_ref
  26.6 1.3 %shard_map.116 = bf16[16,8,16,128]{3,2,1,0:T(8,128)(2,1)} custom-call(bf16[256,128]{1,0:T(8,128)(2,1)S(1)} %collective-permute-done.4.a_ref, bf16[256,128]{1,0:T(8,128)(2,1)S(1)} %collective-permute-done.5.b_ref, bf16[6,768,128]{2,1,0:T(8,128)(2,1)S(1)} %get-tuple-element.74.shifted_ref, bf16[2,768,128]{2,1,0:T(8,128)(2,1)S(1)} %get-tuple-element.75.edge_ref, ...), custom_call_target="tpu_custom_call" | custom-call | flops 301989888 | bytes 3276800 | tf_op jit(solution)/shard_map/pallas_call | solution.py:373
  28.0 0.0 collective-permute-done.11.refs_2_
  28.0 0.0 collective-permute-done.10.refs_1_
  28.0 0.0 collective-permute-done.9.refs_0_
  28.0 0.8 %shard_map.117 = (f32[16,16,27]{2,1,0:T(8,128)}, f32[1,16]{1,0:T(1,128)}, f32[8,16]{1,0:T(8,128)}, f32[1,8]{1,0:T(1,128)}) custom-call(f32[72,128]{1,0:T(8,128)S(1)} %add_add_fusion.own_ref, f32[72,128]{1,0:T(8,128)S(1)} %collective-permute-done.9.refs_0_, f32[72,128]{1,0:T(8,128)S(1)} %collective-permute-done.10.refs_1_, ...), custom_call_target="tpu_custom_call" | custom-call | flops 1000 | bytes 147456 | tf_op jit(solution)/shard_map/pallas_call | solution.py:373
  (1 shorter events, 0.0 us)
Async XLA Ops:
  1.8 6.8 %collective-permute-start = (bf16[16,16,128]{2,1,0:T(8,128)(2,1)S(1)}, bf16[16,16,128]{2,1,0:T(8,128)(2,1)S(1)}, u32[]{:S(2)}, u32[]{:S(2)}) collective-permute-start(bf16[16,16,128]{2,1,0:T(8,128)(2,1)S(1)} %get-tuple-element.53), channel_id=1, source_target_pairs={{0,1},{1,0},{2,3},{3,2},{4,5},{5,4},{6,7},{7,6},{8,9},{9,8},{10,11... | collective-permute-start | bytes 196616 | tf_op jit(solution)/shard_map/ppermute | solution.py:400
  4.8 4.3 %collective-permute-start.1 = (bf16[16,16,128]{2,1,0:T(8,128)(2,1)S(1)}, bf16[16,16,128]{2,1,0:T(8,128)(2,1)S(1)}, u32[]{:S(2)}, u32[]{:S(2)}) collective-permute-start(bf16[16,16,128]{2,1,0:T(8,128)(2,1)S(1)} %get-tuple-element.54), channel_id=1, source_target_pairs={{0,8},{1,2},{2,1},{3,4},{4,3},{5,6},{6,5},{7,15},{8,0},{9,10},{10,... | collective-permute-start | bytes 196616 | tf_op jit(solution)/shard_map/ppermute | solution.py:400
  8.5 1.4 %collective-permute-start.3 = (f32[6,16,128]{2,1,0:T(8,128)S(1)}, f32[6,16,128]{2,1,0:T(8,128)S(1)}, u32[]{:S(2)}, u32[]{:S(2)}) collective-permute-start(f32[6,16,128]{2,1,0:T(8,128)S(1)} %get-tuple-element.65), channel_id=1, source_target_pairs={{0,16},{16,0},{1,17},{17,1},{2,18},{18,2},{3,19},{19,3},{4,20},{20... | collective-permute-start | bytes 147464 | tf_op jit(solution)/shard_map/ppermute | solution.py:460
  9.8 1.2 %collective-permute-start.2 = (f32[2,16,128]{2,1,0:T(8,128)S(1)}, f32[2,16,128]{2,1,0:T(8,128)S(1)}, u32[]{:S(2)}, u32[]{:S(2)}) collective-permute-start(f32[2,16,128]{2,1,0:T(8,128)S(1)} %get-tuple-element.61), channel_id=1, source_target_pairs={{0,16},{16,0},{1,17},{17,1},{2,18},{18,2},{3,19},{19,3},{4,20},{20... | collective-permute-start | bytes 49160 | tf_op jit(solution)/shard_map/ppermute | solution.py:474
  12.5 6.5 %collective-permute-start.8 = (f32[72,128]{1,0:T(8,128)S(1)}, f32[72,128]{1,0:T(8,128)S(1)}, u32[]{:S(2)}, u32[]{:S(2)}) collective-permute-start(f32[72,128]{1,0:T(8,128)S(1)} %get-tuple-element.76), channel_id=1, source_target_pairs={{0,10},{1,11},{2,8},{3,9},{4,14},{5,15},{6,12},{7,13},{8,2},{9,3},... | collective-permute-start | bytes 110600 | tf_op jit(solution)/shard_map/ppermute | solution.py:500
  15.9 4.0 %collective-permute-start.7 = (f32[72,128]{1,0:T(8,128)S(1)}, f32[72,128]{1,0:T(8,128)S(1)}, u32[]{:S(2)}, u32[]{:S(2)}) collective-permute-start(f32[72,128]{1,0:T(8,128)S(1)} %get-tuple-element.76), channel_id=1, source_target_pairs={{0,2},{1,3},{2,0},{3,1},{4,6},{5,7},{6,4},{7,5},{8,10},{9,11},{10,... | collective-permute-start | bytes 110600 | tf_op jit(solution)/shard_map/ppermute | solution.py:500
  15.9 4.3 %collective-permute-start.6 = (f32[72,128]{1,0:T(8,128)S(1)}, f32[72,128]{1,0:T(8,128)S(1)}, u32[]{:S(2)}, u32[]{:S(2)}) collective-permute-start(f32[72,128]{1,0:T(8,128)S(1)} %get-tuple-element.76), channel_id=1, source_target_pairs={{0,8},{1,9},{2,10},{3,11},{4,12},{5,13},{6,14},{7,15},{8,0},{9,1},... | collective-permute-start | bytes 110600 | tf_op jit(solution)/shard_map/ppermute | solution.py:500
  16.5 10.1 %collective-permute-start.4 = (bf16[256,128]{1,0:T(8,128)(2,1)S(1)}, bf16[256,128]{1,0:T(8,128)(2,1)S(1)}, u32[]{:S(2)}, u32[]{:S(2)}) collective-permute-start(bf16[256,128]{1,0:T(8,128)(2,1)S(1)} %get-tuple-element.72), channel_id=1, source_target_pairs={{0,1},{1,0},{2,3},{3,2},{4,5},{5,4},{6,7},{7,6},{8,9},{9,8},{10,11... | collective-permute-start | bytes 196616 | tf_op jit(solution)/shard_map/ppermute | solution.py:502
  17.5 9.2 %collective-permute-start.5 = (bf16[256,128]{1,0:T(8,128)(2,1)S(1)}, bf16[256,128]{1,0:T(8,128)(2,1)S(1)}, u32[]{:S(2)}, u32[]{:S(2)}) collective-permute-start(bf16[256,128]{1,0:T(8,128)(2,1)S(1)} %get-tuple-element.73), channel_id=1, source_target_pairs={{0,8},{1,2},{2,1},{3,4},{4,3},{5,6},{6,5},{7,15},{8,0},{9,10},{10,... | collective-permute-start | bytes 196616 | tf_op jit(solution)/shard_map/ppermute | solution.py:502
  20.2 7.8 %collective-permute-start.11 = (f32[72,128]{1,0:T(8,128)S(1)}, f32[72,128]{1,0:T(8,128)S(1)}, u32[]{:S(2)}, u32[]{:S(2)}) collective-permute-start(f32[72,128]{1,0:T(8,128)S(1)} %add_add_fusion.own_ref), channel_id=1, source_target_pairs={{0,5},{1,4},{2,7},{3,6},{4,1},{5,0},{6,3},{7,2},{8,13},{9,12},{10,... | collective-permute-start | bytes 110600 | tf_op jit(solution)/shard_map/ppermute | solution.py:500
  23.0 5.0 %collective-permute-start.10 = (f32[72,128]{1,0:T(8,128)S(1)}, f32[72,128]{1,0:T(8,128)S(1)}, u32[]{:S(2)}, u32[]{:S(2)}) collective-permute-start(f32[72,128]{1,0:T(8,128)S(1)} %add_add_fusion.own_ref), channel_id=1, source_target_pairs={{0,4},{1,5},{2,6},{3,7},{4,0},{5,1},{6,2},{7,3},{8,12},{9,13},{10,... | collective-permute-start | bytes 110600 | tf_op jit(solution)/shard_map/ppermute | solution.py:500
  23.3 4.7 %collective-permute-start.9 = (f32[72,128]{1,0:T(8,128)S(1)}, f32[72,128]{1,0:T(8,128)S(1)}, u32[]{:S(2)}, u32[]{:S(2)}) collective-permute-start(f32[72,128]{1,0:T(8,128)S(1)} %add_add_fusion.own_ref), channel_id=1, source_target_pairs={{0,1},{1,0},{2,3},{3,2},{4,5},{5,4},{6,7},{7,6},{8,9},{9,8},{10,11... | collective-permute-start | bytes 110600 | tf_op jit(solution)/shard_map/ppermute | solution.py:500

commit v7 on v6

--- a/solution.py
+++ b/solution.py
@@ -296,13 +296,14 @@
     totals = weight_products(shifted_ref, fields, ch, hh, [total_ref[n] for n in range(9)])
     part = over(iota((ch, 256), 1), ch * (STEP + 2))
     for half in range(2):
-        for t in range(32):
+        rows_ref[half, 27 * ch :] = jnp.zeros((512 - 27 * ch, 128), F32)
+        for t in range(27):
             i, j, k = t // 9, t // 3 % 3, t % 3
-            value = jnp.where(part == i, totals[3 * k + j], 0.0) if t < 27 else jnp.zeros((ch, 256), F32)
-            rows_ref[half, pl.ds(t, ch, stride=32)] = value[:, 128 * half : 128 * half + 128]
+            value = jnp.where(part == i, totals[3 * k + j], 0.0)
+            rows_ref[half, pl.ds(t, ch, stride=27)] = value[:, 128 * half : 128 * half + 128]
     pick = (rest(iota((ch, 128), 1), ch) == iota((ch, 128), 0)).astype(F32).astype(BF)
     sums = sum(dot_nt(pick, part) for half in range(2) for part in split3(rows_ref[half]))
-    for q in range(ch // 4):
+    for q in range(3):
         packed_ref[q * ch : (q + 1) * ch] = sums[:, 128 * q : 128 * q + 128]
     product = product.reshape(classes, hh, rows)
     keep = over(iota((classes, hh, rows), 2), ch) == iota((classes, hh, rows), 1)
@@ -316,12 +317,15 @@
     offset = sum(dot_nt(ones, part) for part in split3(offset_sum))
     by_class = (over(iota((classes * hh, 128), 0), hh) == rest(iota((classes * hh, 128), 1), 16)).astype(F32).astype(BF)
     offset = dot_exact(offset, by_class)[:classes]
-    group = over(iota((classes, 128), 1), 16)
-    packed_ref[4 * ch : 4 * ch + classes] = jnp.where(group == 0, head, jnp.where(group == 1, bias, offset))
-
-
-def inner_grad_kernel(shifted_ref, edge_ref, band_ref, turned_ref, out_ref):
-    ch, inner, hh, ww = out_ref.shape
+    lane, row = iota((8, 128), 1), iota((8, 128), 0)
+    small = jnp.where(lane < 112, head, jnp.where(row == 0, bias, offset))
+    low, high = sums[:8, 384:], pltpu.roll(sums[8:, 384:], 48, 1)
+    packed_ref[3 * ch :] = jnp.where(lane < 48, low, jnp.where(lane < 96, high, small))
+
+
+def input_kernel(a_ref, b_ref, shifted_ref, edge_ref, band_ref, out_ref, token_ref, turned_ref, grad_ref, sems):
+    token_ref[...] = jnp.zeros_like(token_ref)
+    ch, planes, hh, ww = grad_ref.shape
     rows = ch * hh
     unit = (iota((rows, rows), 0) == iota((rows, rows), 1)).astype(F32).astype(BF)
     for i in range(3):
@@ -329,52 +333,55 @@
             block = band_ref[:, (3 * i + k) * rows : (3 * i + k + 1) * rows]
             col = (3 * (2 - i) + k) * rows
             turned_ref[:, col : col + rows] = dot_nt(unit, block).astype(BF)
-    planes = [edge_ref[0]] + [shifted_ref[d] for d in range(inner)] + [edge_ref[1]]
-    wide = [jnp.concatenate(planes[d : d + 3], axis=0) for d in range(inner)]
-    grad = dot(turned_ref[...], jnp.concatenate(wide, axis=1)).astype(BF)
-    for d in range(inner):
-        out_ref[:, d] = grad[:, d * ww : (d + 1) * ww].reshape(ch, hh, ww)
-
-
-def edge_grad_kernel(a_ref, b_ref, shifted_ref, edge_ref, turned_ref, inner_ref, out_ref):
-    ch, planes, hh, ww = out_ref.shape
-    rows = ch * hh
-
-    def turned_shifts(x):
+    ends = []
+    for x in sorted_halo(a_ref[...].astype(F32), b_ref[...].astype(F32)):
         before, after = moved(x)
-        return jnp.concatenate([after, x, before], axis=0)
-
-    before, after = sorted_halo(a_ref[...].astype(F32), b_ref[...].astype(F32))
-    left = jnp.concatenate([turned_shifts(before), edge_ref[0], shifted_ref[0]], axis=0)
-    right = jnp.concatenate([shifted_ref[planes - 3], edge_ref[1], turned_shifts(after)], axis=0)
-    grad = dot(turned_ref[...], jnp.concatenate([left, right], axis=1)).astype(BF)
-    out_ref[:, 0] = grad[:, :ww].reshape(ch, hh, ww)
-    out_ref[:, 1 : planes - 1] = inner_ref[...]
-    out_ref[:, planes - 1] = grad[:, ww:].reshape(ch, hh, ww)
-
-
-def unpack_kernel(scale, own_ref, *refs):
+        ends.append(jnp.concatenate([after, x, before], axis=0))
+    field = [ends[0], edge_ref[0]] + [shifted_ref[d] for d in range(planes - 2)] + [edge_ref[1], ends[1]]
+    part, copies = planes // 2, []
+    for n in range(2):
+        own = range(n * part, (n + 1) * part)
+        wide = [jnp.concatenate(field[d : d + 3], axis=0) for d in own]
+        grad = dot(turned_ref[...], jnp.concatenate(wide, axis=1)).astype(BF)
+        for d in own:
+            grad_ref[:, d] = grad[:, (d - n * part) * ww : (d - n * part + 1) * ww].reshape(ch, hh, ww)
+        span = pl.ds(n * part, part)
+        copies.append(pltpu.make_async_copy(grad_ref.at[:, span], out_ref.at[:, span], sems.at[n]))
+        copies[-1].start()
+    for copy in copies:
+        copy.wait()
+
+
+def unpack_kernel(scale, token_ref, own_ref, *refs):
+    del token_ref
     others, (kernel_ref, bias_ref, head_ref, offset_ref) = refs[:-4], refs[-4:]
     ch = kernel_ref.shape[0]
     total = functools.reduce(jnp.add, [r[...] for r in others], own_ref[...]) * scale
-    for q in range(ch // 4):
-        value = total[q * ch : (q + 1) * ch]
-        for r in range(4):
-            turned = pltpu.roll(value, 128 - 32 * r, 1) if r else value
-            kernel_ref[4 * q + r] = turned[:, 0:27]
-    value = total[4 * ch :]
-    head_ref[...] = value[:, 0:16]
-    bias_ref[...] = pltpu.roll(value, 112, 1)[0:1, 0:16]
-    offset_ref[...] = pltpu.roll(value, 96, 1)[0:1, 0:8]
-
-
-def call(kernel, out_shape, in_spaces, scratch, flops, args):
+    tail = total[3 * ch :]
+    tiles = [total[q * ch : (q + 1) * ch] for q in range(3)]
+    tiles.append(jnp.concatenate([tail, pltpu.roll(tail, 80, 1)], axis=0))
+    lane = iota((ch, 128), 1)
+    for co in range(ch):
+        q, off = 27 * co // 128, 27 * co % 128
+        value = pltpu.roll(tiles[q], 128 - off, 1) if off else tiles[q]
+        if off + 27 > 128:
+            value = jnp.where(lane < 128 - off, value, pltpu.roll(tiles[q + 1], 128 - off, 1))
+        kernel_ref[co] = value[:, 0:27]
+    head_ref[...] = pltpu.roll(tail, 32, 1)[:, 0:16]
+    biases = pltpu.roll(tail, 16, 1)
+    bias_ref[...] = biases[0:1, 0:16]
+    offset_ref[...] = biases[1:2, 0:8]
+
+
+def call(kernel, out_shape, in_spaces, scratch, flops, args, out_spaces=None):
     moved_bytes = sum(a.size * a.dtype.itemsize for a in args)
     return pl.pallas_call(
         kernel,
         out_shape=out_shape,
         in_specs=[pl.BlockSpec(memory_space=s) for s in in_spaces],
-        out_specs=jax.tree.map(lambda _: pl.BlockSpec(memory_space=VM), out_shape),
+        out_specs=jax.tree.map(
+            lambda _, s: pl.BlockSpec(memory_space=s), out_shape, out_spaces or jax.tree.map(lambda _: VM, out_shape)
+        ),
         scratch_shapes=scratch,
         compiler_params=pltpu.CompilerParams(vmem_limit_bytes=32 << 20),
         cost_estimate=pl.CostEstimate(flops=flops, bytes_accessed=moved_bytes, transcendentals=0),
@@ -489,7 +496,7 @@
     edge = sds((rows, ww), BF)
     packed, grad_a, grad_b, grad_edge = call(
         edge_backward_kernel,
-        (sds((4 * ch + 8, 128), F32), edge, edge, sds((2, 3 * rows, ww), BF)),
+        (sds((3 * ch + 8, 128), F32), edge, edge, sds((2, 3 * rows, ww), BF)),
         (VM,) * 10,
         [VM((2, 32 * ch, 128), F32)],
         pair_flops,
@@ -504,30 +511,23 @@
             packed = functools.reduce(jnp.add, others, packed)
         if n == len(rounds) - 2:
             packed, band = lax.optimization_barrier((packed, band))
-    turned, grad_inner = call(
-        inner_grad_kernel,
-        (sds((rows, 9 * rows), BF), sds((ch, inner, hh, ww), BF)),
-        (VM,) * 3,
-        [],
-        pair_flops * inner // 2,
-        (grads, grad_edge, band),
-    )
-    grad_input = call(
-        edge_grad_kernel,
-        sds((ch, planes, hh, ww), BF),
-        (VM,) * 6,
-        [],
-        pair_flops,
-        (*grad_far, grads, grad_edge, turned, grad_inner),
+    grad_input, token = call(
+        input_kernel,
+        (sds((ch, planes, hh, ww), BF), sds((8, 128), F32)),
+        (VM,) * 5,
+        [VM((rows, 9 * rows), BF), VM((ch, planes, hh, ww), BF), pltpu.SemaphoreType.DMA((2,))],
+        pair_flops * planes // 2,
+        (*grad_far, grads, grad_edge, band),
+        (pltpu.HBM, VM),
     )
     scale = 1.0 / (lax.axis_size("dp") * size * planes * hh * ww)
     grad_kernel, grad_bias, grad_head, grad_offset = call(
         functools.partial(unpack_kernel, scale),
         (sds((ch, ch, 27), F32), sds((1, ch), F32), sds((classes, ch), F32), sds((1, classes), F32)),
-        (VM,) * (1 + len(others)),
+        (VM,) * (2 + len(others)),
         [],
         1000,
-        (packed, *others),
+        (token, packed, *others),
     )
     return (
         grad_input[None, None],

time: 28.9 us -> 28.3 us (0.979)
  Pallas kernels: 10.6 us -> 9.57 us
  waiting for transfers between devices: 1.86 us -> 2.32 us
    pallas_call x8 -> x7, Pallas kernels: 10.6 us -> 9.57 us  [call(): pl.pallas_call(kernel, out_shape=out_shape, in_specs=[pl.BlockSpec(memory...]
    ppermute x6, waiting for transfers between devices: 1.27 us -> 1.71 us  [body(): others = [lax.ppermute(packed, ('dp', 'depth'), p) for p in masks]]
  transfers between devices with their start and end apart: 12 -> 12, of which waited for: 4 -> 5; matrix products, arithmetic and copies ran while one was open for 0% -> 0% of each run, Pallas kernels for 25% -> 23%
where the time goes in v7:
time: 28.3 us; the launch traced here: 28.2 us
  starting transfers between devices  15.6 us (55%)
  Pallas kernels  9.57 us (34%)
  waiting for transfers between devices  2.32 us (8%)
  between operations  0.7 us (2%)
    pallas_call x7, Pallas kernels, call(): pl.pallas_call(kernel, out_shape=out_shape, in_specs=[pl.BlockSpec(memory...  9.57 us
    ppermute x6, starting transfers between devices, body(): others = [lax.ppermute(packed, ('dp', 'depth'), p) for p in masks]  8.49 us
    ppermute x1, starting transfers between devices, exchanged(): lax.ppermute(a, ('dp', 'depth'), one)  3.03 us
    ppermute x2, starting transfers between devices, body(): lax.ppermute(e, ('dp', 'depth'), p)  2.4 us
    ppermute x6, waiting for transfers between devices, body(): others = [lax.ppermute(packed, ('dp', 'depth'), p) for p in masks]  1.71 us
    ppermute x1, starting transfers between devices, exchanged(): lax.ppermute(b, ('dp', 'depth'), two)  1.49 us
  transfers between devices with their start and end apart: 12, of which 5 were waited for; matrix products, arithmetic and copies ran while one was open for 0% of the time, Pallas kernels for 23%

profile of v7, /device:TPU:0, one launch (start us, length us, event | category | flops | bytes accessed | tf_op | source)
XLA Modules:
  0.0 28.2 jit_solution(13783666880905229977)
XLA Ops:
  0.6 1.1 %shard_map.110 = (bf16[16,8,16,128]{3,2,1,0:T(8,128)(2,1)S(1)}, s32[8,16,128]{2,1,0:T(8,128)S(1)}, s32[8,16,128]{2,1,0:T(8,128)S(1)}, bf16[16,16,27]{2,1,0:T(8,1...) custom-call(bf16[16,8,16,128]{3,2,1,0:T(8,128)(2,1)} %bitcast.12, ...), custom_call_target="tpu_custom_call" | custom-call | bytes 669536 | tf_op jit(solution)/shard_map/pallas_call | solution.py:378
  1.8 3.0 %collective-permute-start = (bf16[16,16,128]{2,1,0:T(8,128)(2,1)S(1)}, bf16[16,16,128]{2,1,0:T(8,128)(2,1)S(1)}, u32[]{:S(2)}, u32[]{:S(2)}) collective-permute-start(bf16[16,16,128]{2,1,0:T(8,128)(2,1)S(1)} %get-tuple-element.53), channel_id=1, source_target_pairs={{0,1},{1,0},{2,3},{3,2},{4,5},{5,4},{6,7},{7,6},{8,9},{9,8},{10,11... | collective-permute-start | bytes 196616 | tf_op jit(solution)/shard_map/ppermute | solution.py:407
  4.8 1.5 %collective-permute-start.1 = (bf16[16,16,128]{2,1,0:T(8,128)(2,1)S(1)}, bf16[16,16,128]{2,1,0:T(8,128)(2,1)S(1)}, u32[]{:S(2)}, u32[]{:S(2)}) collective-permute-start(bf16[16,16,128]{2,1,0:T(8,128)(2,1)S(1)} %get-tuple-element.54), channel_id=1, source_target_pairs={{0,8},{1,2},{2,1},{3,4},{4,3},{5,6},{6,5},{7,15},{8,0},{9,10},{10,... | collective-permute-start | bytes 196616 | tf_op jit(solution)/shard_map/ppermute | solution.py:407
  6.3 2.2 %shard_map.111 = (bf16[256,2304]{1,0:T(8,128)(2,1)S(1)}, bf16[128,256]{1,0:T(8,128)(2,1)S(1)}, bf16[256,128]{1,0:T(8,128)(2,1)S(1)}, bf16[256,256]{1,0:T(8,128)(...) custom-call(bf16[16,8,16,128]{3,2,1,0:T(8,128)(2,1)S(1)} %get-tuple-, ...), custom_call_target="tpu_custom_call" | custom-call | flops 905969664 | bytes 669536 | tf_op jit(solution)/shard_map/pallas_call | solution.py:378
  8.5 0.1 collective-permute-start.3
  8.6 0.0 collective-permute-done.a_ref
  8.6 0.5 %collective-permute-done.1.b_ref = bf16[16,16,128]{2,1,0:T(8,128)(2,1)S(1)} collective-permute-done((bf16[16,16,128]{2,1,0:T(8,128)(2,1)S(1)}, bf16[16,16,128]{2,1,0:T(8,128)(2,1)S(1)}, u32[]{:S(2)}, u32[]{:S(2)}) %collective-permute-start.1) | collective-permute-done | bytes 65568 | tf_op jit(solution)/shard_map/ppermute | solution.py:407
  9.1 0.8 %shard_map.112 = (bf16[2,256,128]{2,1,0:T(8,128)(2,1)S(1)}, bf16[2,256,128]{2,1,0:T(8,128)(2,1)S(1)}, f32[2,128,128]{2,1,0:T(8,128)S(1)}, f32[2,16,128]{2,1,0:T(8,128)S(1)}) custom-call(bf16[16,16,128]{2,1,0:T(8,128)(2,1)S(1)} %collective-permute-done.a_ref, bf16[16,16,128]{2,1,0:T(8,128)(2,1)S(1)} %collective-permute-done.1.b_ref, ...), custom_call_target="tpu_custom_call" | custom-call | flops 301989888 | bytes 3227680 | tf_op jit(solution)/shard_map/pallas_call | solution.py:378
  9.8 0.1 collective-permute-start.2
  9.9 0.0 collective-permute-done.3.weight_ref
  9.9 1.0 %shard_map.113 = (bf16[6,768,128]{2,1,0:T(8,128)(2,1)S(1)}, f32[9,16,256]{2,1,0:T(8,128)S(1)}, f32[256,128]{1,0:T(8,128)S(1)}, f32[128,128]{1,0:T(8,128)S(1)}, f32[128,256]{1,0:T(8,128)S(1)}) custom-call(bf16[8,256,128]{2,1,0:T(8,128)(2,1)S(1)} %get-tuple-element.52.turned_ref, f32[6,16,128]{2,1,0:T(8,128)S(1)} %collective-permute-done.3.weight_ref, ...), custom_call_target="tpu_custom_call" | custom-call | flops 905969664 | bytes 1556480 | tf_op jit(solution)/shard_map/pallas_call | solution.py:378
  11.0 0.1 collective-permute-done.2.weight_ref
  11.1 1.1 %shard_map.114 = (f32[56,128]{1,0:T(8,128)S(1)}, bf16[256,128]{1,0:T(8,128)(2,1)S(1)}, bf16[256,128]{1,0:T(8,128)(2,1)S(1)}, bf16[2,768,128]{2,1,0:T(8,128)(2,1)S(1)}) custom-call(bf16[8,256,128]{2,1,0:T(8,128)(2,1)S(1)} %get-tuple-element.52.turned_ref, bf16[2,256,128]{2,1,0:T(8,128)(2,1)S(1)} %get-tuple-element.60.after_ref.halo_ref, ...), custom_call_target="tpu_custom_call" | custom-call | flops 301989888 | bytes 1474560 | tf_op jit(solution)/shard_map/pallas_call | solution.py:378
  12.2 3.4 %collective-permute-start.8 = (f32[56,128]{1,0:T(8,128)S(1)}, f32[56,128]{1,0:T(8,128)S(1)}, u32[]{:S(2)}, u32[]{:S(2)}) collective-permute-start(f32[56,128]{1,0:T(8,128)S(1)} %get-tuple-element.76), channel_id=1, source_target_pairs={{0,10},{1,11},{2,8},{3,9},{4,14},{5,15},{6,12},{7,13},{8,2},{9,3},... | collective-permute-start | bytes 86024 | tf_op jit(solution)/shard_map/ppermute | solution.py:507
  15.7 0.0 collective-permute-start.7
  15.7 0.6 %collective-permute-start.6 = (f32[56,128]{1,0:T(8,128)S(1)}, f32[56,128]{1,0:T(8,128)S(1)}, u32[]{:S(2)}, u32[]{:S(2)}) collective-permute-start(f32[56,128]{1,0:T(8,128)S(1)} %get-tuple-element.76), channel_id=1, source_target_pairs={{0,8},{1,9},{2,10},{3,11},{4,12},{5,13},{6,14},{7,15},{8,0},{9,1},... | collective-permute-start | bytes 86024 | tf_op jit(solution)/shard_map/ppermute | solution.py:507
  16.2 0.9 %collective-permute-start.4 = (bf16[256,128]{1,0:T(8,128)(2,1)S(1)}, bf16[256,128]{1,0:T(8,128)(2,1)S(1)}, u32[]{:S(2)}, u32[]{:S(2)}) collective-permute-start(bf16[256,128]{1,0:T(8,128)(2,1)S(1)} %get-tuple-element.72), channel_id=1, source_target_pairs={{0,1},{1,0},{2,3},{3,2},{4,5},{5,4},{6,7},{7,6},{8,9},{9,8},{10,11... | collective-permute-start | bytes 196616 | tf_op jit(solution)/shard_map/ppermute | solution.py:509
  17.2 1.5 %collective-permute-start.5 = (bf16[256,128]{1,0:T(8,128)(2,1)S(1)}, bf16[256,128]{1,0:T(8,128)(2,1)S(1)}, u32[]{:S(2)}, u32[]{:S(2)}) collective-permute-start(bf16[256,128]{1,0:T(8,128)(2,1)S(1)} %get-tuple-element.73), channel_id=1, source_target_pairs={{0,8},{1,2},{2,1},{3,4},{4,3},{5,6},{6,5},{7,15},{8,0},{9,10},{10,... | collective-permute-start | bytes 196616 | tf_op jit(solution)/shard_map/ppermute | solution.py:509
  18.6 0.0 collective-permute-done.8
  18.7 0.9 %collective-permute-done.7 = f32[56,128]{1,0:T(8,128)S(1)} collective-permute-done((f32[56,128]{1,0:T(8,128)S(1)}, f32[56,128]{1,0:T(8,128)S(1)}, u32[]{:S(2)}, u32[]{:S(2)}) %collective-permute-start.7) | collective-permute-done | bytes 28704 | tf_op jit(solution)/shard_map/ppermute | solution.py:507
  19.5 0.2 collective-permute-done.6
  19.8 2.8 %collective-permute-start.11 = (f32[56,128]{1,0:T(8,128)S(1)}, f32[56,128]{1,0:T(8,128)S(1)}, u32[]{:S(2)}, u32[]{:S(2)}) collective-permute-start(f32[56,128]{1,0:T(8,128)S(1)} %add_add_fusion.own_ref), channel_id=1, source_target_pairs={{0,5},{1,4},{2,7},{3,6},{4,1},{5,0},{6,3},{7,2},{8,13},{9,12},{10,... | collective-permute-start | bytes 86024 | tf_op jit(solution)/shard_map/ppermute | solution.py:507
  22.6 0.3 %collective-permute-start.10 = (f32[56,128]{1,0:T(8,128)S(1)}, f32[56,128]{1,0:T(8,128)S(1)}, u32[]{:S(2)}, u32[]{:S(2)}) collective-permute-start(f32[56,128]{1,0:T(8,128)S(1)} %add_add_fusion.own_ref), channel_id=1, source_target_pairs={{0,4},{1,5},{2,6},{3,7},{4,0},{5,1},{6,2},{7,3},{8,12},{9,13},{10,... | collective-permute-start | bytes 86024 | tf_op jit(solution)/shard_map/ppermute | solution.py:507
  22.9 1.3 %collective-permute-start.9 = (f32[56,128]{1,0:T(8,128)S(1)}, f32[56,128]{1,0:T(8,128)S(1)}, u32[]{:S(2)}, u32[]{:S(2)}) collective-permute-start(f32[56,128]{1,0:T(8,128)S(1)} %add_add_fusion.own_ref), channel_id=1, source_target_pairs={{0,1},{1,0},{2,3},{3,2},{4,5},{5,4},{6,7},{7,6},{8,9},{9,8},{10,11... | collective-permute-start | bytes 86024 | tf_op jit(solution)/shard_map/ppermute | solution.py:507
  24.2 0.0 collective-permute-done.4.a_ref
  24.2 0.0 collective-permute-done.5.b_ref
  24.2 2.5 %shard_map.115 = (bf16[16,8,16,128]{3,2,1,0:T(8,128)(2,1)}, f32[8,128]{1,0:T(8,128)S(1)}) custom-call(bf16[256,128]{1,0:T(8,128)(2,1)S(1)} %collective-permute-done.4.a_ref, bf16[256,128]{1,0:T(8,128)(2,1)S(1)} %collective-permute-done.5.b_ref, bf16[6,768,128]{2,1,0:T(8,128)(2,1)S(1)} %get-tuple-element.74.shifted_ref, ...), custom_call_target="tpu_custom_call" | custom-call | flops 1207959552 | bytes 2883584 | tf_op jit(solution)/shard_map/pallas_call | solution.py:378
  26.7 0.0 collective-permute-done.11.refs_2_
  26.7 0.6 %collective-permute-done.10.refs_1_ = f32[56,128]{1,0:T(8,128)S(1)} collective-permute-done((f32[56,128]{1,0:T(8,128)S(1)}, f32[56,128]{1,0:T(8,128)S(1)}, u32[]{:S(2)}, u32[]{:S(2)}) %collective-permute-start.10) | collective-permute-done | bytes 28704 | tf_op jit(solution)/shard_map/ppermute | solution.py:507
  27.4 0.0 collective-permute-done.9.refs_0_
  27.4 0.8 %shard_map.116 = (f32[16,16,27]{2,1,0:T(8,128)}, f32[1,16]{1,0:T(1,128)}, f32[8,16]{1,0:T(8,128)}, f32[1,8]{1,0:T(1,128)}) custom-call(f32[8,128]{1,0:T(8,128)S(1)} %get-tuple-element.79.token_ref, f32[56,128]{1,0:T(8,128)S(1)} %add_add_fusion.own_ref, f32[56,128]{1,0:T(8,128)S(1)} %collective-permute-done.9.refs_0_, ...), custom_call_target="tpu_custom_call" | custom-call | flops 1000 | bytes 118784 | tf_op jit(solution)/shard_map/pallas_call | solution.py:378
  (1 shorter events, 0.0 us)
Async XLA Ops:
  1.8 6.8 %collective-permute-start = (bf16[16,16,128]{2,1,0:T(8,128)(2,1)S(1)}, bf16[16,16,128]{2,1,0:T(8,128)(2,1)S(1)}, u32[]{:S(2)}, u32[]{:S(2)}) collective-permute-start(bf16[16,16,128]{2,1,0:T(8,128)(2,1)S(1)} %get-tuple-element.53), channel_id=1, source_target_pairs={{0,1},{1,0},{2,3},{3,2},{4,5},{5,4},{6,7},{7,6},{8,9},{9,8},{10,11... | collective-permute-start | bytes 196616 | tf_op jit(solution)/shard_map/ppermute | solution.py:407
  4.8 4.3 %collective-permute-start.1 = (bf16[16,16,128]{2,1,0:T(8,128)(2,1)S(1)}, bf16[16,16,128]{2,1,0:T(8,128)(2,1)S(1)}, u32[]{:S(2)}, u32[]{:S(2)}) collective-permute-start(bf16[16,16,128]{2,1,0:T(8,128)(2,1)S(1)} %get-tuple-element.54), channel_id=1, source_target_pairs={{0,8},{1,2},{2,1},{3,4},{4,3},{5,6},{6,5},{7,15},{8,0},{9,10},{10,... | collective-permute-start | bytes 196616 | tf_op jit(solution)/shard_map/ppermute | solution.py:407
  8.5 1.4 %collective-permute-start.3 = (f32[6,16,128]{2,1,0:T(8,128)S(1)}, f32[6,16,128]{2,1,0:T(8,128)S(1)}, u32[]{:S(2)}, u32[]{:S(2)}) collective-permute-start(f32[6,16,128]{2,1,0:T(8,128)S(1)} %get-tuple-element.65), channel_id=1, source_target_pairs={{0,16},{16,0},{1,17},{17,1},{2,18},{18,2},{3,19},{19,3},{4,20},{20... | collective-permute-start | bytes 147464 | tf_op jit(solution)/shard_map/ppermute | solution.py:467
  9.8 1.2 %collective-permute-start.2 = (f32[2,16,128]{2,1,0:T(8,128)S(1)}, f32[2,16,128]{2,1,0:T(8,128)S(1)}, u32[]{:S(2)}, u32[]{:S(2)}) collective-permute-start(f32[2,16,128]{2,1,0:T(8,128)S(1)} %get-tuple-element.61), channel_id=1, source_target_pairs={{0,16},{16,0},{1,17},{17,1},{2,18},{18,2},{3,19},{19,3},{4,20},{20... | collective-permute-start | bytes 49160 | tf_op jit(solution)/shard_map/ppermute | solution.py:481
  12.2 6.4 %collective-permute-start.8 = (f32[56,128]{1,0:T(8,128)S(1)}, f32[56,128]{1,0:T(8,128)S(1)}, u32[]{:S(2)}, u32[]{:S(2)}) collective-permute-start(f32[56,128]{1,0:T(8,128)S(1)} %get-tuple-element.76), channel_id=1, source_target_pairs={{0,10},{1,11},{2,8},{3,9},{4,14},{5,15},{6,12},{7,13},{8,2},{9,3},... | collective-permute-start | bytes 86024 | tf_op jit(solution)/shard_map/ppermute | solution.py:507
  15.7 3.9 %collective-permute-start.7 = (f32[56,128]{1,0:T(8,128)S(1)}, f32[56,128]{1,0:T(8,128)S(1)}, u32[]{:S(2)}, u32[]{:S(2)}) collective-permute-start(f32[56,128]{1,0:T(8,128)S(1)} %get-tuple-element.76), channel_id=1, source_target_pairs={{0,2},{1,3},{2,0},{3,1},{4,6},{5,7},{6,4},{7,5},{8,10},{9,11},{10,... | collective-permute-start | bytes 86024 | tf_op jit(solution)/shard_map/ppermute | solution.py:507
  15.7 4.1 %collective-permute-start.6 = (f32[56,128]{1,0:T(8,128)S(1)}, f32[56,128]{1,0:T(8,128)S(1)}, u32[]{:S(2)}, u32[]{:S(2)}) collective-permute-start(f32[56,128]{1,0:T(8,128)S(1)} %get-tuple-element.76), channel_id=1, source_target_pairs={{0,8},{1,9},{2,10},{3,11},{4,12},{5,13},{6,14},{7,15},{8,0},{9,1},... | collective-permute-start | bytes 86024 | tf_op jit(solution)/shard_map/ppermute | solution.py:507
  16.2 8.0 %collective-permute-start.4 = (bf16[256,128]{1,0:T(8,128)(2,1)S(1)}, bf16[256,128]{1,0:T(8,128)(2,1)S(1)}, u32[]{:S(2)}, u32[]{:S(2)}) collective-permute-start(bf16[256,128]{1,0:T(8,128)(2,1)S(1)} %get-tuple-element.72), channel_id=1, source_target_pairs={{0,1},{1,0},{2,3},{3,2},{4,5},{5,4},{6,7},{7,6},{8,9},{9,8},{10,11... | collective-permute-start | bytes 196616 | tf_op jit(solution)/shard_map/ppermute | solution.py:509
  17.2 7.1 %collective-permute-start.5 = (bf16[256,128]{1,0:T(8,128)(2,1)S(1)}, bf16[256,128]{1,0:T(8,128)(2,1)S(1)}, u32[]{:S(2)}, u32[]{:S(2)}) collective-permute-start(bf16[256,128]{1,0:T(8,128)(2,1)S(1)} %get-tuple-element.73), channel_id=1, source_target_pairs={{0,8},{1,2},{2,1},{3,4},{4,3},{5,6},{6,5},{7,15},{8,0},{9,10},{10,... | collective-permute-start | bytes 196616 | tf_op jit(solution)/shard_map/ppermute | solution.py:509
  19.8 7.0 %collective-permute-start.11 = (f32[56,128]{1,0:T(8,128)S(1)}, f32[56,128]{1,0:T(8,128)S(1)}, u32[]{:S(2)}, u32[]{:S(2)}) collective-permute-start(f32[56,128]{1,0:T(8,128)S(1)} %add_add_fusion.own_ref), channel_id=1, source_target_pairs={{0,5},{1,4},{2,7},{3,6},{4,1},{5,0},{6,3},{7,2},{8,13},{9,12},{10,... | collective-permute-start | bytes 86024 | tf_op jit(solution)/shard_map/ppermute | solution.py:507
  22.6 4.8 %collective-permute-start.10 = (f32[56,128]{1,0:T(8,128)S(1)}, f32[56,128]{1,0:T(8,128)S(1)}, u32[]{:S(2)}, u32[]{:S(2)}) collective-permute-start(f32[56,128]{1,0:T(8,128)S(1)} %add_add_fusion.own_ref), channel_id=1, source_target_pairs={{0,4},{1,5},{2,6},{3,7},{4,0},{5,1},{6,2},{7,3},{8,12},{9,13},{10,... | collective-permute-start | bytes 86024 | tf_op jit(solution)/shard_map/ppermute | solution.py:507
  22.9 4.4 %collective-permute-start.9 = (f32[56,128]{1,0:T(8,128)S(1)}, f32[56,128]{1,0:T(8,128)S(1)}, u32[]{:S(2)}, u32[]{:S(2)}) collective-permute-start(f32[56,128]{1,0:T(8,128)S(1)} %add_add_fusion.own_ref), channel_id=1, source_target_pairs={{0,1},{1,0},{2,3},{3,2},{4,5},{5,4},{6,7},{7,6},{8,9},{9,8},{10,11... | collective-permute-start | bytes 86024 | tf_op jit(solution)/shard_map/ppermute | solution.py:507

commit v8 on v7

--- a/solution.py
+++ b/solution.py
@@ -33,15 +33,13 @@
     return lax.dot_general(a, b, (((1,), (1,)), ((), ())), preferred_element_type=F32)
 
 
-def split3(x):
+def split(x):
     high = x.astype(BF)
-    rest = x - high.astype(F32)
-    mid = rest.astype(BF)
-    return high, mid, (rest - mid.astype(F32)).astype(BF)
+    return high, (x - high.astype(F32)).astype(BF)
 
 
 def dot_exact(x, ones):
-    return sum(dot(part, ones) for part in split3(x))
+    return sum(dot(part, ones) for part in split(x))
 
 
 def moved(x):
@@ -184,7 +182,7 @@
 
 
 def edge_kernel(
-    a_ref, b_ref, label_ref, mask_ref, head_bias_ref, band_ref, mat_ref, turner_ref, bias_ref, shifted_ref,
+    a_ref, b_ref, label_ref, mask_ref, head_bias_ref, band_ref, mat_ref, bias_ref, shifted_ref,
     halo_ref, hidden_ref, diff_ref, offered_ref,
 ):
     ch, hh, ww = a_ref.shape
@@ -201,8 +199,7 @@
     put_pair(hidden_ref, 0, 1, hidden, ww)
     put_pair(diff_ref, 0, 1, diff, ww)
     put_pair(offered_ref, 0, 1, offered, ww)
-    turned = dot(turner_ref[...], jnp.concatenate([before, after], axis=1)).astype(BF)
-    put_pair(halo_ref, 0, 1, turned, ww)
+    halo_ref[0], halo_ref[1] = before, after
 
 
 def backward_planes(diff_ref, weight_ref, hidden_ref, mat_t_ref, shifted_ref):
@@ -259,11 +256,11 @@
 
 
 def inner_backward_kernel(
-    turned_ref, weight_ref, hidden_ref, diff_ref, mat_t_ref, after_ref,
-    shifted_ref, total_ref, bias_ref, offset_ref, product_ref,
+    turned_ref, weight_ref, hidden_ref, diff_ref, mat_t_ref, halo_ref, turner_ref,
+    shifted_ref, total_ref, bias_ref, offset_ref, product_ref, halo_turned_ref,
 ):
-    del after_ref
     inner, rows, ww = hidden_ref.shape
+    put_pair(halo_turned_ref, 0, 1, dot(turner_ref[...], beside(halo_ref, 0, 1)).astype(BF), ww)
     hh = weight_ref.shape[1]
     _, bias_ref[...], offset_ref[...], product_ref[...] = backward_planes(
         diff_ref, weight_ref, hidden_ref, mat_t_ref, shifted_ref
@@ -284,6 +281,13 @@
     values, bias_sum, offset_sum, product = backward_planes(diff_ref, weight_ref, hidden_ref, mat_t_ref, shifted_ref)
     bias_sum, offset_sum = bias_sum + bias_in_ref[...], offset_sum + offset_in_ref[...]
     product = product + product_in_ref[...]
+    product = product.reshape(classes, hh, rows)
+    keep = over(iota((classes, hh, rows), 2), ch) == iota((classes, hh, rows), 1)
+    head = jnp.sum(jnp.where(keep, product, 0.0), axis=1)
+    by_last = (rest(iota((rows, 128), 0), ch) == rest(iota((rows, 128), 1), 16)).astype(F32).astype(BF)
+    head = dot_exact(head, by_last)
+    bias = jnp.sum(jnp.sum(bias_sum.reshape(hh, ch, ww), axis=0), axis=1, keepdims=True)
+    offset = jnp.sum(jnp.sum(offset_sum.reshape(classes, hh, ww), axis=1), axis=1, keepdims=True)
     odd = lax.rem(lax.axis_index("depth"), 2) == 1
     first, last = values[0].astype(F32), values[1].astype(F32)
     a_ref[...] = jnp.where(odd, first, last).astype(BF)
@@ -301,24 +305,12 @@
             i, j, k = t // 9, t // 3 % 3, t % 3
             value = jnp.where(part == i, totals[3 * k + j], 0.0)
             rows_ref[half, pl.ds(t, ch, stride=27)] = value[:, 128 * half : 128 * half + 128]
-    pick = (rest(iota((ch, 128), 1), ch) == iota((ch, 128), 0)).astype(F32).astype(BF)
-    sums = sum(dot_nt(pick, part) for half in range(2) for part in split3(rows_ref[half]))
+    pick = (rest(iota((ch, 256), 1), ch) == iota((ch, 256), 0)).astype(F32).astype(BF)
+    sums = sum(dot_nt(pick, part) for part in split(jnp.concatenate([rows_ref[0], rows_ref[1]], axis=1)))
     for q in range(3):
         packed_ref[q * ch : (q + 1) * ch] = sums[:, 128 * q : 128 * q + 128]
-    product = product.reshape(classes, hh, rows)
-    keep = over(iota((classes, hh, rows), 2), ch) == iota((classes, hh, rows), 1)
-    head = jnp.sum(jnp.where(keep, product, 0.0), axis=1)
-    by_last = (rest(iota((rows, 128), 0), ch) == rest(iota((rows, 128), 1), 16)).astype(F32).astype(BF)
-    head = dot_exact(head, by_last)
-    ones = jnp.ones((16, ww), F32).astype(BF)
-    bias = jnp.sum(bias_sum.reshape(hh, ch, ww), axis=0)
-    bias = jnp.concatenate([bias] * 8, axis=0)
-    bias = sum(dot_nt(ones, part) for part in split3(bias))[:classes]
-    offset = sum(dot_nt(ones, part) for part in split3(offset_sum))
-    by_class = (over(iota((classes * hh, 128), 0), hh) == rest(iota((classes * hh, 128), 1), 16)).astype(F32).astype(BF)
-    offset = dot_exact(offset, by_class)[:classes]
-    lane, row = iota((8, 128), 1), iota((8, 128), 0)
-    small = jnp.where(lane < 112, head, jnp.where(row == 0, bias, offset))
+    lane = iota((8, 128), 1)
+    small = jnp.where(lane < 112, head, jnp.where(lane == 112, bias[:8], jnp.where(lane == 113, bias[8:], offset)))
     low, high = sums[:8, 384:], pltpu.roll(sums[8:, 384:], 48, 1)
     packed_ref[3 * ch :] = jnp.where(lane < 48, low, jnp.where(lane < 96, high, small))
 
@@ -368,9 +360,11 @@
             value = jnp.where(lane < 128 - off, value, pltpu.roll(tiles[q + 1], 128 - off, 1))
         kernel_ref[co] = value[:, 0:27]
     head_ref[...] = pltpu.roll(tail, 32, 1)[:, 0:16]
-    biases = pltpu.roll(tail, 16, 1)
-    bias_ref[...] = biases[0:1, 0:16]
-    offset_ref[...] = biases[1:2, 0:8]
+    column, row = iota((8, ch), 1), iota((8, ch), 0)
+    low = jnp.where(column == row, tail[:, 112:113], 0.0) + jnp.where(column == row + 8, tail[:, 113:114], 0.0)
+    bias_ref[...] = jnp.sum(low, axis=0, keepdims=True)
+    diagonal = jnp.where(column[:, :8] == row[:, :8], tail[:, 114:115], 0.0)
+    offset_ref[...] = jnp.sum(diagonal, axis=0, keepdims=True)
 
 
 def call(kernel, out_shape, in_spaces, scratch, flops, args, out_spaces=None):
@@ -473,10 +467,10 @@
             sds((2, classes * hh, ww), F32),
             sds((2, hh, ww), F32),
         ),
-        (VM,) * 10,
+        (VM,) * 9,
         [],
         pair_flops,
-        (*far, label, mask, head_bias, band, mat, turn, bias, shifted),
+        (*far, label, mask, head_bias, band, mat, bias, shifted),
     )
     weight_edge = lax.ppermute(offered_edge, "net", peers)
     sums = (
@@ -485,13 +479,13 @@
         sds((classes * hh, ww), F32),
         sds((classes * hh, rows), F32),
     )
-    grads, *sums = call(
+    grads, *sums, halo = call(
         inner_backward_kernel,
-        (sds((inner, 3 * rows, ww), BF), *sums),
-        (VM,) * 6,
+        (sds((inner, 3 * rows, ww), BF), *sums, sds((2, rows, ww), BF)),
+        (VM,) * 7,
         [],
         pair_flops * inner // 2,
-        (turned_x, weight_in, hidden_in, diff_in, mat_t, halo),
+        (turned_x, weight_in, hidden_in, diff_in, mat_t, halo, turn),
     )
     edge = sds((rows, ww), BF)
     packed, grad_a, grad_b, grad_edge = call(

time: 28.3 us -> 28.2 us (level)
  no operation moved by 1% of the time
where the time goes in v8:
time: 28.2 us; the launch traced here: 28 us
  starting transfers between devices  15.6 us (55%)
  Pallas kernels  9.41 us (33%)
  waiting for transfers between devices  2.27 us (8%)
  between operations  0.7 us (2%)
    pallas_call x7, Pallas kernels, call(): pl.pallas_call(kernel, out_shape=out_shape, in_specs=[pl.BlockSpec(memory...  9.41 us
    ppermute x6, starting transfers between devices, body(): others = [lax.ppermute(packed, ('dp', 'depth'), p) for p in masks]  8.44 us
    ppermute x1, starting transfers between devices, exchanged(): lax.ppermute(a, ('dp', 'depth'), one)  3.03 us
    ppermute x2, starting transfers between devices, body(): lax.ppermute(e, ('dp', 'depth'), p)  2.49 us
    ppermute x6, waiting for transfers between devices, body(): others = [lax.ppermute(packed, ('dp', 'depth'), p) for p in masks]  1.7 us
    ppermute x1, starting transfers between devices, exchanged(): lax.ppermute(b, ('dp', 'depth'), two)  1.49 us
  transfers between devices with their start and end apart: 12, of which 5 were waited for; matrix products, arithmetic and copies ran while one was open for 0% of the time, Pallas kernels for 23%

profile of v8, /device:TPU:0, one launch (start us, length us, event | category | flops | bytes accessed | tf_op | source)
XLA Modules:
  0.0 28.0 jit_solution(776714023505543676)
XLA Ops:
  0.6 1.1 %shard_map.110 = (bf16[16,8,16,128]{3,2,1,0:T(8,128)(2,1)S(1)}, s32[8,16,128]{2,1,0:T(8,128)S(1)}, s32[8,16,128]{2,1,0:T(8,128)S(1)}, bf16[16,16,27]{2,1,0:T(8,1...) custom-call(bf16[16,8,16,128]{3,2,1,0:T(8,128)(2,1)} %bitcast.12, ...), custom_call_target="tpu_custom_call" | custom-call | bytes 669536 | tf_op jit(solution)/shard_map/pallas_call | solution.py:372
  1.8 3.0 %collective-permute-start.1 = (bf16[16,16,128]{2,1,0:T(8,128)(2,1)S(1)}, bf16[16,16,128]{2,1,0:T(8,128)(2,1)S(1)}, u32[]{:S(2)}, u32[]{:S(2)}) collective-permute-start(bf16[16,16,128]{2,1,0:T(8,128)(2,1)S(1)} %get-tuple-element.58), channel_id=1, source_target_pairs={{0,1},{1,0},{2,3},{3,2},{4,5},{5,4},{6,7},{7,6},{8,9},{9,8},{10,11... | collective-permute-start | bytes 196616 | tf_op jit(solution)/shard_map/ppermute | solution.py:401
  4.8 1.5 %collective-permute-start.2 = (bf16[16,16,128]{2,1,0:T(8,128)(2,1)S(1)}, bf16[16,16,128]{2,1,0:T(8,128)(2,1)S(1)}, u32[]{:S(2)}, u32[]{:S(2)}) collective-permute-start(bf16[16,16,128]{2,1,0:T(8,128)(2,1)S(1)} %get-tuple-element.59), channel_id=1, source_target_pairs={{0,8},{1,2},{2,1},{3,4},{4,3},{5,6},{6,5},{7,15},{8,0},{9,10},{10,... | collective-permute-start | bytes 196616 | tf_op jit(solution)/shard_map/ppermute | solution.py:401
  6.3 2.2 %shard_map.111 = (bf16[256,2304]{1,0:T(8,128)(2,1)S(1)}, bf16[128,256]{1,0:T(8,128)(2,1)S(1)}, bf16[256,128]{1,0:T(8,128)(2,1)S(1)}, bf16[256,256]{1,0:T(8,128)(...) custom-call(bf16[16,8,16,128]{3,2,1,0:T(8,128)(2,1)S(1)} %get-tuple-, ...), custom_call_target="tpu_custom_call" | custom-call | flops 905969664 | bytes 669536 | tf_op jit(solution)/shard_map/pallas_call | solution.py:372
  8.5 0.1 collective-permute-start
  8.6 0.0 collective-permute-done.1.a_ref
  8.6 0.5 %collective-permute-done.2.b_ref = bf16[16,16,128]{2,1,0:T(8,128)(2,1)S(1)} collective-permute-done((bf16[16,16,128]{2,1,0:T(8,128)(2,1)S(1)}, bf16[16,16,128]{2,1,0:T(8,128)(2,1)S(1)}, u32[]{:S(2)}, u32[]{:S(2)}) %collective-permute-start.2) | collective-permute-done | bytes 65568 | tf_op jit(solution)/shard_map/ppermute | solution.py:401
  9.1 0.7 %shard_map.112 = (bf16[2,256,128]{2,1,0:T(8,128)(2,1)S(1)}, bf16[2,256,128]{2,1,0:T(8,128)(2,1)S(1)}, f32[2,128,128]{2,1,0:T(8,128)S(1)}, f32[2,16,128]{2,1,0:T(8,128)S(1)}) custom-call(bf16[16,16,128]{2,1,0:T(8,128)(2,1)S(1)} %collective-permute-done.1.a_ref, bf16[16,16,128]{2,1,0:T(8,128)(2,1)S(1)} %collective-permute-done.2.b_ref, ...), custom_call_target="tpu_custom_call" | custom-call | flops 301989888 | bytes 3096608 | tf_op jit(solution)/shard_map/pallas_call | solution.py:372
  9.8 0.1 collective-permute-start.3
  9.9 0.0 collective-permute-done.weight_ref
  9.9 1.1 %shard_map.113 = (bf16[6,768,128]{2,1,0:T(8,128)(2,1)S(1)}, f32[9,16,256]{2,1,0:T(8,128)S(1)}, f32[256,128]{1,0:T(8,128)S(1)}, f32[128,128]{1,0:T(8,128)S(1)}, f...) custom-call(bf16[8,256,128]{2,1,0:T(8,128)(2,1)S(1)} %get-tuple-element.53.turned_ref, ...), custom_call_target="tpu_custom_call" | custom-call | flops 905969664 | bytes 1687552 | tf_op jit(solution)/shard_map/pallas_call | solution.py:372
  11.0 0.1 collective-permute-done.3.weight_ref
  11.0 1.0 %shard_map.114 = (f32[56,128]{1,0:T(8,128)S(1)}, bf16[256,128]{1,0:T(8,128)(2,1)S(1)}, bf16[256,128]{1,0:T(8,128)(2,1)S(1)}, bf16[2,768,128]{2,1,0:T(8,128)(2,1)S(1)}) custom-call(bf16[8,256,128]{2,1,0:T(8,128)(2,1)S(1)} %get-tuple-element.53.turned_ref, bf16[2,256,128]{2,1,0:T(8,128)(2,1)S(1)} %get-tuple-element.66.halo_ref, ...), custom_call_target="tpu_custom_call" | custom-call | flops 301989888 | bytes 1474560 | tf_op jit(solution)/shard_map/pallas_call | solution.py:372
  12.0 3.4 %collective-permute-start.8 = (f32[56,128]{1,0:T(8,128)S(1)}, f32[56,128]{1,0:T(8,128)S(1)}, u32[]{:S(2)}, u32[]{:S(2)}) collective-permute-start(f32[56,128]{1,0:T(8,128)S(1)} %get-tuple-element.78), channel_id=1, source_target_pairs={{0,10},{1,11},{2,8},{3,9},{4,14},{5,15},{6,12},{7,13},{8,2},{9,3},... | collective-permute-start | bytes 86024 | tf_op jit(solution)/shard_map/ppermute | solution.py:501
  15.4 0.0 collective-permute-start.7
  15.4 0.6 %collective-permute-start.6 = (f32[56,128]{1,0:T(8,128)S(1)}, f32[56,128]{1,0:T(8,128)S(1)}, u32[]{:S(2)}, u32[]{:S(2)}) collective-permute-start(f32[56,128]{1,0:T(8,128)S(1)} %get-tuple-element.78), channel_id=1, source_target_pairs={{0,8},{1,9},{2,10},{3,11},{4,12},{5,13},{6,14},{7,15},{8,0},{9,1},... | collective-permute-start | bytes 86024 | tf_op jit(solution)/shard_map/ppermute | solution.py:501
  16.0 1.0 %collective-permute-start.4 = (bf16[256,128]{1,0:T(8,128)(2,1)S(1)}, bf16[256,128]{1,0:T(8,128)(2,1)S(1)}, u32[]{:S(2)}, u32[]{:S(2)}) collective-permute-start(bf16[256,128]{1,0:T(8,128)(2,1)S(1)} %get-tuple-element.74), channel_id=1, source_target_pairs={{0,1},{1,0},{2,3},{3,2},{4,5},{5,4},{6,7},{7,6},{8,9},{9,8},{10,11... | collective-permute-start | bytes 196616 | tf_op jit(solution)/shard_map/ppermute | solution.py:503
  17.0 1.5 %collective-permute-start.5 = (bf16[256,128]{1,0:T(8,128)(2,1)S(1)}, bf16[256,128]{1,0:T(8,128)(2,1)S(1)}, u32[]{:S(2)}, u32[]{:S(2)}) collective-permute-start(bf16[256,128]{1,0:T(8,128)(2,1)S(1)} %get-tuple-element.75), channel_id=1, source_target_pairs={{0,8},{1,2},{2,1},{3,4},{4,3},{5,6},{6,5},{7,15},{8,0},{9,10},{10,... | collective-permute-start | bytes 196616 | tf_op jit(solution)/shard_map/ppermute | solution.py:503
  18.5 0.0 collective-permute-done.8
  18.5 0.8 %collective-permute-done.7 = f32[56,128]{1,0:T(8,128)S(1)} collective-permute-done((f32[56,128]{1,0:T(8,128)S(1)}, f32[56,128]{1,0:T(8,128)S(1)}, u32[]{:S(2)}, u32[]{:S(2)}) %collective-permute-start.7) | collective-permute-done | bytes 28704 | tf_op jit(solution)/shard_map/ppermute | solution.py:501
  19.3 0.3 %collective-permute-done.6 = f32[56,128]{1,0:T(8,128)S(1)} collective-permute-done((f32[56,128]{1,0:T(8,128)S(1)}, f32[56,128]{1,0:T(8,128)S(1)}, u32[]{:S(2)}, u32[]{:S(2)}) %collective-permute-start.6) | collective-permute-done | bytes 28704 | tf_op jit(solution)/shard_map/ppermute | solution.py:501
  19.6 2.8 %collective-permute-start.11 = (f32[56,128]{1,0:T(8,128)S(1)}, f32[56,128]{1,0:T(8,128)S(1)}, u32[]{:S(2)}, u32[]{:S(2)}) collective-permute-start(f32[56,128]{1,0:T(8,128)S(1)} %add_add_fusion.own_ref), channel_id=1, source_target_pairs={{0,5},{1,4},{2,7},{3,6},{4,1},{5,0},{6,3},{7,2},{8,13},{9,12},{10,... | collective-permute-start | bytes 86024 | tf_op jit(solution)/shard_map/ppermute | solution.py:501
  22.4 0.3 %collective-permute-start.10 = (f32[56,128]{1,0:T(8,128)S(1)}, f32[56,128]{1,0:T(8,128)S(1)}, u32[]{:S(2)}, u32[]{:S(2)}) collective-permute-start(f32[56,128]{1,0:T(8,128)S(1)} %add_add_fusion.own_ref), channel_id=1, source_target_pairs={{0,4},{1,5},{2,6},{3,7},{4,0},{5,1},{6,2},{7,3},{8,12},{9,13},{10,... | collective-permute-start | bytes 86024 | tf_op jit(solution)/shard_map/ppermute | solution.py:501
  22.8 1.3 %collective-permute-start.9 = (f32[56,128]{1,0:T(8,128)S(1)}, f32[56,128]{1,0:T(8,128)S(1)}, u32[]{:S(2)}, u32[]{:S(2)}) collective-permute-start(f32[56,128]{1,0:T(8,128)S(1)} %add_add_fusion.own_ref), channel_id=1, source_target_pairs={{0,1},{1,0},{2,3},{3,2},{4,5},{5,4},{6,7},{7,6},{8,9},{9,8},{10,11... | collective-permute-start | bytes 86024 | tf_op jit(solution)/shard_map/ppermute | solution.py:501
  24.1 0.0 collective-permute-done.4.a_ref
  24.1 0.0 collective-permute-done.5.b_ref
  24.1 2.5 %shard_map.115 = (bf16[16,8,16,128]{3,2,1,0:T(8,128)(2,1)}, f32[8,128]{1,0:T(8,128)S(1)}) custom-call(bf16[256,128]{1,0:T(8,128)(2,1)S(1)} %collective-permute-done.4.a_ref, bf16[256,128]{1,0:T(8,128)(2,1)S(1)} %collective-permute-done.5.b_ref, bf16[6,768,128]{2,1,0:T(8,128)(2,1)S(1)} %get-tuple-element.76.shifted_ref, ...), custom_call_target="tpu_custom_call" | custom-call | flops 1207959552 | bytes 2883584 | tf_op jit(solution)/shard_map/pallas_call | solution.py:372
  26.6 0.0 collective-permute-done.11.refs_2_
  26.6 0.6 %collective-permute-done.10.refs_1_ = f32[56,128]{1,0:T(8,128)S(1)} collective-permute-done((f32[56,128]{1,0:T(8,128)S(1)}, f32[56,128]{1,0:T(8,128)S(1)}, u32[]{:S(2)}, u32[]{:S(2)}) %collective-permute-start.10) | collective-permute-done | bytes 28704 | tf_op jit(solution)/shard_map/ppermute | solution.py:501
  27.2 0.0 collective-permute-done.9.refs_0_
  27.2 0.8 %shard_map.116 = (f32[16,16,27]{2,1,0:T(8,128)}, f32[1,16]{1,0:T(1,128)}, f32[8,16]{1,0:T(8,128)}, f32[1,8]{1,0:T(1,128)}) custom-call(f32[8,128]{1,0:T(8,128)S(1)} %get-tuple-element.81.token_ref, f32[56,128]{1,0:T(8,128)S(1)} %add_add_fusion.own_ref, f32[56,128]{1,0:T(8,128)S(1)} %collective-permute-done.9.refs_0_, ...), custom_call_target="tpu_custom_call" | custom-call | flops 1000 | bytes 118784 | tf_op jit(solution)/shard_map/pallas_call | solution.py:372
  (1 shorter events, 0.0 us)
Async XLA Ops:
  1.8 6.8 %collective-permute-start.1 = (bf16[16,16,128]{2,1,0:T(8,128)(2,1)S(1)}, bf16[16,16,128]{2,1,0:T(8,128)(2,1)S(1)}, u32[]{:S(2)}, u32[]{:S(2)}) collective-permute-start(bf16[16,16,128]{2,1,0:T(8,128)(2,1)S(1)} %get-tuple-element.58), channel_id=1, source_target_pairs={{0,1},{1,0},{2,3},{3,2},{4,5},{5,4},{6,7},{7,6},{8,9},{9,8},{10,11... | collective-permute-start | bytes 196616 | tf_op jit(solution)/shard_map/ppermute | solution.py:401
  4.8 4.3 %collective-permute-start.2 = (bf16[16,16,128]{2,1,0:T(8,128)(2,1)S(1)}, bf16[16,16,128]{2,1,0:T(8,128)(2,1)S(1)}, u32[]{:S(2)}, u32[]{:S(2)}) collective-permute-start(bf16[16,16,128]{2,1,0:T(8,128)(2,1)S(1)} %get-tuple-element.59), channel_id=1, source_target_pairs={{0,8},{1,2},{2,1},{3,4},{4,3},{5,6},{6,5},{7,15},{8,0},{9,10},{10,... | collective-permute-start | bytes 196616 | tf_op jit(solution)/shard_map/ppermute | solution.py:401
  8.5 1.4 %collective-permute-start = (f32[6,16,128]{2,1,0:T(8,128)S(1)}, f32[6,16,128]{2,1,0:T(8,128)S(1)}, u32[]{:S(2)}, u32[]{:S(2)}) collective-permute-start(f32[6,16,128]{2,1,0:T(8,128)S(1)} %get-tuple-element.54), channel_id=1, source_target_pairs={{0,16},{16,0},{1,17},{17,1},{2,18},{18,2},{3,19},{19,3},{4,20},{20... | collective-permute-start | bytes 147464 | tf_op jit(solution)/shard_map/ppermute | solution.py:461
  9.8 1.2 %collective-permute-start.3 = (f32[2,16,128]{2,1,0:T(8,128)S(1)}, f32[2,16,128]{2,1,0:T(8,128)S(1)}, u32[]{:S(2)}, u32[]{:S(2)}) collective-permute-start(f32[2,16,128]{2,1,0:T(8,128)S(1)} %get-tuple-element.67), channel_id=1, source_target_pairs={{0,16},{16,0},{1,17},{17,1},{2,18},{18,2},{3,19},{19,3},{4,20},{20... | collective-permute-start | bytes 49160 | tf_op jit(solution)/shard_map/ppermute | solution.py:475
  12.0 6.5 %collective-permute-start.8 = (f32[56,128]{1,0:T(8,128)S(1)}, f32[56,128]{1,0:T(8,128)S(1)}, u32[]{:S(2)}, u32[]{:S(2)}) collective-permute-start(f32[56,128]{1,0:T(8,128)S(1)} %get-tuple-element.78), channel_id=1, source_target_pairs={{0,10},{1,11},{2,8},{3,9},{4,14},{5,15},{6,12},{7,13},{8,2},{9,3},... | collective-permute-start | bytes 86024 | tf_op jit(solution)/shard_map/ppermute | solution.py:501
  15.4 3.9 %collective-permute-start.7 = (f32[56,128]{1,0:T(8,128)S(1)}, f32[56,128]{1,0:T(8,128)S(1)}, u32[]{:S(2)}, u32[]{:S(2)}) collective-permute-start(f32[56,128]{1,0:T(8,128)S(1)} %get-tuple-element.78), channel_id=1, source_target_pairs={{0,2},{1,3},{2,0},{3,1},{4,6},{5,7},{6,4},{7,5},{8,10},{9,11},{10,... | collective-permute-start | bytes 86024 | tf_op jit(solution)/shard_map/ppermute | solution.py:501
  15.4 4.2 %collective-permute-start.6 = (f32[56,128]{1,0:T(8,128)S(1)}, f32[56,128]{1,0:T(8,128)S(1)}, u32[]{:S(2)}, u32[]{:S(2)}) collective-permute-start(f32[56,128]{1,0:T(8,128)S(1)} %get-tuple-element.78), channel_id=1, source_target_pairs={{0,8},{1,9},{2,10},{3,11},{4,12},{5,13},{6,14},{7,15},{8,0},{9,1},... | collective-permute-start | bytes 86024 | tf_op jit(solution)/shard_map/ppermute | solution.py:501
  16.0 8.1 %collective-permute-start.4 = (bf16[256,128]{1,0:T(8,128)(2,1)S(1)}, bf16[256,128]{1,0:T(8,128)(2,1)S(1)}, u32[]{:S(2)}, u32[]{:S(2)}) collective-permute-start(bf16[256,128]{1,0:T(8,128)(2,1)S(1)} %get-tuple-element.74), channel_id=1, source_target_pairs={{0,1},{1,0},{2,3},{3,2},{4,5},{5,4},{6,7},{7,6},{8,9},{9,8},{10,11... | collective-permute-start | bytes 196616 | tf_op jit(solution)/shard_map/ppermute | solution.py:503
  17.0 7.1 %collective-permute-start.5 = (bf16[256,128]{1,0:T(8,128)(2,1)S(1)}, bf16[256,128]{1,0:T(8,128)(2,1)S(1)}, u32[]{:S(2)}, u32[]{:S(2)}) collective-permute-start(bf16[256,128]{1,0:T(8,128)(2,1)S(1)} %get-tuple-element.75), channel_id=1, source_target_pairs={{0,8},{1,2},{2,1},{3,4},{4,3},{5,6},{6,5},{7,15},{8,0},{9,10},{10,... | collective-permute-start | bytes 196616 | tf_op jit(solution)/shard_map/ppermute | solution.py:503
  19.6 7.0 %collective-permute-start.11 = (f32[56,128]{1,0:T(8,128)S(1)}, f32[56,128]{1,0:T(8,128)S(1)}, u32[]{:S(2)}, u32[]{:S(2)}) collective-permute-start(f32[56,128]{1,0:T(8,128)S(1)} %add_add_fusion.own_ref), channel_id=1, source_target_pairs={{0,5},{1,4},{2,7},{3,6},{4,1},{5,0},{6,3},{7,2},{8,13},{9,12},{10,... | collective-permute-start | bytes 86024 | tf_op jit(solution)/shard_map/ppermute | solution.py:501
  22.4 4.8 %collective-permute-start.10 = (f32[56,128]{1,0:T(8,128)S(1)}, f32[56,128]{1,0:T(8,128)S(1)}, u32[]{:S(2)}, u32[]{:S(2)}) collective-permute-start(f32[56,128]{1,0:T(8,128)S(1)} %add_add_fusion.own_ref), channel_id=1, source_target_pairs={{0,4},{1,5},{2,6},{3,7},{4,0},{5,1},{6,2},{7,3},{8,12},{9,13},{10,... | collective-permute-start | bytes 86024 | tf_op jit(solution)/shard_map/ppermute | solution.py:501
  22.8 4.4 %collective-permute-start.9 = (f32[56,128]{1,0:T(8,128)S(1)}, f32[56,128]{1,0:T(8,128)S(1)}, u32[]{:S(2)}, u32[]{:S(2)}) collective-permute-start(f32[56,128]{1,0:T(8,128)S(1)} %add_add_fusion.own_ref), channel_id=1, source_target_pairs={{0,1},{1,0},{2,3},{3,2},{4,5},{5,4},{6,7},{7,6},{8,9},{9,8},{10,11... | collective-permute-start | bytes 86024 | tf_op jit(solution)/shard_map/ppermute | solution.py:501

commit v9 on v8

--- a/solution.py
+++ b/solution.py
@@ -300,7 +300,6 @@
     totals = weight_products(shifted_ref, fields, ch, hh, [total_ref[n] for n in range(9)])
     part = over(iota((ch, 256), 1), ch * (STEP + 2))
     for half in range(2):
-        rows_ref[half, 27 * ch :] = jnp.zeros((512 - 27 * ch, 128), F32)
         for t in range(27):
             i, j, k = t // 9, t // 3 % 3, t % 3
             value = jnp.where(part == i, totals[3 * k + j], 0.0)
@@ -311,7 +310,8 @@
         packed_ref[q * ch : (q + 1) * ch] = sums[:, 128 * q : 128 * q + 128]
     lane = iota((8, 128), 1)
     small = jnp.where(lane < 112, head, jnp.where(lane == 112, bias[:8], jnp.where(lane == 113, bias[8:], offset)))
-    low, high = sums[:8, 384:], pltpu.roll(sums[8:, 384:], 48, 1)
+    last = jnp.concatenate([sums[:, 384:], jnp.zeros((ch, 80), F32)], axis=1)
+    low, high = last[:8], pltpu.roll(last[8:], 48, 1)
     packed_ref[3 * ch :] = jnp.where(lane < 48, low, jnp.where(lane < 96, high, small))
 
 
@@ -492,7 +492,7 @@
         edge_backward_kernel,
         (sds((3 * ch + 8, 128), F32), edge, edge, sds((2, 3 * rows, ww), BF)),
         (VM,) * 10,
-        [VM((2, 32 * ch, 128), F32)],
+        [VM((2, 27 * ch, 128), F32)],
         pair_flops,
         (turned_x, halo, weight_edge, hidden_edge, diff_edge, mat_t, *sums),
     )

time: 28.2 us -> 28.1 us (level)
  no operation moved by 1% of the time
where the time goes in v9:
time: 28.1 us; the launch traced here: 27.9 us
  starting transfers between devices  15.6 us (56%)
  Pallas kernels  9.31 us (33%)
  waiting for transfers between devices  2.27 us (8%)
  between operations  0.7 us (2%)
    pallas_call x7, Pallas kernels, call(): pl.pallas_call(kernel, out_shape=out_shape, in_specs=[pl.BlockSpec(memory...  9.31 us
    ppermute x6, starting transfers between devices, body(): others = [lax.ppermute(packed, ('dp', 'depth'), p) for p in masks]  8.47 us
    ppermute x1, starting transfers between devices, exchanged(): lax.ppermute(a, ('dp', 'depth'), one)  3.03 us
    ppermute x2, starting transfers between devices, body(): lax.ppermute(e, ('dp', 'depth'), p)  2.47 us
    ppermute x6, waiting for transfers between devices, body(): others = [lax.ppermute(packed, ('dp', 'depth'), p) for p in masks]  1.7 us
    ppermute x1, starting transfers between devices, exchanged(): lax.ppermute(b, ('dp', 'depth'), two)  1.49 us
  transfers between devices with their start and end apart: 12, of which 5 were waited for; matrix products, arithmetic and copies ran while one was open for 0% of the time, Pallas kernels for 23%

profile of v9, /device:TPU:0, one launch (start us, length us, event | category | flops | bytes accessed | tf_op | source)
XLA Modules:
  0.0 27.9 jit_solution(12220853082623918799)
XLA Ops:
  0.6 1.1 %shard_map.110 = (bf16[16,8,16,128]{3,2,1,0:T(8,128)(2,1)S(1)}, s32[8,16,128]{2,1,0:T(8,128)S(1)}, s32[8,16,128]{2,1,0:T(8,128)S(1)}, bf16[16,16,27]{2,1,0:T(8,1...) custom-call(bf16[16,8,16,128]{3,2,1,0:T(8,128)(2,1)} %bitcast.12, ...), custom_call_target="tpu_custom_call" | custom-call | bytes 669536 | tf_op jit(solution)/shard_map/pallas_call | solution.py:372
  1.8 3.0 %collective-permute-start.1 = (bf16[16,16,128]{2,1,0:T(8,128)(2,1)S(1)}, bf16[16,16,128]{2,1,0:T(8,128)(2,1)S(1)}, u32[]{:S(2)}, u32[]{:S(2)}) collective-permute-start(bf16[16,16,128]{2,1,0:T(8,128)(2,1)S(1)} %get-tuple-element.58), channel_id=1, source_target_pairs={{0,1},{1,0},{2,3},{3,2},{4,5},{5,4},{6,7},{7,6},{8,9},{9,8},{10,11... | collective-permute-start | bytes 196616 | tf_op jit(solution)/shard_map/ppermute | solution.py:401
  4.8 1.5 %collective-permute-start.2 = (bf16[16,16,128]{2,1,0:T(8,128)(2,1)S(1)}, bf16[16,16,128]{2,1,0:T(8,128)(2,1)S(1)}, u32[]{:S(2)}, u32[]{:S(2)}) collective-permute-start(bf16[16,16,128]{2,1,0:T(8,128)(2,1)S(1)} %get-tuple-element.59), channel_id=1, source_target_pairs={{0,8},{1,2},{2,1},{3,4},{4,3},{5,6},{6,5},{7,15},{8,0},{9,10},{10,... | collective-permute-start | bytes 196616 | tf_op jit(solution)/shard_map/ppermute | solution.py:401
  6.3 2.2 %shard_map.111 = (bf16[256,2304]{1,0:T(8,128)(2,1)S(1)}, bf16[128,256]{1,0:T(8,128)(2,1)S(1)}, bf16[256,128]{1,0:T(8,128)(2,1)S(1)}, bf16[256,256]{1,0:T(8,128)(...) custom-call(bf16[16,8,16,128]{3,2,1,0:T(8,128)(2,1)S(1)} %get-tuple-, ...), custom_call_target="tpu_custom_call" | custom-call | flops 905969664 | bytes 669536 | tf_op jit(solution)/shard_map/pallas_call | solution.py:372
  8.5 0.1 collective-permute-start
  8.6 0.0 collective-permute-done.1.a_ref
  8.6 0.5 %collective-permute-done.2.b_ref = bf16[16,16,128]{2,1,0:T(8,128)(2,1)S(1)} collective-permute-done((bf16[16,16,128]{2,1,0:T(8,128)(2,1)S(1)}, bf16[16,16,128]{2,1,0:T(8,128)(2,1)S(1)}, u32[]{:S(2)}, u32[]{:S(2)}) %collective-permute-start.2) | collective-permute-done | bytes 65568 | tf_op jit(solution)/shard_map/ppermute | solution.py:401
  9.1 0.7 %shard_map.112 = (bf16[2,256,128]{2,1,0:T(8,128)(2,1)S(1)}, bf16[2,256,128]{2,1,0:T(8,128)(2,1)S(1)}, f32[2,128,128]{2,1,0:T(8,128)S(1)}, f32[2,16,128]{2,1,0:T(8,128)S(1)}) custom-call(bf16[16,16,128]{2,1,0:T(8,128)(2,1)S(1)} %collective-permute-done.1.a_ref, bf16[16,16,128]{2,1,0:T(8,128)(2,1)S(1)} %collective-permute-done.2.b_ref, ...), custom_call_target="tpu_custom_call" | custom-call | flops 301989888 | bytes 3096608 | tf_op jit(solution)/shard_map/pallas_call | solution.py:372
  9.8 0.1 collective-permute-start.3
  9.9 0.0 collective-permute-done.weight_ref
  9.9 1.1 %shard_map.113 = (bf16[6,768,128]{2,1,0:T(8,128)(2,1)S(1)}, f32[9,16,256]{2,1,0:T(8,128)S(1)}, f32[256,128]{1,0:T(8,128)S(1)}, f32[128,128]{1,0:T(8,128)S(1)}, f...) custom-call(bf16[8,256,128]{2,1,0:T(8,128)(2,1)S(1)} %get-tuple-element.53.turned_ref, ...), custom_call_target="tpu_custom_call" | custom-call | flops 905969664 | bytes 1687552 | tf_op jit(solution)/shard_map/pallas_call | solution.py:372
  11.0 0.1 collective-permute-done.3.weight_ref
  11.0 0.9 %shard_map.114 = (f32[56,128]{1,0:T(8,128)S(1)}, bf16[256,128]{1,0:T(8,128)(2,1)S(1)}, bf16[256,128]{1,0:T(8,128)(2,1)S(1)}, bf16[2,768,128]{2,1,0:T(8,128)(2,1)S(1)}) custom-call(bf16[8,256,128]{2,1,0:T(8,128)(2,1)S(1)} %get-tuple-element.53.turned_ref, bf16[2,256,128]{2,1,0:T(8,128)(2,1)S(1)} %get-tuple-element.66.halo_ref, ...), custom_call_target="tpu_custom_call" | custom-call | flops 301989888 | bytes 1474560 | tf_op jit(solution)/shard_map/pallas_call | solution.py:372
  11.9 3.4 %collective-permute-start.8 = (f32[56,128]{1,0:T(8,128)S(1)}, f32[56,128]{1,0:T(8,128)S(1)}, u32[]{:S(2)}, u32[]{:S(2)}) collective-permute-start(f32[56,128]{1,0:T(8,128)S(1)} %get-tuple-element.78), channel_id=1, source_target_pairs={{0,10},{1,11},{2,8},{3,9},{4,14},{5,15},{6,12},{7,13},{8,2},{9,3},... | collective-permute-start | bytes 86024 | tf_op jit(solution)/shard_map/ppermute | solution.py:501
  15.3 0.0 collective-permute-start.7
  15.3 0.6 %collective-permute-start.6 = (f32[56,128]{1,0:T(8,128)S(1)}, f32[56,128]{1,0:T(8,128)S(1)}, u32[]{:S(2)}, u32[]{:S(2)}) collective-permute-start(f32[56,128]{1,0:T(8,128)S(1)} %get-tuple-element.78), channel_id=1, source_target_pairs={{0,8},{1,9},{2,10},{3,11},{4,12},{5,13},{6,14},{7,15},{8,0},{9,1},... | collective-permute-start | bytes 86024 | tf_op jit(solution)/shard_map/ppermute | solution.py:501
  15.9 1.0 %collective-permute-start.4 = (bf16[256,128]{1,0:T(8,128)(2,1)S(1)}, bf16[256,128]{1,0:T(8,128)(2,1)S(1)}, u32[]{:S(2)}, u32[]{:S(2)}) collective-permute-start(bf16[256,128]{1,0:T(8,128)(2,1)S(1)} %get-tuple-element.74), channel_id=1, source_target_pairs={{0,1},{1,0},{2,3},{3,2},{4,5},{5,4},{6,7},{7,6},{8,9},{9,8},{10,11... | collective-permute-start | bytes 196616 | tf_op jit(solution)/shard_map/ppermute | solution.py:503
  16.9 1.5 %collective-permute-start.5 = (bf16[256,128]{1,0:T(8,128)(2,1)S(1)}, bf16[256,128]{1,0:T(8,128)(2,1)S(1)}, u32[]{:S(2)}, u32[]{:S(2)}) collective-permute-start(bf16[256,128]{1,0:T(8,128)(2,1)S(1)} %get-tuple-element.75), channel_id=1, source_target_pairs={{0,8},{1,2},{2,1},{3,4},{4,3},{5,6},{6,5},{7,15},{8,0},{9,10},{10,... | collective-permute-start | bytes 196616 | tf_op jit(solution)/shard_map/ppermute | solution.py:503
  18.4 0.0 collective-permute-done.8
  18.4 0.8 %collective-permute-done.7 = f32[56,128]{1,0:T(8,128)S(1)} collective-permute-done((f32[56,128]{1,0:T(8,128)S(1)}, f32[56,128]{1,0:T(8,128)S(1)}, u32[]{:S(2)}, u32[]{:S(2)}) %collective-permute-start.7) | collective-permute-done | bytes 28704 | tf_op jit(solution)/shard_map/ppermute | solution.py:501
  19.2 0.3 %collective-permute-done.6 = f32[56,128]{1,0:T(8,128)S(1)} collective-permute-done((f32[56,128]{1,0:T(8,128)S(1)}, f32[56,128]{1,0:T(8,128)S(1)}, u32[]{:S(2)}, u32[]{:S(2)}) %collective-permute-start.6) | collective-permute-done | bytes 28704 | tf_op jit(solution)/shard_map/ppermute | solution.py:501
  19.5 2.8 %collective-permute-start.11 = (f32[56,128]{1,0:T(8,128)S(1)}, f32[56,128]{1,0:T(8,128)S(1)}, u32[]{:S(2)}, u32[]{:S(2)}) collective-permute-start(f32[56,128]{1,0:T(8,128)S(1)} %add_add_fusion.own_ref), channel_id=1, source_target_pairs={{0,5},{1,4},{2,7},{3,6},{4,1},{5,0},{6,3},{7,2},{8,13},{9,12},{10,... | collective-permute-start | bytes 86024 | tf_op jit(solution)/shard_map/ppermute | solution.py:501
  22.3 0.3 %collective-permute-start.10 = (f32[56,128]{1,0:T(8,128)S(1)}, f32[56,128]{1,0:T(8,128)S(1)}, u32[]{:S(2)}, u32[]{:S(2)}) collective-permute-start(f32[56,128]{1,0:T(8,128)S(1)} %add_add_fusion.own_ref), channel_id=1, source_target_pairs={{0,4},{1,5},{2,6},{3,7},{4,0},{5,1},{6,2},{7,3},{8,12},{9,13},{10,... | collective-permute-start | bytes 86024 | tf_op jit(solution)/shard_map/ppermute | solution.py:501
  22.7 1.3 %collective-permute-start.9 = (f32[56,128]{1,0:T(8,128)S(1)}, f32[56,128]{1,0:T(8,128)S(1)}, u32[]{:S(2)}, u32[]{:S(2)}) collective-permute-start(f32[56,128]{1,0:T(8,128)S(1)} %add_add_fusion.own_ref), channel_id=1, source_target_pairs={{0,1},{1,0},{2,3},{3,2},{4,5},{5,4},{6,7},{7,6},{8,9},{9,8},{10,11... | collective-permute-start | bytes 86024 | tf_op jit(solution)/shard_map/ppermute | solution.py:501
  24.0 0.0 collective-permute-done.4.a_ref
  24.0 0.0 collective-permute-done.5.b_ref
  24.0 2.5 %shard_map.115 = (bf16[16,8,16,128]{3,2,1,0:T(8,128)(2,1)}, f32[8,128]{1,0:T(8,128)S(1)}) custom-call(bf16[256,128]{1,0:T(8,128)(2,1)S(1)} %collective-permute-done.4.a_ref, bf16[256,128]{1,0:T(8,128)(2,1)S(1)} %collective-permute-done.5.b_ref, bf16[6,768,128]{2,1,0:T(8,128)(2,1)S(1)} %get-tuple-element.76.shifted_ref, ...), custom_call_target="tpu_custom_call" | custom-call | flops 1207959552 | bytes 2883584 | tf_op jit(solution)/shard_map/pallas_call | solution.py:372
  26.5 0.0 collective-permute-done.11.refs_2_
  26.5 0.6 %collective-permute-done.10.refs_1_ = f32[56,128]{1,0:T(8,128)S(1)} collective-permute-done((f32[56,128]{1,0:T(8,128)S(1)}, f32[56,128]{1,0:T(8,128)S(1)}, u32[]{:S(2)}, u32[]{:S(2)}) %collective-permute-start.10) | collective-permute-done | bytes 28704 | tf_op jit(solution)/shard_map/ppermute | solution.py:501
  27.1 0.0 collective-permute-done.9.refs_0_
  27.1 0.8 %shard_map.116 = (f32[16,16,27]{2,1,0:T(8,128)}, f32[1,16]{1,0:T(1,128)}, f32[8,16]{1,0:T(8,128)}, f32[1,8]{1,0:T(1,128)}) custom-call(f32[8,128]{1,0:T(8,128)S(1)} %get-tuple-element.81.token_ref, f32[56,128]{1,0:T(8,128)S(1)} %add_add_fusion.own_ref, f32[56,128]{1,0:T(8,128)S(1)} %collective-permute-done.9.refs_0_, ...), custom_call_target="tpu_custom_call" | custom-call | flops 1000 | bytes 118784 | tf_op jit(solution)/shard_map/pallas_call | solution.py:372
  (1 shorter events, 0.0 us)
Async XLA Ops:
  1.8 6.8 %collective-permute-start.1 = (bf16[16,16,128]{2,1,0:T(8,128)(2,1)S(1)}, bf16[16,16,128]{2,1,0:T(8,128)(2,1)S(1)}, u32[]{:S(2)}, u32[]{:S(2)}) collective-permute-start(bf16[16,16,128]{2,1,0:T(8,128)(2,1)S(1)} %get-tuple-element.58), channel_id=1, source_target_pairs={{0,1},{1,0},{2,3},{3,2},{4,5},{5,4},{6,7},{7,6},{8,9},{9,8},{10,11... | collective-permute-start | bytes 196616 | tf_op jit(solution)/shard_map/ppermute | solution.py:401
  4.8 4.3 %collective-permute-start.2 = (bf16[16,16,128]{2,1,0:T(8,128)(2,1)S(1)}, bf16[16,16,128]{2,1,0:T(8,128)(2,1)S(1)}, u32[]{:S(2)}, u32[]{:S(2)}) collective-permute-start(bf16[16,16,128]{2,1,0:T(8,128)(2,1)S(1)} %get-tuple-element.59), channel_id=1, source_target_pairs={{0,8},{1,2},{2,1},{3,4},{4,3},{5,6},{6,5},{7,15},{8,0},{9,10},{10,... | collective-permute-start | bytes 196616 | tf_op jit(solution)/shard_map/ppermute | solution.py:401
  8.5 1.4 %collective-permute-start = (f32[6,16,128]{2,1,0:T(8,128)S(1)}, f32[6,16,128]{2,1,0:T(8,128)S(1)}, u32[]{:S(2)}, u32[]{:S(2)}) collective-permute-start(f32[6,16,128]{2,1,0:T(8,128)S(1)} %get-tuple-element.54), channel_id=1, source_target_pairs={{0,16},{16,0},{1,17},{17,1},{2,18},{18,2},{3,19},{19,3},{4,20},{20... | collective-permute-start | bytes 147464 | tf_op jit(solution)/shard_map/ppermute | solution.py:461
  9.8 1.2 %collective-permute-start.3 = (f32[2,16,128]{2,1,0:T(8,128)S(1)}, f32[2,16,128]{2,1,0:T(8,128)S(1)}, u32[]{:S(2)}, u32[]{:S(2)}) collective-permute-start(f32[2,16,128]{2,1,0:T(8,128)S(1)} %get-tuple-element.67), channel_id=1, source_target_pairs={{0,16},{16,0},{1,17},{17,1},{2,18},{18,2},{3,19},{19,3},{4,20},{20... | collective-permute-start | bytes 49160 | tf_op jit(solution)/shard_map/ppermute | solution.py:475
  11.9 6.5 %collective-permute-start.8 = (f32[56,128]{1,0:T(8,128)S(1)}, f32[56,128]{1,0:T(8,128)S(1)}, u32[]{:S(2)}, u32[]{:S(2)}) collective-permute-start(f32[56,128]{1,0:T(8,128)S(1)} %get-tuple-element.78), channel_id=1, source_target_pairs={{0,10},{1,11},{2,8},{3,9},{4,14},{5,15},{6,12},{7,13},{8,2},{9,3},... | collective-permute-start | bytes 86024 | tf_op jit(solution)/shard_map/ppermute | solution.py:501
  15.3 3.9 %collective-permute-start.7 = (f32[56,128]{1,0:T(8,128)S(1)}, f32[56,128]{1,0:T(8,128)S(1)}, u32[]{:S(2)}, u32[]{:S(2)}) collective-permute-start(f32[56,128]{1,0:T(8,128)S(1)} %get-tuple-element.78), channel_id=1, source_target_pairs={{0,2},{1,3},{2,0},{3,1},{4,6},{5,7},{6,4},{7,5},{8,10},{9,11},{10,... | collective-permute-start | bytes 86024 | tf_op jit(solution)/shard_map/ppermute | solution.py:501
  15.3 4.2 %collective-permute-start.6 = (f32[56,128]{1,0:T(8,128)S(1)}, f32[56,128]{1,0:T(8,128)S(1)}, u32[]{:S(2)}, u32[]{:S(2)}) collective-permute-start(f32[56,128]{1,0:T(8,128)S(1)} %get-tuple-element.78), channel_id=1, source_target_pairs={{0,8},{1,9},{2,10},{3,11},{4,12},{5,13},{6,14},{7,15},{8,0},{9,1},... | collective-permute-start | bytes 86024 | tf_op jit(solution)/shard_map/ppermute | solution.py:501
  15.9 8.1 %collective-permute-start.4 = (bf16[256,128]{1,0:T(8,128)(2,1)S(1)}, bf16[256,128]{1,0:T(8,128)(2,1)S(1)}, u32[]{:S(2)}, u32[]{:S(2)}) collective-permute-start(bf16[256,128]{1,0:T(8,128)(2,1)S(1)} %get-tuple-element.74), channel_id=1, source_target_pairs={{0,1},{1,0},{2,3},{3,2},{4,5},{5,4},{6,7},{7,6},{8,9},{9,8},{10,11... | collective-permute-start | bytes 196616 | tf_op jit(solution)/shard_map/ppermute | solution.py:503
  16.9 7.1 %collective-permute-start.5 = (bf16[256,128]{1,0:T(8,128)(2,1)S(1)}, bf16[256,128]{1,0:T(8,128)(2,1)S(1)}, u32[]{:S(2)}, u32[]{:S(2)}) collective-permute-start(bf16[256,128]{1,0:T(8,128)(2,1)S(1)} %get-tuple-element.75), channel_id=1, source_target_pairs={{0,8},{1,2},{2,1},{3,4},{4,3},{5,6},{6,5},{7,15},{8,0},{9,10},{10,... | collective-permute-start | bytes 196616 | tf_op jit(solution)/shard_map/ppermute | solution.py:503
  19.5 7.0 %collective-permute-start.11 = (f32[56,128]{1,0:T(8,128)S(1)}, f32[56,128]{1,0:T(8,128)S(1)}, u32[]{:S(2)}, u32[]{:S(2)}) collective-permute-start(f32[56,128]{1,0:T(8,128)S(1)} %add_add_fusion.own_ref), channel_id=1, source_target_pairs={{0,5},{1,4},{2,7},{3,6},{4,1},{5,0},{6,3},{7,2},{8,13},{9,12},{10,... | collective-permute-start | bytes 86024 | tf_op jit(solution)/shard_map/ppermute | solution.py:501
  22.3 4.8 %collective-permute-start.10 = (f32[56,128]{1,0:T(8,128)S(1)}, f32[56,128]{1,0:T(8,128)S(1)}, u32[]{:S(2)}, u32[]{:S(2)}) collective-permute-start(f32[56,128]{1,0:T(8,128)S(1)} %add_add_fusion.own_ref), channel_id=1, source_target_pairs={{0,4},{1,5},{2,6},{3,7},{4,0},{5,1},{6,2},{7,3},{8,12},{9,13},{10,... | collective-permute-start | bytes 86024 | tf_op jit(solution)/shard_map/ppermute | solution.py:501
  22.7 4.4 %collective-permute-start.9 = (f32[56,128]{1,0:T(8,128)S(1)}, f32[56,128]{1,0:T(8,128)S(1)}, u32[]{:S(2)}, u32[]{:S(2)}) collective-permute-start(f32[56,128]{1,0:T(8,128)S(1)} %add_add_fusion.own_ref), channel_id=1, source_target_pairs={{0,1},{1,0},{2,3},{3,2},{4,5},{5,4},{6,7},{7,6},{8,9},{9,8},{10,11... | collective-permute-start | bytes 86024 | tf_op jit(solution)/shard_map/ppermute | solution.py:501

commit v10 on v9

--- a/solution.py
+++ b/solution.py
@@ -118,18 +118,25 @@
     return jnp.concatenate([ref[first], ref[second]], axis=1)
 
 
+PARTS = 4
+
+
 def load_kernel(*refs):
     count = (len(refs) - 3) // 2
     sources, targets, (a_ref, b_ref, sems) = refs[:count], refs[count : 2 * count], refs[2 * count :]
     planes = sources[0].shape[1]
-    copies = [pltpu.make_async_copy(s, t, sems.at[n]) for n, (s, t) in enumerate(zip(sources, targets))]
+    part = sources[0].shape[0] // PARTS
+    spans = [pl.ds(n * part, part) for n in range(PARTS)]
+    pairs = [(sources[0].at[span], targets[0].at[span]) for span in spans] + list(zip(sources[1:], targets[1:]))
+    copies = [pltpu.make_async_copy(s, t, sems.at[n]) for n, (s, t) in enumerate(pairs)]
     for copy in copies:
         copy.start()
-    copies[0].wait()
+    for copy in copies[:PARTS]:
+        copy.wait()
     odd = lax.rem(lax.axis_index("depth"), 2)
     a_ref[...] = targets[0][:, (1 - odd) * (planes - 1)]
     b_ref[...] = targets[0][:, odd * (planes - 1)]
-    for copy in copies[1:]:
+    for copy in copies[PARTS:]:
         copy.wait()
 
 
@@ -431,7 +438,7 @@
         load_kernel,
         (*shapes, plane, plane),
         (pltpu.HBM,) * len(inputs),
-        [pltpu.SemaphoreType.DMA((len(inputs),))],
+        [pltpu.SemaphoreType.DMA((len(inputs) - 1 + PARTS,))],
         0,
         inputs,
     )

time: 28.1 us -> 28.2 us (level)
  no operation moved by 1% of the time
where the time goes in v10:
time: 28.2 us; the launch traced here: 28 us
  starting transfers between devices  15.6 us (55%)
  Pallas kernels  9.4 us (33%)
  waiting for transfers between devices  2.28 us (8%)
  between operations  0.7 us (2%)
    pallas_call x7, Pallas kernels, call(): pl.pallas_call(kernel, out_shape=out_shape, in_specs=[pl.BlockSpec(memory...  9.4 us
    ppermute x6, starting transfers between devices, body(): others = [lax.ppermute(packed, ('dp', 'depth'), p) for p in masks]  8.48 us
    ppermute x1, starting transfers between devices, exchanged(): lax.ppermute(a, ('dp', 'depth'), one)  3.03 us
    ppermute x2, starting transfers between devices, body(): lax.ppermute(e, ('dp', 'depth'), p)  2.47 us
    ppermute x6, waiting for transfers between devices, body(): others = [lax.ppermute(packed, ('dp', 'depth'), p) for p in masks]  1.71 us
    ppermute x1, starting transfers between devices, exchanged(): lax.ppermute(b, ('dp', 'depth'), two)  1.49 us
  transfers between devices with their start and end apart: 12, of which 5 were waited for; matrix products, arithmetic and copies ran while one was open for 0% of the time, Pallas kernels for 23%

profile of v10, /device:TPU:0, one launch (start us, length us, event | category | flops | bytes accessed | tf_op | source)
XLA Modules:
  0.0 28.0 jit_solution(5409795205664782636)
XLA Ops:
  0.6 1.2 %shard_map.110 = (bf16[16,8,16,128]{3,2,1,0:T(8,128)(2,1)S(1)}, s32[8,16,128]{2,1,0:T(8,128)S(1)}, s32[8,16,128]{2,1,0:T(8,128)S(1)}, bf16[16,16,27]{2,1,0:T(8,1...) custom-call(bf16[16,8,16,128]{3,2,1,0:T(8,128)(2,1)} %bitcast.12, ...), custom_call_target="tpu_custom_call" | custom-call | bytes 669536 | tf_op jit(solution)/shard_map/pallas_call | solution.py:379
  1.9 3.0 %collective-permute-start.1 = (bf16[16,16,128]{2,1,0:T(8,128)(2,1)S(1)}, bf16[16,16,128]{2,1,0:T(8,128)(2,1)S(1)}, u32[]{:S(2)}, u32[]{:S(2)}) collective-permute-start(bf16[16,16,128]{2,1,0:T(8,128)(2,1)S(1)} %get-tuple-element.58), channel_id=1, source_target_pairs={{0,1},{1,0},{2,3},{3,2},{4,5},{5,4},{6,7},{7,6},{8,9},{9,8},{10,11... | collective-permute-start | bytes 196616 | tf_op jit(solution)/shard_map/ppermute | solution.py:408
  4.9 1.5 %collective-permute-start.2 = (bf16[16,16,128]{2,1,0:T(8,128)(2,1)S(1)}, bf16[16,16,128]{2,1,0:T(8,128)(2,1)S(1)}, u32[]{:S(2)}, u32[]{:S(2)}) collective-permute-start(bf16[16,16,128]{2,1,0:T(8,128)(2,1)S(1)} %get-tuple-element.59), channel_id=1, source_target_pairs={{0,8},{1,2},{2,1},{3,4},{4,3},{5,6},{6,5},{7,15},{8,0},{9,10},{10,... | collective-permute-start | bytes 196616 | tf_op jit(solution)/shard_map/ppermute | solution.py:408
  6.4 2.2 %shard_map.111 = (bf16[256,2304]{1,0:T(8,128)(2,1)S(1)}, bf16[128,256]{1,0:T(8,128)(2,1)S(1)}, bf16[256,128]{1,0:T(8,128)(2,1)S(1)}, bf16[256,256]{1,0:T(8,128)(...) custom-call(bf16[16,8,16,128]{3,2,1,0:T(8,128)(2,1)S(1)} %get-tuple-, ...), custom_call_target="tpu_custom_call" | custom-call | flops 905969664 | bytes 669536 | tf_op jit(solution)/shard_map/pallas_call | solution.py:379
  8.6 0.1 collective-permute-start
  8.7 0.0 collective-permute-done.1.a_ref
  8.7 0.5 %collective-permute-done.2.b_ref = bf16[16,16,128]{2,1,0:T(8,128)(2,1)S(1)} collective-permute-done((bf16[16,16,128]{2,1,0:T(8,128)(2,1)S(1)}, bf16[16,16,128]{2,1,0:T(8,128)(2,1)S(1)}, u32[]{:S(2)}, u32[]{:S(2)}) %collective-permute-start.2) | collective-permute-done | bytes 65568 | tf_op jit(solution)/shard_map/ppermute | solution.py:408
  9.2 0.7 %shard_map.112 = (bf16[2,256,128]{2,1,0:T(8,128)(2,1)S(1)}, bf16[2,256,128]{2,1,0:T(8,128)(2,1)S(1)}, f32[2,128,128]{2,1,0:T(8,128)S(1)}, f32[2,16,128]{2,1,0:T(8,128)S(1)}) custom-call(bf16[16,16,128]{2,1,0:T(8,128)(2,1)S(1)} %collective-permute-done.1.a_ref, bf16[16,16,128]{2,1,0:T(8,128)(2,1)S(1)} %collective-permute-done.2.b_ref, ...), custom_call_target="tpu_custom_call" | custom-call | flops 301989888 | bytes 3096608 | tf_op jit(solution)/shard_map/pallas_call | solution.py:379
  9.9 0.1 collective-permute-start.3
  10.0 0.0 collective-permute-done.weight_ref
  10.0 1.1 %shard_map.113 = (bf16[6,768,128]{2,1,0:T(8,128)(2,1)S(1)}, f32[9,16,256]{2,1,0:T(8,128)S(1)}, f32[256,128]{1,0:T(8,128)S(1)}, f32[128,128]{1,0:T(8,128)S(1)}, f...) custom-call(bf16[8,256,128]{2,1,0:T(8,128)(2,1)S(1)} %get-tuple-element.53.turned_ref, ...), custom_call_target="tpu_custom_call" | custom-call | flops 905969664 | bytes 1687552 | tf_op jit(solution)/shard_map/pallas_call | solution.py:379
  11.0 0.1 collective-permute-done.3.weight_ref
  11.1 0.9 %shard_map.114 = (f32[56,128]{1,0:T(8,128)S(1)}, bf16[256,128]{1,0:T(8,128)(2,1)S(1)}, bf16[256,128]{1,0:T(8,128)(2,1)S(1)}, bf16[2,768,128]{2,1,0:T(8,128)(2,1)S(1)}) custom-call(bf16[8,256,128]{2,1,0:T(8,128)(2,1)S(1)} %get-tuple-element.53.turned_ref, bf16[2,256,128]{2,1,0:T(8,128)(2,1)S(1)} %get-tuple-element.66.halo_ref, ...), custom_call_target="tpu_custom_call" | custom-call | flops 301989888 | bytes 1474560 | tf_op jit(solution)/shard_map/pallas_call | solution.py:379
  12.0 3.4 %collective-permute-start.8 = (f32[56,128]{1,0:T(8,128)S(1)}, f32[56,128]{1,0:T(8,128)S(1)}, u32[]{:S(2)}, u32[]{:S(2)}) collective-permute-start(f32[56,128]{1,0:T(8,128)S(1)} %get-tuple-element.78), channel_id=1, source_target_pairs={{0,10},{1,11},{2,8},{3,9},{4,14},{5,15},{6,12},{7,13},{8,2},{9,3},... | collective-permute-start | bytes 86024 | tf_op jit(solution)/shard_map/ppermute | solution.py:508
  15.4 0.0 collective-permute-start.7
  15.4 0.6 %collective-permute-start.6 = (f32[56,128]{1,0:T(8,128)S(1)}, f32[56,128]{1,0:T(8,128)S(1)}, u32[]{:S(2)}, u32[]{:S(2)}) collective-permute-start(f32[56,128]{1,0:T(8,128)S(1)} %get-tuple-element.78), channel_id=1, source_target_pairs={{0,8},{1,9},{2,10},{3,11},{4,12},{5,13},{6,14},{7,15},{8,0},{9,1},... | collective-permute-start | bytes 86024 | tf_op jit(solution)/shard_map/ppermute | solution.py:508
  16.0 1.0 %collective-permute-start.4 = (bf16[256,128]{1,0:T(8,128)(2,1)S(1)}, bf16[256,128]{1,0:T(8,128)(2,1)S(1)}, u32[]{:S(2)}, u32[]{:S(2)}) collective-permute-start(bf16[256,128]{1,0:T(8,128)(2,1)S(1)} %get-tuple-element.74), channel_id=1, source_target_pairs={{0,1},{1,0},{2,3},{3,2},{4,5},{5,4},{6,7},{7,6},{8,9},{9,8},{10,11... | collective-permute-start | bytes 196616 | tf_op jit(solution)/shard_map/ppermute | solution.py:510
  17.0 1.5 %collective-permute-start.5 = (bf16[256,128]{1,0:T(8,128)(2,1)S(1)}, bf16[256,128]{1,0:T(8,128)(2,1)S(1)}, u32[]{:S(2)}, u32[]{:S(2)}) collective-permute-start(bf16[256,128]{1,0:T(8,128)(2,1)S(1)} %get-tuple-element.75), channel_id=1, source_target_pairs={{0,8},{1,2},{2,1},{3,4},{4,3},{5,6},{6,5},{7,15},{8,0},{9,10},{10,... | collective-permute-start | bytes 196616 | tf_op jit(solution)/shard_map/ppermute | solution.py:510
  18.5 0.0 collective-permute-done.8
  18.5 0.8 %collective-permute-done.7 = f32[56,128]{1,0:T(8,128)S(1)} collective-permute-done((f32[56,128]{1,0:T(8,128)S(1)}, f32[56,128]{1,0:T(8,128)S(1)}, u32[]{:S(2)}, u32[]{:S(2)}) %collective-permute-start.7) | collective-permute-done | bytes 28704 | tf_op jit(solution)/shard_map/ppermute | solution.py:508
  19.3 0.3 %collective-permute-done.6 = f32[56,128]{1,0:T(8,128)S(1)} collective-permute-done((f32[56,128]{1,0:T(8,128)S(1)}, f32[56,128]{1,0:T(8,128)S(1)}, u32[]{:S(2)}, u32[]{:S(2)}) %collective-permute-start.6) | collective-permute-done | bytes 28704 | tf_op jit(solution)/shard_map/ppermute | solution.py:508
  19.6 2.8 %collective-permute-start.11 = (f32[56,128]{1,0:T(8,128)S(1)}, f32[56,128]{1,0:T(8,128)S(1)}, u32[]{:S(2)}, u32[]{:S(2)}) collective-permute-start(f32[56,128]{1,0:T(8,128)S(1)} %add_add_fusion.own_ref), channel_id=1, source_target_pairs={{0,5},{1,4},{2,7},{3,6},{4,1},{5,0},{6,3},{7,2},{8,13},{9,12},{10,... | collective-permute-start | bytes 86024 | tf_op jit(solution)/shard_map/ppermute | solution.py:508
  22.4 0.3 %collective-permute-start.10 = (f32[56,128]{1,0:T(8,128)S(1)}, f32[56,128]{1,0:T(8,128)S(1)}, u32[]{:S(2)}, u32[]{:S(2)}) collective-permute-start(f32[56,128]{1,0:T(8,128)S(1)} %add_add_fusion.own_ref), channel_id=1, source_target_pairs={{0,4},{1,5},{2,6},{3,7},{4,0},{5,1},{6,2},{7,3},{8,12},{9,13},{10,... | collective-permute-start | bytes 86024 | tf_op jit(solution)/shard_map/ppermute | solution.py:508
  22.8 1.3 %collective-permute-start.9 = (f32[56,128]{1,0:T(8,128)S(1)}, f32[56,128]{1,0:T(8,128)S(1)}, u32[]{:S(2)}, u32[]{:S(2)}) collective-permute-start(f32[56,128]{1,0:T(8,128)S(1)} %add_add_fusion.own_ref), channel_id=1, source_target_pairs={{0,1},{1,0},{2,3},{3,2},{4,5},{5,4},{6,7},{7,6},{8,9},{9,8},{10,11... | collective-permute-start | bytes 86024 | tf_op jit(solution)/shard_map/ppermute | solution.py:508
  24.1 0.0 collective-permute-done.4.a_ref
  24.1 0.0 collective-permute-done.5.b_ref
  24.1 2.5 %shard_map.115 = (bf16[16,8,16,128]{3,2,1,0:T(8,128)(2,1)}, f32[8,128]{1,0:T(8,128)S(1)}) custom-call(bf16[256,128]{1,0:T(8,128)(2,1)S(1)} %collective-permute-done.4.a_ref, bf16[256,128]{1,0:T(8,128)(2,1)S(1)} %collective-permute-done.5.b_ref, bf16[6,768,128]{2,1,0:T(8,128)(2,1)S(1)} %get-tuple-element.76.shifted_ref, ...), custom_call_target="tpu_custom_call" | custom-call | flops 1207959552 | bytes 2883584 | tf_op jit(solution)/shard_map/pallas_call | solution.py:379
  26.6 0.0 collective-permute-done.11.refs_2_
  26.6 0.6 %collective-permute-done.10.refs_1_ = f32[56,128]{1,0:T(8,128)S(1)} collective-permute-done((f32[56,128]{1,0:T(8,128)S(1)}, f32[56,128]{1,0:T(8,128)S(1)}, u32[]{:S(2)}, u32[]{:S(2)}) %collective-permute-start.10) | collective-permute-done | bytes 28704 | tf_op jit(solution)/shard_map/ppermute | solution.py:508
  27.2 0.0 collective-permute-done.9.refs_0_
  27.2 0.8 %shard_map.116 = (f32[16,16,27]{2,1,0:T(8,128)}, f32[1,16]{1,0:T(1,128)}, f32[8,16]{1,0:T(8,128)}, f32[1,8]{1,0:T(1,128)}) custom-call(f32[8,128]{1,0:T(8,128)S(1)} %get-tuple-element.81.token_ref, f32[56,128]{1,0:T(8,128)S(1)} %add_add_fusion.own_ref, f32[56,128]{1,0:T(8,128)S(1)} %collective-permute-done.9.refs_0_, ...), custom_call_target="tpu_custom_call" | custom-call | flops 1000 | bytes 118784 | tf_op jit(solution)/shard_map/pallas_call | solution.py:379
  (1 shorter events, 0.0 us)
Async XLA Ops:
  1.9 6.8 %collective-permute-start.1 = (bf16[16,16,128]{2,1,0:T(8,128)(2,1)S(1)}, bf16[16,16,128]{2,1,0:T(8,128)(2,1)S(1)}, u32[]{:S(2)}, u32[]{:S(2)}) collective-permute-start(bf16[16,16,128]{2,1,0:T(8,128)(2,1)S(1)} %get-tuple-element.58), channel_id=1, source_target_pairs={{0,1},{1,0},{2,3},{3,2},{4,5},{5,4},{6,7},{7,6},{8,9},{9,8},{10,11... | collective-permute-start | bytes 196616 | tf_op jit(solution)/shard_map/ppermute | solution.py:408
  4.9 4.3 %collective-permute-start.2 = (bf16[16,16,128]{2,1,0:T(8,128)(2,1)S(1)}, bf16[16,16,128]{2,1,0:T(8,128)(2,1)S(1)}, u32[]{:S(2)}, u32[]{:S(2)}) collective-permute-start(bf16[16,16,128]{2,1,0:T(8,128)(2,1)S(1)} %get-tuple-element.59), channel_id=1, source_target_pairs={{0,8},{1,2},{2,1},{3,4},{4,3},{5,6},{6,5},{7,15},{8,0},{9,10},{10,... | collective-permute-start | bytes 196616 | tf_op jit(solution)/shard_map/ppermute | solution.py:408
  8.6 1.4 %collective-permute-start = (f32[6,16,128]{2,1,0:T(8,128)S(1)}, f32[6,16,128]{2,1,0:T(8,128)S(1)}, u32[]{:S(2)}, u32[]{:S(2)}) collective-permute-start(f32[6,16,128]{2,1,0:T(8,128)S(1)} %get-tuple-element.54), channel_id=1, source_target_pairs={{0,16},{16,0},{1,17},{17,1},{2,18},{18,2},{3,19},{19,3},{4,20},{20... | collective-permute-start | bytes 147464 | tf_op jit(solution)/shard_map/ppermute | solution.py:468
  9.9 1.2 %collective-permute-start.3 = (f32[2,16,128]{2,1,0:T(8,128)S(1)}, f32[2,16,128]{2,1,0:T(8,128)S(1)}, u32[]{:S(2)}, u32[]{:S(2)}) collective-permute-start(f32[2,16,128]{2,1,0:T(8,128)S(1)} %get-tuple-element.67), channel_id=1, source_target_pairs={{0,16},{16,0},{1,17},{17,1},{2,18},{18,2},{3,19},{19,3},{4,20},{20... | collective-permute-start | bytes 49160 | tf_op jit(solution)/shard_map/ppermute | solution.py:482
  12.0 6.5 %collective-permute-start.8 = (f32[56,128]{1,0:T(8,128)S(1)}, f32[56,128]{1,0:T(8,128)S(1)}, u32[]{:S(2)}, u32[]{:S(2)}) collective-permute-start(f32[56,128]{1,0:T(8,128)S(1)} %get-tuple-element.78), channel_id=1, source_target_pairs={{0,10},{1,11},{2,8},{3,9},{4,14},{5,15},{6,12},{7,13},{8,2},{9,3},... | collective-permute-start | bytes 86024 | tf_op jit(solution)/shard_map/ppermute | solution.py:508
  15.4 3.9 %collective-permute-start.7 = (f32[56,128]{1,0:T(8,128)S(1)}, f32[56,128]{1,0:T(8,128)S(1)}, u32[]{:S(2)}, u32[]{:S(2)}) collective-permute-start(f32[56,128]{1,0:T(8,128)S(1)} %get-tuple-element.78), channel_id=1, source_target_pairs={{0,2},{1,3},{2,0},{3,1},{4,6},{5,7},{6,4},{7,5},{8,10},{9,11},{10,... | collective-permute-start | bytes 86024 | tf_op jit(solution)/shard_map/ppermute | solution.py:508
  15.4 4.2 %collective-permute-start.6 = (f32[56,128]{1,0:T(8,128)S(1)}, f32[56,128]{1,0:T(8,128)S(1)}, u32[]{:S(2)}, u32[]{:S(2)}) collective-permute-start(f32[56,128]{1,0:T(8,128)S(1)} %get-tuple-element.78), channel_id=1, source_target_pairs={{0,8},{1,9},{2,10},{3,11},{4,12},{5,13},{6,14},{7,15},{8,0},{9,1},... | collective-permute-start | bytes 86024 | tf_op jit(solution)/shard_map/ppermute | solution.py:508
  16.0 8.1 %collective-permute-start.4 = (bf16[256,128]{1,0:T(8,128)(2,1)S(1)}, bf16[256,128]{1,0:T(8,128)(2,1)S(1)}, u32[]{:S(2)}, u32[]{:S(2)}) collective-permute-start(bf16[256,128]{1,0:T(8,128)(2,1)S(1)} %get-tuple-element.74), channel_id=1, source_target_pairs={{0,1},{1,0},{2,3},{3,2},{4,5},{5,4},{6,7},{7,6},{8,9},{9,8},{10,11... | collective-permute-start | bytes 196616 | tf_op jit(solution)/shard_map/ppermute | solution.py:510
  17.0 7.1 %collective-permute-start.5 = (bf16[256,128]{1,0:T(8,128)(2,1)S(1)}, bf16[256,128]{1,0:T(8,128)(2,1)S(1)}, u32[]{:S(2)}, u32[]{:S(2)}) collective-permute-start(bf16[256,128]{1,0:T(8,128)(2,1)S(1)} %get-tuple-element.75), channel_id=1, source_target_pairs={{0,8},{1,2},{2,1},{3,4},{4,3},{5,6},{6,5},{7,15},{8,0},{9,10},{10,... | collective-permute-start | bytes 196616 | tf_op jit(solution)/shard_map/ppermute | solution.py:510
  19.6 7.0 %collective-permute-start.11 = (f32[56,128]{1,0:T(8,128)S(1)}, f32[56,128]{1,0:T(8,128)S(1)}, u32[]{:S(2)}, u32[]{:S(2)}) collective-permute-start(f32[56,128]{1,0:T(8,128)S(1)} %add_add_fusion.own_ref), channel_id=1, source_target_pairs={{0,5},{1,4},{2,7},{3,6},{4,1},{5,0},{6,3},{7,2},{8,13},{9,12},{10,... | collective-permute-start | bytes 86024 | tf_op jit(solution)/shard_map/ppermute | solution.py:508
  22.4 4.8 %collective-permute-start.10 = (f32[56,128]{1,0:T(8,128)S(1)}, f32[56,128]{1,0:T(8,128)S(1)}, u32[]{:S(2)}, u32[]{:S(2)}) collective-permute-start(f32[56,128]{1,0:T(8,128)S(1)} %add_add_fusion.own_ref), channel_id=1, source_target_pairs={{0,4},{1,5},{2,6},{3,7},{4,0},{5,1},{6,2},{7,3},{8,12},{9,13},{10,... | collective-permute-start | bytes 86024 | tf_op jit(solution)/shard_map/ppermute | solution.py:508
  22.8 4.4 %collective-permute-start.9 = (f32[56,128]{1,0:T(8,128)S(1)}, f32[56,128]{1,0:T(8,128)S(1)}, u32[]{:S(2)}, u32[]{:S(2)}) collective-permute-start(f32[56,128]{1,0:T(8,128)S(1)} %add_add_fusion.own_ref), channel_id=1, source_target_pairs={{0,1},{1,0},{2,3},{3,2},{4,5},{5,4},{6,7},{7,6},{8,9},{9,8},{10,11... | collective-permute-start | bytes 86024 | tf_op jit(solution)/shard_map/ppermute | solution.py:508

commit v11 on v9

--- a/solution.py
+++ b/solution.py
@@ -222,7 +222,7 @@
     return values, bias_sum, offset_sum, dot_nt(halves, hiddens)
 
 
-STEP = 3
+STEP = 2
 
 
 def weight_products(shifted_ref, fields, ch, hh, totals):

time: 28.1 us -> 28.3 us (level)
  transfers between devices with their start and end apart: 12 -> 12, of which waited for: 5 -> 4; matrix products, arithmetic and copies ran while one was open for 0% -> 0% of each run, Pallas kernels for 23% -> 24%
where the time goes in v11:
time: 28.3 us; the launch traced here: 28.1 us
  starting transfers between devices  15.7 us (55%)
  Pallas kernels  9.51 us (34%)
  waiting for transfers between devices  2.2 us (8%)
  between operations  0.71 us (3%)
    pallas_call x7, Pallas kernels, call(): pl.pallas_call(kernel, out_shape=out_shape, in_specs=[pl.BlockSpec(memory...  9.51 us
    ppermute x6, starting transfers between devices, body(): others = [lax.ppermute(packed, ('dp', 'depth'), p) for p in masks]  8.47 us
    ppermute x1, starting transfers between devices, exchanged(): lax.ppermute(a, ('dp', 'depth'), one)  3.03 us
    ppermute x2, starting transfers between devices, body(): lax.ppermute(e, ('dp', 'depth'), p)  2.55 us
    ppermute x6, waiting for transfers between devices, body(): others = [lax.ppermute(packed, ('dp', 'depth'), p) for p in masks]  1.71 us
    ppermute x1, starting transfers between devices, exchanged(): lax.ppermute(b, ('dp', 'depth'), two)  1.49 us
  transfers between devices with their start and end apart: 12, of which 4 were waited for; matrix products, arithmetic and copies ran while one was open for 0% of the time, Pallas kernels for 24%

profile of v11, /device:TPU:0, one launch (start us, length us, event | category | flops | bytes accessed | tf_op | source)
XLA Modules:
  0.0 28.1 jit_solution(6172496780835377241)
XLA Ops:
  0.6 1.1 %shard_map.110 = (bf16[16,8,16,128]{3,2,1,0:T(8,128)(2,1)S(1)}, s32[8,16,128]{2,1,0:T(8,128)S(1)}, s32[8,16,128]{2,1,0:T(8,128)S(1)}, bf16[16,16,27]{2,1,0:T(8,1...) custom-call(bf16[16,8,16,128]{3,2,1,0:T(8,128)(2,1)} %bitcast.12, ...), custom_call_target="tpu_custom_call" | custom-call | bytes 669536 | tf_op jit(solution)/shard_map/pallas_call | solution.py:372
  1.8 3.0 %collective-permute-start.1 = (bf16[16,16,128]{2,1,0:T(8,128)(2,1)S(1)}, bf16[16,16,128]{2,1,0:T(8,128)(2,1)S(1)}, u32[]{:S(2)}, u32[]{:S(2)}) collective-permute-start(bf16[16,16,128]{2,1,0:T(8,128)(2,1)S(1)} %get-tuple-element.58), channel_id=1, source_target_pairs={{0,1},{1,0},{2,3},{3,2},{4,5},{5,4},{6,7},{7,6},{8,9},{9,8},{10,11... | collective-permute-start | bytes 196616 | tf_op jit(solution)/shard_map/ppermute | solution.py:401
  4.8 1.5 %collective-permute-start.2 = (bf16[16,16,128]{2,1,0:T(8,128)(2,1)S(1)}, bf16[16,16,128]{2,1,0:T(8,128)(2,1)S(1)}, u32[]{:S(2)}, u32[]{:S(2)}) collective-permute-start(bf16[16,16,128]{2,1,0:T(8,128)(2,1)S(1)} %get-tuple-element.59), channel_id=1, source_target_pairs={{0,8},{1,2},{2,1},{3,4},{4,3},{5,6},{6,5},{7,15},{8,0},{9,10},{10,... | collective-permute-start | bytes 196616 | tf_op jit(solution)/shard_map/ppermute | solution.py:401
  6.3 2.2 %shard_map.111 = (bf16[256,2304]{1,0:T(8,128)(2,1)S(1)}, bf16[128,256]{1,0:T(8,128)(2,1)S(1)}, bf16[256,128]{1,0:T(8,128)(2,1)S(1)}, bf16[256,256]{1,0:T(8,128)(...) custom-call(bf16[16,8,16,128]{3,2,1,0:T(8,128)(2,1)S(1)} %get-tuple-, ...), custom_call_target="tpu_custom_call" | custom-call | flops 905969664 | bytes 669536 | tf_op jit(solution)/shard_map/pallas_call | solution.py:372
  8.5 0.1 collective-permute-start
  8.6 0.0 collective-permute-done.1.a_ref
  8.6 0.5 %collective-permute-done.2.b_ref = bf16[16,16,128]{2,1,0:T(8,128)(2,1)S(1)} collective-permute-done((bf16[16,16,128]{2,1,0:T(8,128)(2,1)S(1)}, bf16[16,16,128]{2,1,0:T(8,128)(2,1)S(1)}, u32[]{:S(2)}, u32[]{:S(2)}) %collective-permute-start.2) | collective-permute-done | bytes 65568 | tf_op jit(solution)/shard_map/ppermute | solution.py:401
  9.1 0.7 %shard_map.112 = (bf16[2,256,128]{2,1,0:T(8,128)(2,1)S(1)}, bf16[2,256,128]{2,1,0:T(8,128)(2,1)S(1)}, f32[2,128,128]{2,1,0:T(8,128)S(1)}, f32[2,16,128]{2,1,0:T(8,128)S(1)}) custom-call(bf16[16,16,128]{2,1,0:T(8,128)(2,1)S(1)} %collective-permute-done.1.a_ref, bf16[16,16,128]{2,1,0:T(8,128)(2,1)S(1)} %collective-permute-done.2.b_ref, ...), custom_call_target="tpu_custom_call" | custom-call | flops 301989888 | bytes 3096608 | tf_op jit(solution)/shard_map/pallas_call | solution.py:372
  9.8 0.1 collective-permute-start.3
  9.9 0.0 collective-permute-done.weight_ref
  9.9 1.2 %shard_map.113 = (bf16[6,768,128]{2,1,0:T(8,128)(2,1)S(1)}, f32[9,16,256]{2,1,0:T(8,128)S(1)}, f32[256,128]{1,0:T(8,128)S(1)}, f32[128,128]{1,0:T(8,128)S(1)}, f...) custom-call(bf16[8,256,128]{2,1,0:T(8,128)(2,1)S(1)} %get-tuple-element.53.turned_ref, ...), custom_call_target="tpu_custom_call" | custom-call | flops 905969664 | bytes 1687552 | tf_op jit(solution)/shard_map/pallas_call | solution.py:372
  11.1 0.0 collective-permute-done.3.weight_ref
  11.1 0.9 %shard_map.114 = (f32[56,128]{1,0:T(8,128)S(1)}, bf16[256,128]{1,0:T(8,128)(2,1)S(1)}, bf16[256,128]{1,0:T(8,128)(2,1)S(1)}, bf16[2,768,128]{2,1,0:T(8,128)(2,1)S(1)}) custom-call(bf16[8,256,128]{2,1,0:T(8,128)(2,1)S(1)} %get-tuple-element.53.turned_ref, bf16[2,256,128]{2,1,0:T(8,128)(2,1)S(1)} %get-tuple-element.66.halo_ref, ...), custom_call_target="tpu_custom_call" | custom-call | flops 301989888 | bytes 1474560 | tf_op jit(solution)/shard_map/pallas_call | solution.py:372
  12.0 3.4 %collective-permute-start.8 = (f32[56,128]{1,0:T(8,128)S(1)}, f32[56,128]{1,0:T(8,128)S(1)}, u32[]{:S(2)}, u32[]{:S(2)}) collective-permute-start(f32[56,128]{1,0:T(8,128)S(1)} %get-tuple-element.78), channel_id=1, source_target_pairs={{0,10},{1,11},{2,8},{3,9},{4,14},{5,15},{6,12},{7,13},{8,2},{9,3},... | collective-permute-start | bytes 86024 | tf_op jit(solution)/shard_map/ppermute | solution.py:501
  15.5 0.0 collective-permute-start.7
  15.5 0.6 %collective-permute-start.6 = (f32[56,128]{1,0:T(8,128)S(1)}, f32[56,128]{1,0:T(8,128)S(1)}, u32[]{:S(2)}, u32[]{:S(2)}) collective-permute-start(f32[56,128]{1,0:T(8,128)S(1)} %get-tuple-element.78), channel_id=1, source_target_pairs={{0,8},{1,9},{2,10},{3,11},{4,12},{5,13},{6,14},{7,15},{8,0},{9,1},... | collective-permute-start | bytes 86024 | tf_op jit(solution)/shard_map/ppermute | solution.py:501
  16.0 1.1 %collective-permute-start.4 = (bf16[256,128]{1,0:T(8,128)(2,1)S(1)}, bf16[256,128]{1,0:T(8,128)(2,1)S(1)}, u32[]{:S(2)}, u32[]{:S(2)}) collective-permute-start(bf16[256,128]{1,0:T(8,128)(2,1)S(1)} %get-tuple-element.74), channel_id=1, source_target_pairs={{0,1},{1,0},{2,3},{3,2},{4,5},{5,4},{6,7},{7,6},{8,9},{9,8},{10,11... | collective-permute-start | bytes 196616 | tf_op jit(solution)/shard_map/ppermute | solution.py:503
  17.1 1.5 %collective-permute-start.5 = (bf16[256,128]{1,0:T(8,128)(2,1)S(1)}, bf16[256,128]{1,0:T(8,128)(2,1)S(1)}, u32[]{:S(2)}, u32[]{:S(2)}) collective-permute-start(bf16[256,128]{1,0:T(8,128)(2,1)S(1)} %get-tuple-element.75), channel_id=1, source_target_pairs={{0,8},{1,2},{2,1},{3,4},{4,3},{5,6},{6,5},{7,15},{8,0},{9,10},{10,... | collective-permute-start | bytes 196616 | tf_op jit(solution)/shard_map/ppermute | solution.py:503
  18.6 0.0 collective-permute-done.8
  18.6 0.7 %collective-permute-done.7 = f32[56,128]{1,0:T(8,128)S(1)} collective-permute-done((f32[56,128]{1,0:T(8,128)S(1)}, f32[56,128]{1,0:T(8,128)S(1)}, u32[]{:S(2)}, u32[]{:S(2)}) %collective-permute-start.7) | collective-permute-done | bytes 28704 | tf_op jit(solution)/shard_map/ppermute | solution.py:501
  19.3 0.3 %collective-permute-done.6 = f32[56,128]{1,0:T(8,128)S(1)} collective-permute-done((f32[56,128]{1,0:T(8,128)S(1)}, f32[56,128]{1,0:T(8,128)S(1)}, u32[]{:S(2)}, u32[]{:S(2)}) %collective-permute-start.6) | collective-permute-done | bytes 28704 | tf_op jit(solution)/shard_map/ppermute | solution.py:501
  19.7 2.9 %collective-permute-start.11 = (f32[56,128]{1,0:T(8,128)S(1)}, f32[56,128]{1,0:T(8,128)S(1)}, u32[]{:S(2)}, u32[]{:S(2)}) collective-permute-start(f32[56,128]{1,0:T(8,128)S(1)} %add_add_fusion.own_ref), channel_id=1, source_target_pairs={{0,5},{1,4},{2,7},{3,6},{4,1},{5,0},{6,3},{7,2},{8,13},{9,12},{10,... | collective-permute-start | bytes 86024 | tf_op jit(solution)/shard_map/ppermute | solution.py:501
  22.5 0.3 %collective-permute-start.10 = (f32[56,128]{1,0:T(8,128)S(1)}, f32[56,128]{1,0:T(8,128)S(1)}, u32[]{:S(2)}, u32[]{:S(2)}) collective-permute-start(f32[56,128]{1,0:T(8,128)S(1)} %add_add_fusion.own_ref), channel_id=1, source_target_pairs={{0,4},{1,5},{2,6},{3,7},{4,0},{5,1},{6,2},{7,3},{8,12},{9,13},{10,... | collective-permute-start | bytes 86024 | tf_op jit(solution)/shard_map/ppermute | solution.py:501
  22.9 1.2 %collective-permute-start.9 = (f32[56,128]{1,0:T(8,128)S(1)}, f32[56,128]{1,0:T(8,128)S(1)}, u32[]{:S(2)}, u32[]{:S(2)}) collective-permute-start(f32[56,128]{1,0:T(8,128)S(1)} %add_add_fusion.own_ref), channel_id=1, source_target_pairs={{0,1},{1,0},{2,3},{3,2},{4,5},{5,4},{6,7},{7,6},{8,9},{9,8},{10,11... | collective-permute-start | bytes 86024 | tf_op jit(solution)/shard_map/ppermute | solution.py:501
  24.1 0.0 collective-permute-done.4.a_ref
  24.1 0.0 collective-permute-done.5.b_ref
  24.1 2.5 %shard_map.115 = (bf16[16,8,16,128]{3,2,1,0:T(8,128)(2,1)}, f32[8,128]{1,0:T(8,128)S(1)}) custom-call(bf16[256,128]{1,0:T(8,128)(2,1)S(1)} %collective-permute-done.4.a_ref, bf16[256,128]{1,0:T(8,128)(2,1)S(1)} %collective-permute-done.5.b_ref, bf16[6,768,128]{2,1,0:T(8,128)(2,1)S(1)} %get-tuple-element.76.shifted_ref, ...), custom_call_target="tpu_custom_call" | custom-call | flops 1207959552 | bytes 2883584 | tf_op jit(solution)/shard_map/pallas_call | solution.py:372
  26.6 0.0 collective-permute-done.11.refs_2_
  26.6 0.7 %collective-permute-done.10.refs_1_ = f32[56,128]{1,0:T(8,128)S(1)} collective-permute-done((f32[56,128]{1,0:T(8,128)S(1)}, f32[56,128]{1,0:T(8,128)S(1)}, u32[]{:S(2)}, u32[]{:S(2)}) %collective-permute-start.10) | collective-permute-done | bytes 28704 | tf_op jit(solution)/shard_map/ppermute | solution.py:501
  27.3 0.0 collective-permute-done.9.refs_0_
  27.3 0.8 %shard_map.116 = (f32[16,16,27]{2,1,0:T(8,128)}, f32[1,16]{1,0:T(1,128)}, f32[8,16]{1,0:T(8,128)}, f32[1,8]{1,0:T(1,128)}) custom-call(f32[8,128]{1,0:T(8,128)S(1)} %get-tuple-element.81.token_ref, f32[56,128]{1,0:T(8,128)S(1)} %add_add_fusion.own_ref, f32[56,128]{1,0:T(8,128)S(1)} %collective-permute-done.9.refs_0_, ...), custom_call_target="tpu_custom_call" | custom-call | flops 1000 | bytes 118784 | tf_op jit(solution)/shard_map/pallas_call | solution.py:372
  (1 shorter events, 0.0 us)
Async XLA Ops:
  1.8 6.8 %collective-permute-start.1 = (bf16[16,16,128]{2,1,0:T(8,128)(2,1)S(1)}, bf16[16,16,128]{2,1,0:T(8,128)(2,1)S(1)}, u32[]{:S(2)}, u32[]{:S(2)}) collective-permute-start(bf16[16,16,128]{2,1,0:T(8,128)(2,1)S(1)} %get-tuple-element.58), channel_id=1, source_target_pairs={{0,1},{1,0},{2,3},{3,2},{4,5},{5,4},{6,7},{7,6},{8,9},{9,8},{10,11... | collective-permute-start | bytes 196616 | tf_op jit(solution)/shard_map/ppermute | solution.py:401
  4.8 4.3 %collective-permute-start.2 = (bf16[16,16,128]{2,1,0:T(8,128)(2,1)S(1)}, bf16[16,16,128]{2,1,0:T(8,128)(2,1)S(1)}, u32[]{:S(2)}, u32[]{:S(2)}) collective-permute-start(bf16[16,16,128]{2,1,0:T(8,128)(2,1)S(1)} %get-tuple-element.59), channel_id=1, source_target_pairs={{0,8},{1,2},{2,1},{3,4},{4,3},{5,6},{6,5},{7,15},{8,0},{9,10},{10,... | collective-permute-start | bytes 196616 | tf_op jit(solution)/shard_map/ppermute | solution.py:401
  8.5 1.4 %collective-permute-start = (f32[6,16,128]{2,1,0:T(8,128)S(1)}, f32[6,16,128]{2,1,0:T(8,128)S(1)}, u32[]{:S(2)}, u32[]{:S(2)}) collective-permute-start(f32[6,16,128]{2,1,0:T(8,128)S(1)} %get-tuple-element.54), channel_id=1, source_target_pairs={{0,16},{16,0},{1,17},{17,1},{2,18},{18,2},{3,19},{19,3},{4,20},{20... | collective-permute-start | bytes 147464 | tf_op jit(solution)/shard_map/ppermute | solution.py:461
  9.8 1.3 %collective-permute-start.3 = (f32[2,16,128]{2,1,0:T(8,128)S(1)}, f32[2,16,128]{2,1,0:T(8,128)S(1)}, u32[]{:S(2)}, u32[]{:S(2)}) collective-permute-start(f32[2,16,128]{2,1,0:T(8,128)S(1)} %get-tuple-element.67), channel_id=1, source_target_pairs={{0,16},{16,0},{1,17},{17,1},{2,18},{18,2},{3,19},{19,3},{4,20},{20... | collective-permute-start | bytes 49160 | tf_op jit(solution)/shard_map/ppermute | solution.py:475
  12.0 6.6 %collective-permute-start.8 = (f32[56,128]{1,0:T(8,128)S(1)}, f32[56,128]{1,0:T(8,128)S(1)}, u32[]{:S(2)}, u32[]{:S(2)}) collective-permute-start(f32[56,128]{1,0:T(8,128)S(1)} %get-tuple-element.78), channel_id=1, source_target_pairs={{0,10},{1,11},{2,8},{3,9},{4,14},{5,15},{6,12},{7,13},{8,2},{9,3},... | collective-permute-start | bytes 86024 | tf_op jit(solution)/shard_map/ppermute | solution.py:501
  15.5 3.9 %collective-permute-start.7 = (f32[56,128]{1,0:T(8,128)S(1)}, f32[56,128]{1,0:T(8,128)S(1)}, u32[]{:S(2)}, u32[]{:S(2)}) collective-permute-start(f32[56,128]{1,0:T(8,128)S(1)} %get-tuple-element.78), channel_id=1, source_target_pairs={{0,2},{1,3},{2,0},{3,1},{4,6},{5,7},{6,4},{7,5},{8,10},{9,11},{10,... | collective-permute-start | bytes 86024 | tf_op jit(solution)/shard_map/ppermute | solution.py:501
  15.5 4.2 %collective-permute-start.6 = (f32[56,128]{1,0:T(8,128)S(1)}, f32[56,128]{1,0:T(8,128)S(1)}, u32[]{:S(2)}, u32[]{:S(2)}) collective-permute-start(f32[56,128]{1,0:T(8,128)S(1)} %get-tuple-element.78), channel_id=1, source_target_pairs={{0,8},{1,9},{2,10},{3,11},{4,12},{5,13},{6,14},{7,15},{8,0},{9,1},... | collective-permute-start | bytes 86024 | tf_op jit(solution)/shard_map/ppermute | solution.py:501
  16.0 8.1 %collective-permute-start.4 = (bf16[256,128]{1,0:T(8,128)(2,1)S(1)}, bf16[256,128]{1,0:T(8,128)(2,1)S(1)}, u32[]{:S(2)}, u32[]{:S(2)}) collective-permute-start(bf16[256,128]{1,0:T(8,128)(2,1)S(1)} %get-tuple-element.74), channel_id=1, source_target_pairs={{0,1},{1,0},{2,3},{3,2},{4,5},{5,4},{6,7},{7,6},{8,9},{9,8},{10,11... | collective-permute-start | bytes 196616 | tf_op jit(solution)/shard_map/ppermute | solution.py:503
  17.1 7.0 %collective-permute-start.5 = (bf16[256,128]{1,0:T(8,128)(2,1)S(1)}, bf16[256,128]{1,0:T(8,128)(2,1)S(1)}, u32[]{:S(2)}, u32[]{:S(2)}) collective-permute-start(bf16[256,128]{1,0:T(8,128)(2,1)S(1)} %get-tuple-element.75), channel_id=1, source_target_pairs={{0,8},{1,2},{2,1},{3,4},{4,3},{5,6},{6,5},{7,15},{8,0},{9,10},{10,... | collective-permute-start | bytes 196616 | tf_op jit(solution)/shard_map/ppermute | solution.py:503
  19.7 7.0 %collective-permute-start.11 = (f32[56,128]{1,0:T(8,128)S(1)}, f32[56,128]{1,0:T(8,128)S(1)}, u32[]{:S(2)}, u32[]{:S(2)}) collective-permute-start(f32[56,128]{1,0:T(8,128)S(1)} %add_add_fusion.own_ref), channel_id=1, source_target_pairs={{0,5},{1,4},{2,7},{3,6},{4,1},{5,0},{6,3},{7,2},{8,13},{9,12},{10,... | collective-permute-start | bytes 86024 | tf_op jit(solution)/shard_map/ppermute | solution.py:501
  22.5 4.8 %collective-permute-start.10 = (f32[56,128]{1,0:T(8,128)S(1)}, f32[56,128]{1,0:T(8,128)S(1)}, u32[]{:S(2)}, u32[]{:S(2)}) collective-permute-start(f32[56,128]{1,0:T(8,128)S(1)} %add_add_fusion.own_ref), channel_id=1, source_target_pairs={{0,4},{1,5},{2,6},{3,7},{4,0},{5,1},{6,2},{7,3},{8,12},{9,13},{10,... | collective-permute-start | bytes 86024 | tf_op jit(solution)/shard_map/ppermute | solution.py:501
  22.9 4.4 %collective-permute-start.9 = (f32[56,128]{1,0:T(8,128)S(1)}, f32[56,128]{1,0:T(8,128)S(1)}, u32[]{:S(2)}, u32[]{:S(2)}) collective-permute-start(f32[56,128]{1,0:T(8,128)S(1)} %add_add_fusion.own_ref), channel_id=1, source_target_pairs={{0,1},{1,0},{2,3},{3,2},{4,5},{5,4},{6,7},{7,6},{8,9},{9,8},{10,11... | collective-permute-start | bytes 86024 | tf_op jit(solution)/shard_map/ppermute | solution.py:501
